TPU v7x, 32 devices: a whole 2x2x4 slice. The times are simulated.
32 devices in a mesh: gx: 4 (over y, x), gy: 2 (over core), gz: 4 (over z).
Axes of the slice: x: 2, y: 2, z: 4, core: 2. Of those that a mesh axis runs over, the one named last changes fastest.
Arguments:
- flow_state: float32 [4, 16, 64, 512], P(None, 'gx', 'gy', 'gz'), may hold values from -6 to 6
- viscosity: float32 [4, 16, 64, 512], P(None, 'gx', 'gy', 'gz'), may hold values from 0.05 to 0.5
- lift_weight: float32 [8, 128], replicated, may hold values from -6 to 6
- lift_bias: float32 [128], replicated, may hold values from -2 to 2
- norm_gains: float32 [6, 128], replicated, may hold values from 0.1 to 1.9
- query_weight: bfloat16 [2, 128, 128], replicated, may hold values from -4 to 4
- key_weight: bfloat16 [2, 128, 128], replicated, may hold values from -4 to 4
- value_weight: bfloat16 [2, 128, 128], replicated, may hold values from -0.5 to 0.5
- output_weight: bfloat16 [2, 128, 128], replicated, may hold values from -0.5 to 0.5
- up_weight: bfloat16 [2, 128, 512], replicated, may hold values from -0.5 to 0.5
- down_weight: bfloat16 [2, 512, 128], replicated, may hold values from -0.25 to 0.25
- head_weight: bfloat16 [128, 4], replicated, may hold values from -1.5 to 1.5
Outputs:
- state_next: float32 [4, 16, 64, 512], P(None, 'gx', 'gy', 'gz')
- eddy_field: float32 [4, 16, 64, 512], P(None, 'gx', 'gy', 'gz')
All inputs are finite; a program needn't handle non-finite values.
Results may differ from a plain program's by a relative error of at most 0.0058.
The roundings to bfloat16 on the way count: a program that leaves them out, or rounds other values in their place, can miss the bound.
Values may be sent and summed in bfloat16 or wider, within the bound.
No kernel may reach another device: no remote copies, remote signals or barrier semaphores. Data moves between devices by JAX's collectives and lax.ppermute only.
A program may use at most 64 MiB of HBM per device.

v0:
```python
import functools
import math

import jax
import jax.numpy as jnp
import numpy as np
from jax import lax
from jax.experimental import pallas as pl
from jax.experimental.pallas import tpu as pltpu
from jax.sharding import PartitionSpec as P

EPSILON = 1e-06
TIME_STEP = 0.3
HALO = 5
MASKED = -1e30
F32 = jnp.float32
BF16 = jnp.bfloat16
VMEM = pl.BlockSpec(memory_space=pltpu.VMEM)


def call(body, outs, args, scratch=(), flops=0, moved=0):
    return pl.pallas_call(
        body,
        out_shape=tuple(jax.ShapeDtypeStruct(s, d) for s, d in outs),
        in_specs=[VMEM] * len(args),
        out_specs=tuple([VMEM] * len(outs)),
        scratch_shapes=list(scratch),
        cost_estimate=pl.CostEstimate(flops=flops, bytes_accessed=moved, transcendentals=0),
    )(*args)


def iota(shape, dim):
    return lax.broadcasted_iota(jnp.int32, shape, dim)


def pack_kernel(nx, ny, flow, visc, *rest):
    outs, turned = rest[:nx], rest[nx]
    fields, xl, yl, zl = flow.shape
    lanes = xl * yl
    both = 2 * fields
    for f in range(both):
        source = flow[f] if f < fields else visc[f - fields]
        turned[pl.ds(f, zl, stride=both), :] = source.reshape(lanes, zl).T
    rows = zl * both // (nx * ny)
    a, b = lax.axis_index("gx"), lax.axis_index("gy")
    for d in range(nx):
        for e in range(ny):
            chunk = lax.rem(a + d, nx) * ny + lax.rem(b + e, ny)
            start = pl.multiple_of(chunk * rows, 8)
            outs[d][e] = turned[pl.ds(start, rows), :]


def unify_kernel(nx, fields, ring, *refs):
    parts, got = refs[:nx], refs[nx]
    whole = refs[nx + 1]
    ends = refs[nx + 2 :]
    a, b = lax.axis_index("gx"), lax.axis_index("gy")
    rows, lanes = got.shape[1:]
    zc = rows // (2 * fields)
    low = iota((zc, 2 * fields, lanes), 1) < fields
    first = jnp.full((zc, 2 * fields, lanes), b) == 0
    for d in range(nx):
        mine = parts[d][0].reshape(zc, 2 * fields, lanes)
        theirs = got[d].reshape(zc, 2 * fields, lanes)
        p = jnp.where(first, mine, theirs)
        q = jnp.where(first, theirs, mine)
        where_from = lax.rem(a + nx - d, nx)
        whole[:, 0, where_from] = jnp.where(low, p, pltpu.roll(q, fields, 1))
        whole[:, 1, where_from] = jnp.where(low, pltpu.roll(p, fields, 1), q)
    for s, count in enumerate(ring):
        ends[2 * s][...] = whole[:count]
        ends[2 * s + 1][...] = whole[zc - count :]


class Shifts:
    def __init__(self, shape, yl, fields):
        self.lanes, self.yl, self.fields = shape[-1], yl, fields
        lane = iota(shape, 2)
        self.last_x = lane >= self.lanes - yl
        self.first_x = lane < yl
        inner = lax.rem(lane, yl)
        self.last_y = inner == yl - 1
        self.first_y = inner == 0

    def pairs(self, v):
        n, yl = self.lanes, self.yl
        r = pltpu.roll(v, n - yl, 2)
        xp = jnp.where(self.last_x, jnp.concatenate([r[1:], r[:1]], 0), r)
        r = pltpu.roll(v, yl, 2)
        xm = jnp.where(self.first_x, jnp.concatenate([r[-1:], r[:-1]], 0), r)
        other = pltpu.roll(v, self.fields, 1)
        yp = jnp.where(self.last_y, pltpu.roll(other, yl - 1, 2), pltpu.roll(v, n - 1, 2))
        ym = jnp.where(self.first_y, pltpu.roll(other, n - yl + 1, 2), pltpu.roll(v, 1, 2))
        return xp, xm, yp, ym


def stencil_kernel(nx, ny, fields, yl, blocks, first_state, planes, send, *refs):
    ins, refs = refs[:blocks], refs[blocks:]
    filtered, refs = refs[0], refs[1:]
    if send:
        outs, refs = refs[:nx], refs[nx:]
    whole, coef, one, two, three = refs
    position = 0
    for ref in ins:
        count = ref.shape[0]
        whole[position : position + count] = ref[...]
        position += count
    zz = position
    shape = whole.shape[2:]
    lanes = shape[-1]
    shifts = Shifts(shape, yl, fields)
    upper = iota(shape, 1) < fields

    def coefficients(z, carry):
        nu = whole[z, 1]
        for k, other in enumerate(shifts.pairs(nu)):
            coef[z, k] = 0.5 * (nu + other)
        coef[z, 4] = 0.5 * (nu + whole[z + 1, 1])
        coef[z, 5] = 0.5 * (nu + whole[z - 1, 1])
        return carry

    lax.fori_loop(1, zz - 1, coefficients, 0)

    def half_velocity(load, d):
        top = jnp.broadcast_to(load(d), shape)
        bottom = jnp.broadcast_to(load(fields + d), shape)
        return 0.5 * jnp.where(upper, top, bottom)

    def advanced(load, row, z):
        c = load(z)
        xp, xm, yp, ym = shifts.pairs(c)
        zp, zm = load(z + 1), load(z - 1)
        total = None
        for d, (p, m) in enumerate(((xp, xm), (yp, ym), (zp, zm))):
            h = half_velocity(lambda r: row(z, r), d)
            term = (coef[z, 2 * d] - h) * (p - c) + (coef[z, 2 * d + 1] + h) * (m - c)
            total = term if total is None else total + term
        return c + TIME_STEP * total

    def segment_one(z, carry):
        one[z] = advanced(
            lambda i: whole[i, 0], lambda i, r: whole[i, 0, :, r : r + 1, :], z
        )
        return carry

    def segment_two(z, carry):
        moved = advanced(lambda i: one[i], lambda i, r: one[i, :, r : r + 1, :], z)
        two[z] = 0.75 * whole[z, 0] + 0.25 * moved
        return carry

    def last_segment(z, carry):
        moved = advanced(lambda i: two[i], lambda i, r: two[i, :, r : r + 1, :], z)
        three[z] = whole[z, 0] * (1.0 / 3.0) + (2.0 / 3.0) * moved
        return carry

    lax.fori_loop(1, zz - 1, segment_one, 0)
    lax.fori_loop(2, zz - 2, segment_two, 0)
    lax.fori_loop(3, zz - 3, last_segment, 0)

    if send:
        a, b = lax.axis_index("gx"), lax.axis_index("gy")
        zc = outs[0].shape[1] // fields
        mask = iota((zc // 2, 2 * fields, lanes), 1) < fields
        first = jnp.full((zc // 2, 2 * fields, lanes), b) == 0
        for d in range(nx):
            target = lax.rem(a + d, nx)
            block = three[first_state : first_state + zc, target]
            block = block.reshape(zc // 2, 2, 2 * fields, lanes)
            even, odd = block[:, 0], block[:, 1]
            zero = jnp.where(mask, even, pltpu.roll(odd, fields, 1))
            other = jnp.where(mask, pltpu.roll(even, fields, 1), odd)
            outs[d][0] = jnp.where(first, zero, other).reshape(zc * fields, lanes)
            outs[d][1] = jnp.where(first, other, zero).reshape(zc * fields, lanes)

    for i, plane in enumerate(planes):
        z = first_state + 2 * plane
        s0, s1 = three[z], three[z + 1]
        rows = []
        for value in (s0 + s1, s0 * s0 + s1 * s1):
            value = value + pltpu.roll(value, lanes - yl, 2)
            rows.append(value + pltpu.roll(value, lanes - 1, 2))
        both = jnp.concatenate(rows, axis=1)
        height = both.shape[1]
        for part in range(3):
            rounded = both.astype(BF16)
            both = both - rounded.astype(F32)
            for k in range(shape[0]):
                filtered[
                    i, part * height : (part + 1) * height, k * lanes : (k + 1) * lanes
                ] = rounded[k]


def gelu(x):
    inner = x * (0.7978845608028654 + 0.035677408136300125 * (x * x))
    half = 0.5 * x
    return half + half * jnp.tanh(inner)


def rms_scale(v, gain):
    return v * lax.rsqrt(jnp.mean(v * v, axis=-1, keepdims=True) + EPSILON) * gain


def matmul(v, w):
    return jnp.dot(v, w, preferred_element_type=F32)


def against(v, w):
    return lax.dot_general(v, w, (((1,), (1,)), ((), ())), preferred_element_type=F32)


def mixer(section, groups, same, weights, gains):
    qkv_w, out_w, up_w, down_w = weights
    channels = section.shape[1]
    carried = section.astype(F32)
    normed = rms_scale(carried, gains[0]).astype(BF16)
    qkv = matmul(normed, qkv_w).astype(BF16)
    scale = channels ** (-0.5)
    pieces = {}
    for group in groups:
        rows = jnp.concatenate([qkv[s : s + n] for s, n in group], axis=0)
        q = rows[:, :channels]
        k = rows[:, channels : 2 * channels]
        v = rows[:, 2 * channels :]
        scores = jnp.where(same, against(q, k) * scale, MASKED)
        exponent = jnp.exp(scores - jnp.max(scores, axis=-1, keepdims=True))
        total = jnp.sum(exponent, axis=-1, keepdims=True)
        attention = (exponent * (1.0 / total)).astype(BF16)
        result = matmul(attention, v).astype(BF16)
        at = 0
        for s, n in group:
            pieces[s] = result[at : at + n]
            at += n
    attended = jnp.concatenate([pieces[s] for s in sorted(pieces)], axis=0)
    residual = carried + matmul(attended, out_w)
    again = rms_scale(residual, gains[1]).astype(BF16)
    hidden = gelu(matmul(again, up_w)).astype(BF16)
    return (residual + matmul(hidden, down_w)).astype(BF16)


def attention_kernel(nx, ny, fields, cells, step, last, earlier, *refs):
    (filtered, sel, lift_w, bias, gains, qkv_w, out_w, up_w, down_w, head), refs = (
        refs[:10],
        refs[10:],
    )
    if last:
        if earlier:
            before, refs = refs[0], refs[1:]
        spread, refs = refs[0], refs[1:]
        outs, coefficient = refs[:nx], refs[nx]
    else:
        coefficient = refs[0]
    xc, yc = cells
    channels = bias.shape[1]
    planes, height, wide = filtered.shape
    side = nx * xc * yc
    per_plane = ny * side
    span = sel.shape[0]
    cut = sel.shape[1]
    along_x = [[(p * per_plane + b * side, side)] for p in range(step) for b in range(ny)]
    together = max(1, 128 // (ny * xc * yc))
    piece = together * xc * yc
    along_y = [
        [(p * per_plane + b * side + g * piece, piece) for b in range(ny)]
        for p in range(step)
        for g in range(nx // together)
    ]
    row, column = iota((side, side), 0), iota((side, side), 1)
    same_x_line = lax.rem(row, yc) == lax.rem(column, yc)
    count = ny * piece
    row, column = iota((count, count), 0), iota((count, count), 1)
    same_y_line = lax.rem(row, piece) // yc == lax.rem(column, piece) // yc

    def some_planes(i, carry):
        block = filtered[pl.ds(i * step, step)].reshape(step * height, wide)
        found = []
        for g in range(wide // span):
            picked = matmul(block[:, g * span : (g + 1) * span], sel[...])
            third = height // 3
            found.append(
                [
                    picked[p * height : p * height + third]
                    + picked[p * height + third : p * height + 2 * third]
                    + picked[p * height + 2 * third : (p + 1) * height]
                    for p in range(step)
                ]
            )
        lifted = []
        for p in range(step):
            by_core = [[] for _ in range(ny)]
            for g in range(wide // span):
                both = lax.dot_general(
                    found[g][p],
                    lift_w[...],
                    (((0,), (0,)), ((), ())),
                    precision=lax.Precision.HIGHEST,
                    preferred_element_type=F32,
                )
                for b in range(ny):
                    by_core[b].append(both[:, b * channels : (b + 1) * channels])
            for b in range(ny):
                lifted += by_core[b]
        lifted = jnp.concatenate(lifted, axis=0) + bias[...]
        features = gelu(rms_scale(lifted, gains[0:1])).astype(BF16)
        first = mixer(
            features,
            along_x,
            same_x_line,
            (qkv_w[0], out_w[0], up_w[0], down_w[0]),
            (gains[1:2], gains[2:3]),
        )
        second = mixer(
            first,
            along_y,
            same_y_line,
            (qkv_w[1], out_w[1], up_w[1], down_w[1]),
            (gains[3:4], gains[4:5]),
        )
        final = rms_scale(second.astype(F32), gains[5:6]).astype(BF16)
        logits = against(head[0], final[:per_plane])
        for p in range(1, step):
            logits = logits + against(head[p], final[p * per_plane : (p + 1) * per_plane])
        coefficient[i] = 0.05 + 0.45 * jax.nn.sigmoid(logits)
        return carry

    lax.fori_loop(0, planes // step, some_planes, 0)

    if last:
        a, b = lax.axis_index("gx"), lax.axis_index("gy")
        every = coefficient[...].reshape(-1, per_plane)
        if earlier:
            every = jnp.concatenate([before[...].reshape(-1, per_plane), every], axis=0)
        depth = outs[0].shape[1]
        if every.shape[0] < depth:
            blank = jnp.zeros((depth - every.shape[0], per_plane), F32)
            every = jnp.concatenate([every, blank], axis=0)
        every = every.astype(BF16).astype(F32)
        width = spread.shape[1] // ny
        first = jnp.full((depth, width), b) == 0
        for d in range(nx):
            target = lax.rem(a + d, nx)
            shift = lax.rem((nx + 1 - target) * (xc * yc), side)
            near = [
                pltpu.roll(every[:, k * side : (k + 1) * side], shift, 1)[:, :cut]
                for k in range(ny)
            ]
            near = jnp.concatenate(near, axis=1).astype(BF16)
            found = matmul(near, spread[...])
            zero, other = found[:, :width], found[:, width:]
            outs[d][0] = jnp.where(first, zero, other).astype(BF16)
            outs[d][1] = jnp.where(first, other, zero).astype(BF16)


def state_kernel(nx, ny, *refs):
    parts, got, out, rows = refs[:nx], refs[nx], refs[nx + 1], refs[nx + 2]
    fields, xl, yl, zl = out.shape
    a, b = lax.axis_index("gx"), lax.axis_index("gy")
    size = got.shape[1]
    for d in range(nx):
        source = lax.rem(a + nx - d, nx)
        mine = pl.multiple_of((source * ny + b) * size, 8)
        theirs = pl.multiple_of((source * ny + lax.rem(b + 1, ny)) * size, 8)
        rows[pl.ds(mine, size), :] = parts[d][0]
        rows[pl.ds(theirs, size), :] = got[d]
    for f in range(fields):
        out[f] = rows[pl.ds(f, zl, stride=fields), :].T.reshape(xl, yl, zl)


def refine_kernel(nx, ny, *refs):
    parts, (got, along_z, across, out, rows) = refs[:nx], refs[nx:]
    fields, xl, yl, zl = out.shape
    a, b = lax.axis_index("gx"), lax.axis_index("gy")
    for d in range(nx):
        source = lax.rem(a + nx - d, nx)
        rows[source * ny + b] = parts[d][0]
        rows[source * ny + lax.rem(b + 1, ny)] = got[d]
    count, depth, width = rows.shape
    coarse = rows[...].reshape(count * depth, width)
    spread = lax.dot_general(
        coarse, along_z[...], (((0,), (0,)), ((), ())), preferred_element_type=F32
    )
    total = None
    for part in range(3):
        rounded = spread.astype(BF16)
        spread = spread - rounded.astype(F32)
        product = matmul(across[...], rounded)
        total = product if total is None else total + product
    for f in range(fields):
        out[f] = total[:, f * zl : (f + 1) * zl].reshape(xl, yl, zl)


def pick_matrix(group, xl, yl):
    xc, yc = xl // 2, yl // 2
    table = np.zeros((group, xl, yl, group, xc, yc), np.float32)
    for k in range(group):
        for x in range(xc):
            for y in range(yc):
                table[k, 2 * x, 2 * y, k, x, y] = 0.125
    return table.reshape(group * xl * yl, group * xc * yc)


def spread_matrix(ny, near, xc, yc, width):
    table = np.zeros((ny, near, xc, yc, ny, width), np.float32)
    for target in range(ny):
        for i in range(xc + 2):
            x = i - 1 + xc
            for j in range(yc + 2):
                y = (target * yc + j - 1) % (ny * yc)
                table[y // yc, x // xc, x % xc, y % yc, target, i * (yc + 2) + j] = 1.0
    return table.reshape(ny * near * xc * yc, ny * width)


def taps(fine):
    return ((fine // 2, 0.75), (fine // 2 + (1 if fine % 2 else -1), 0.25))


def across_matrix(xl, yl, width):
    yc = yl // 2
    table = np.zeros((xl, yl, width), np.float32)
    for x in range(xl):
        for y in range(yl):
            for i, u in taps(x):
                for j, v in taps(y):
                    table[x, y, (i + 1) * (yc + 2) + j + 1] += u * v
    return table.reshape(xl * yl, width)


def along_z_matrix(chunks, depth, place, fields, zc):
    table = np.zeros((chunks, depth, fields, chunks, zc), np.float32)
    for c in range(chunks):
        for z in range(zc):
            for i, u in taps(z):
                for f in range(fields):
                    table[c, place[i] + f, f, c, z] += u
    return table.reshape(chunks * depth, fields * chunks * zc)


def over_x(messages, nx):
    received = [messages[0]]
    for d in range(1, nx):
        received.append(lax.ppermute(messages[d], "gx", [(i, (i + d) % nx) for i in range(nx)]))
    return received


def over_y(received, ny):
    away = jnp.stack([piece[1] for piece in received], axis=0)
    return lax.ppermute(away, "gy", [(i, (i + 1) % ny) for i in range(ny)])


def per_device(
    nx,
    ny,
    nz,
    flow_state,
    viscosity,
    lift_weight,
    lift_bias,
    norm_gains,
    query_weight,
    key_weight,
    value_weight,
    output_weight,
    up_weight,
    down_weight,
    head_weight,
):
    fields, xl, yl, zl = flow_state.shape
    lanes = xl * yl
    chunks = nx * ny
    zc = zl // chunks
    half = zc // 2
    xc, yc = xl // 2, yl // 2
    channels = lift_bias.shape[0]
    hidden = up_weight.shape[-1]
    both = 2 * fields
    per_plane = chunks * xc * yc

    eye = jnp.eye(ny, dtype=F32)
    lift_w = lift_weight.reshape(2, 1, fields, 1, channels) * eye.reshape(1, ny, 1, ny, 1)
    lift_w = lift_w.reshape(2 * ny * fields, ny * channels)
    qkv_w = jnp.concatenate([query_weight, key_weight, value_weight], axis=-1)
    group = max(1, 512 // lanes)
    sel = jnp.asarray(pick_matrix(group, xl, yl), BF16)
    turned_head = head_weight.T

    packed = call(
        functools.partial(pack_kernel, nx, ny),
        [((ny, zc * both, lanes), F32)] * nx,
        [flow_state, viscosity],
        [pltpu.VMEM((zl * both, lanes), F32)],
        flops=1000000,
        moved=4 * zl * both * lanes,
    )
    received = over_x(packed, nx)
    got = over_y(received, ny)
    ring = []
    while sum(ring) < HALO:
        ring.append(min(zc, HALO - sum(ring)))
    block = (2, nx, ny * fields, lanes)
    unified = call(
        functools.partial(unify_kernel, nx, fields, ring),
        [((zc,) + block, F32)] + [((n,) + block, F32) for n in ring for _ in range(2)],
        [*received, got],
        flops=1000000,
        moved=8 * zl * both * lanes,
    )
    own, ends = unified[0], unified[1:]
    total = nz * chunks

    def ring_step(value, move):
        pairs = []
        for k in range(total):
            t = (k + move) % total
            pairs.append(((k % chunks) * nz + k // chunks, (t % chunks) * nz + t // chunks))
        return lax.ppermute(value, ("gx", "gy", "gz"), pairs)

    above = [ring_step(ends[2 * s], -(s + 1)) for s in range(len(ring))]
    below = [ring_step(ends[2 * s + 1], s + 1) for s in range(len(ring))]

    inner = list(range(2, half - 2))
    outer = [p for p in range(-1, half + 1) if p not in inner]

    def stencil(inputs, first_state, planes, send):
        zz = sum(v.shape[0] for v in inputs)
        size = (zz,) + block[1:]
        outs = [((len(planes), 3 * 2 * ny * fields, nx * lanes), BF16)]
        if send:
            outs += [((ny, zc * fields, lanes), F32)] * nx
        return call(
            functools.partial(
                stencil_kernel, nx, ny, fields, yl, len(inputs), first_state, planes, send
            ),
            outs,
            inputs,
            [
                pltpu.VMEM((zz,) + block, F32),
                pltpu.VMEM((zz, 6) + block[1:], F32),
                pltpu.VMEM(size, F32),
                pltpu.VMEM(size, F32),
                pltpu.VMEM(size, F32),
            ],
            flops=300000000,
            moved=8 * zz * nx * 8 * lanes,
        )

    def pairing(planes):
        return 2 if len(planes) % 2 == 0 else 1

    def heads(step):
        out = jnp.zeros((step, 8, channels), BF16)
        for p in range(step):
            out = out.at[p, p * fields : (p + 1) * fields].set(turned_head)
        return out

    def attention(filtered, planes, more, outs, last):
        step = pairing(planes)
        args = [
            filtered,
            sel,
            lift_w,
            lift_bias.reshape(1, channels),
            norm_gains,
            qkv_w,
            output_weight,
            up_weight,
            down_weight,
            heads(step),
        ] + more
        size = (len(planes) // step, 8, per_plane)
        work = len(planes) * per_plane * channels * (8 * channels + 4 * hidden) * 2
        return call(
            functools.partial(
                attention_kernel, nx, ny, fields, (xc, yc), step, last, len(more) > 1
            ),
            outs if last else [(size, F32)],
            args,
            [pltpu.VMEM(size, F32)] if last else [],
            flops=3 * work,
            moved=1000000,
        )

    place = {}
    depth = 0
    for planes in (inner, outer):
        step = pairing(planes)
        for i, p in enumerate(planes):
            place[p] = depth + (i // step) * 8 + (i % step) * fields
        depth += len(planes) // step * 8
    depth = -(-depth // 16) * 16

    more = []
    if inner:
        (filtered,) = stencil([own], 0, inner, False)
        more = list(attention(filtered, inner, [], None, False))

    ordered = below[::-1] + [own] + above
    second = stencil(ordered, HALO, outer, True)
    filtered, state_messages = second[0], list(second[1:])
    state_received = over_x(state_messages, nx)

    width = -(-(xc + 2) * (yc + 2) // 128) * 128
    near = 128 // (xc * yc)
    spread = jnp.asarray(spread_matrix(ny, near, xc, yc, width), BF16)
    messages = attention(
        filtered, outer, more + [spread], [((ny, depth, width), BF16)] * nx, True
    )
    coarse_received = over_x(list(messages), nx)
    state_got = over_y(state_received, ny)
    (state_next,) = call(
        functools.partial(state_kernel, nx, ny),
        [(flow_state.shape, F32)],
        [*state_received, state_got],
        [pltpu.VMEM((zl * fields, lanes), F32)],
        flops=1000000,
        moved=8 * zl * fields * lanes,
    )
    coarse_got = over_y(coarse_received, ny)
    along_z = jnp.asarray(along_z_matrix(chunks, depth, place, fields, zc), BF16)
    across = jnp.asarray(across_matrix(xl, yl, width), BF16)
    (eddy_field,) = call(
        functools.partial(refine_kernel, nx, ny),
        [(flow_state.shape, F32)],
        [*coarse_received, coarse_got, along_z, across],
        [pltpu.VMEM((chunks, depth, width), BF16)],
        flops=1000000,
        moved=8 * zl * fields * lanes,
    )
    return (state_next, eddy_field)


def solution(mesh):
    sizes = [mesh.shape[name] for name in ("gx", "gy", "gz")]
    return jax.shard_map(
        functools.partial(per_device, *sizes),
        mesh=mesh,
        in_specs=(
            P(None, "gx", "gy", "gz"),
            P(None, "gx", "gy", "gz"),
            P(),
            P(),
            P(),
            P(),
            P(),
            P(),
            P(),
            P(),
            P(),
            P(),
        ),
        out_specs=(P(None, "gx", "gy", "gz"), P(None, "gx", "gy", "gz")),
        check_vma=False,
    )
```

profile of v0, /device:TPU:0, one launch (start us, length us, event | category | flops | bytes accessed | tf_op | source)
XLA Modules:
  0.0 95.6 jit_solution(9284295050724343207)
XLA Ops:
  0.6 0.0 copy-start.20
  0.7 2.1 %shard_map.167 = (f32[2,128,128]{2,1,0:T(8,128)}, f32[2,128,128]{2,1,0:T(8,128)}, f32[2,128,128]{2,1,0:T(8,128)}, f32[2,128,128]{2,1,0:T(8,128)}) custom-call(f32[4,4,32,128]{3,2,1,0:T(8,128)} %flow.1, f32[4,4,32,128]{3,2,1,0:T(8,128)} %visc.1), custom_call_target="tpu_custom_call" | custom-call | flops 1000000 | bytes 524288 | tf_op jit(solution)/shard_map/pallas_call | solution.py:22
  2.7 3.0 %collective-permute-start = (f32[2,128,128]{2,1,0:T(8,128)}, f32[2,128,128]{2,1,0:T(8,128)S(1)}, u32[]{:S(2)}, u32[]{:S(2)}) collective-permute-start(f32[2,128,128]{2,1,0:T(8,128)} %get-tuple-element.59), channel_id=1, source_target_pairs={{0,8},{8,16},{16,24},{24,0},{1,9},{9,17},{17,25},{25,1},{2,10},{10... | collective-permute-start | bytes 393224 | tf_op jit(solution)/shard_map/ppermute | solution.py:440
  5.7 1.5 %collective-permute-start.1 = (f32[2,128,128]{2,1,0:T(8,128)}, f32[2,128,128]{2,1,0:T(8,128)S(1)}, u32[]{:S(2)}, u32[]{:S(2)}) collective-permute-start(f32[2,128,128]{2,1,0:T(8,128)} %get-tuple-element.60), channel_id=1, source_target_pairs={{0,16},{8,24},{16,0},{24,8},{1,17},{9,25},{17,1},{25,9},{2,18},{10... | collective-permute-start | bytes 393224 | tf_op jit(solution)/shard_map/ppermute | solution.py:440
  7.2 1.4 %collective-permute-start.2 = (f32[2,128,128]{2,1,0:T(8,128)}, f32[2,128,128]{2,1,0:T(8,128)S(1)}, u32[]{:S(2)}, u32[]{:S(2)}) collective-permute-start(f32[2,128,128]{2,1,0:T(8,128)} %get-tuple-element.61), channel_id=1, source_target_pairs={{0,24},{8,0},{16,8},{24,16},{1,25},{9,1},{17,9},{25,17},{2,26},{10... | collective-permute-start | bytes 393224 | tf_op jit(solution)/shard_map/ppermute | solution.py:440
  8.6 0.1 broadcast_multiply_fusion
  8.7 0.0 copy-start.11
  8.8 0.8 copy-done.11
  9.6 1.6 %collective-permute-done.refs_1_ = f32[2,128,128]{2,1,0:T(8,128)S(1)} collective-permute-done((f32[2,128,128]{2,1,0:T(8,128)}, f32[2,128,128]{2,1,0:T(8,128)S(1)}, u32[]{:S(2)}, u32[]{:S(2)}) %collective-permute-start) | collective-permute-done | bytes 131104 | tf_op jit(solution)/shard_map/ppermute | solution.py:440
  11.2 0.7 copy-done.1
  11.8 1.3 %collective-permute-done.1.refs_2_ = f32[2,128,128]{2,1,0:T(8,128)S(1)} collective-permute-done((f32[2,128,128]{2,1,0:T(8,128)}, f32[2,128,128]{2,1,0:T(8,128)S(1)}, u32[]{:S(2)}, u32[]{:S(2)}) %collective-permute-start.1) | collective-permute-done | bytes 131104 | tf_op jit(solution)/shard_map/ppermute | solution.py:440
  13.1 0.6 copy-done.2
  13.8 0.0 collective-permute-done.2.refs_3_
  13.8 0.8 slice-done
  14.7 0.1 slice-done.1
  14.7 0.1 collective-permute-start.3
  14.8 0.7 copy-done.12
  15.6 0.0 copy-start.17
  15.6 0.7 copy.20
  16.2 0.7 copy-done.19
  16.9 0.0 collective-permute-done.3.refs_4_
  16.9 0.0 copy-start.4
  16.9 0.7 copy-done.4
  17.6 2.2 %shard_map.168 = (f32[16,2,4,8,128]{4,3,2,1,0:T(8,128)}, f32[5,2,4,8,128]{4,3,2,1,0:T(8,128)}, f32[5,2,4,8,128]{4,3,2,1,0:T(8,128)}) custom-call(f32[2,128,128]{2,1,0:T(8,128)} %get-tuple-element.58.refs_0_, f32[2,128,128]{2,1,0:T(8,128)} %copy-done.1, f32[2,128,128]{2,1,0:T(8,128)} %copy-done.2, f32[2,128,128]{2,1,0:T(8,128)} %copy-done.3, ...), custom_call_target="tpu_custom_call" | custom-call | flops 1000000 | bytes 1048576 | tf_op jit(solution)/shard_map/pallas_call | solution.py:22
  19.8 0.0 collective-permute-start.4
  19.9 5.3 %collective-permute-start.5 = (f32[5,2,4,8,128]{4,3,2,1,0:T(8,128)}, f32[5,2,4,8,128]{4,3,2,1,0:T(8,128)S(1)}, u32[]{:S(2)}, u32[]{:S(2)}) collective-permute-start(f32[5,2,4,8,128]{4,3,2,1,0:T(8,128)} %get-tuple-element.64), channel_id=1, source_target_pairs={{0,31},{4,0},{8,4},{12,8},{16,12},{20,16},{24,20},{28,24},{1,28},{... | collective-permute-start | bytes 491528 | tf_op jit(solution)/shard_map/ppermute | solution.py:514
  25.2 6.9 %shard_map.171.refs_0_ = bf16[4,48,512]{2,1,0:T(8,128)(2,1)} custom-call(f32[16,2,4,8,128]{4,3,2,1,0:T(8,128)} %get-tuple-element.63.refs_1_.refs_0_), custom_call_target="tpu_custom_call" | custom-call | flops 300000000 | bytes 524288 | tf_op jit(solution)/shard_map/pallas_call | solution.py:22
  32.1 11.8 %shard_map.172.refs_10_ = f32[2,8,256]{2,1,0:T(8,128)} custom-call(bf16[4,48,512]{2,1,0:T(8,128)(2,1)} %shard_map.171.refs_0_, bf16[512,128]{1,0:T(8,128)(2,1)} %constant.100.clone.refs_1_, f32[16,256]{1,0:T(8,128)} %bitcast.12, f32[1,128]{1,0:T(1,128)} %bitcast.16, f32[6,128]{1,0:T(8,128)} %refs_4_.3, bf16[2,128,384]{2,1,0:T(8,128)(2,1)} %copy-done.17, ...), custom_call_target="tpu_custom_call" | custom-call | flops 2415919104 | bytes 1000000 | tf_op jit(solution)/shard_map/pallas_call | solution.py:22
  43.9 0.0 collective-permute-done.4.refs_0_
  43.9 0.0 collective-permute-done.5.refs_2_
  43.9 0.7 copy-done.21
  44.6 0.7 copy-done.22
  45.3 11.1 %shard_map.169 = (bf16[6,48,512]{2,1,0:T(8,128)(2,1)}, f32[2,64,128]{2,1,0:T(8,128)}, f32[2,64,128]{2,1,0:T(8,128)}, f32[2,64,128]{2,1,0:T(8,128)}, f32[2,64,128]{2,1,0:T(8,128)}) custom-call(f32[5,2,4,8,128]{4,3,2,1,0:T(8,128)} %copy-done.21, f32[16,2,4,8,128]{4,3,2,1,0:T(8,128)} %get-tuple-element.63.refs_1_.refs_0_, f32[5,2,4,8,128]{4,3,2,1,0:T(8,128)} %copy-done.22), custom_call_target="tpu_custom_call" | custom-call | flops 300000000 | bytes 851968 | tf_op jit(solution)/shard_map/pallas_call | solution.py:22
  56.4 0.0 collective-permute-start.6
  56.4 0.0 collective-permute-start.7
  56.4 2.9 %collective-permute-start.8 = (f32[2,64,128]{2,1,0:T(8,128)}, f32[2,64,128]{2,1,0:T(8,128)S(1)}, u32[]{:S(2)}, u32[]{:S(2)}) collective-permute-start(f32[2,64,128]{2,1,0:T(8,128)} %get-tuple-element.68), channel_id=1, source_target_pairs={{0,24},{8,0},{16,8},{24,16},{1,25},{9,1},{17,9},{25,17},{2,26},{10... | collective-permute-start | bytes 196616 | tf_op jit(solution)/shard_map/ppermute | solution.py:440
  59.3 17.1 %shard_map.173 = (bf16[2,48,128]{2,1,0:T(8,128)(2,1)}, bf16[2,48,128]{2,1,0:T(8,128)(2,1)}, bf16[2,48,128]{2,1,0:T(8,128)(2,1)}, bf16[2,48,128]{2,1,0:T(8,128)(2,1)}) custom-call(bf16[6,48,512]{2,1,0:T(8,128)(2,1)} %get-tuple-element.69.refs_0_, bf16[512,128]{1,0:T(8,128)(2,1)} %constant.100.clone.refs_1_, f32[16,256]{1,0:T(8,128)} %bitcast.13, ...), custom_call_target="tpu_custom_call" | custom-call | flops 3623878656 | bytes 1000000 | tf_op jit(solution)/shard_map/pallas_call | solution.py:22
  76.4 0.6 collective-permute-start.10
  77.0 1.5 %collective-permute-start.11 = (bf16[2,48,128]{2,1,0:T(8,128)(2,1)}, bf16[2,48,128]{2,1,0:T(8,128)(2,1)S(1)}, u32[]{:S(2)}, u32[]{:S(2)}) collective-permute-start(bf16[2,48,128]{2,1,0:T(8,128)(2,1)} %get-tuple-element.72), channel_id=1, source_target_pairs={{0,16},{8,24},{16,0},{24,8},{1,17},{9,25},{17,1},{25,9},{2,18},{10... | collective-permute-start | bytes 73736 | tf_op jit(solution)/shard_map/ppermute | solution.py:440
  78.5 2.8 %collective-permute-done.10.refs_1_ = bf16[2,48,128]{2,1,0:T(8,128)(2,1)S(1)} collective-permute-done((bf16[2,48,128]{2,1,0:T(8,128)(2,1)}, bf16[2,48,128]{2,1,0:T(8,128)(2,1)S(1)}, u32[]{:S(2)}, u32[]{:S(2)}) %collective-permute-start.10) | collective-permute-done | bytes 24608 | tf_op jit(solution)/shard_map/ppermute | solution.py:440
  81.4 0.6 collective-permute-start.12
  81.9 0.7 slice.119
  82.6 0.0 collective-permute-done.11.refs_2_
  82.7 0.6 copy-done.14
  83.3 2.1 %collective-permute-done.12.refs_3_ = bf16[2,48,128]{2,1,0:T(8,128)(2,1)S(1)} collective-permute-done((bf16[2,48,128]{2,1,0:T(8,128)(2,1)}, bf16[2,48,128]{2,1,0:T(8,128)(2,1)S(1)}, u32[]{:S(2)}, u32[]{:S(2)}) %collective-permute-start.12) | collective-permute-done | bytes 24608 | tf_op jit(solution)/shard_map/ppermute | solution.py:440
  85.4 0.6 copy-done.15
  86.0 0.0 collective-permute-done.6.refs_1_
  86.0 0.6 copy-done.6
  86.6 0.0 collective-permute-done.7.refs_2_
  86.6 0.6 copy-done.7
  87.3 0.0 collective-permute-done.8.refs_3_
  87.3 0.7 slice-done.2
  88.0 0.0 slice-done.3
  88.1 0.1 collective-permute-start.9
  88.2 0.6 slice-done.4
  88.8 0.0 slice-done.5
  88.8 0.0 slice-done.6
  88.8 0.1 collective-permute-start.13
  88.9 1.2 %collective-permute-done.13.refs_4_ = bf16[4,48,128]{2,1,0:T(8,128)(2,1)S(1)} collective-permute-done((bf16[4,48,128]{2,1,0:T(8,128)(2,1)S(1)}, bf16[4,48,128]{2,1,0:T(8,128)(2,1)S(1)}, u32[]{:S(2)}, u32[]{:S(2)}) %collective-permute-start.13) | collective-permute-done | bytes 49184 | tf_op jit(solution)/shard_map/ppermute | solution.py:446
  90.1 0.6 copy-done.16
  90.7 2.3 %shard_map.174 = f32[4,4,32,128]{3,2,1,0:T(8,128)} custom-call(bf16[2,48,128]{2,1,0:T(8,128)(2,1)} %get-tuple-element.70.refs_0_, bf16[2,48,128]{2,1,0:T(8,128)(2,1)} %copy-done.13, bf16[2,48,128]{2,1,0:T(8,128)(2,1)} %copy-done.14, bf16[2,48,128]{2,1,0:T(8,128)(2,1)} %copy-done.15, bf16[4,48,128]{2,1,0:T(8,128)(2,1)} %copy-done.16, ...), custom_call_target="tpu_custom_call" | custom-call | flops 1000000 | bytes 524288 | tf_op jit(solution)/shard_map/pallas_call | solution.py:22
  93.0 0.0 collective-permute-done.9.refs_4_
  93.0 0.7 copy-done.9
  93.7 1.9 %shard_map.170 = f32[4,4,32,128]{3,2,1,0:T(8,128)} custom-call(f32[2,64,128]{2,1,0:T(8,128)} %get-tuple-element.65.refs_0_, f32[2,64,128]{2,1,0:T(8,128)} %copy-done.6, f32[2,64,128]{2,1,0:T(8,128)} %copy-done.7, f32[2,64,128]{2,1,0:T(8,128)} %copy-done.8, f32[4,64,128]{2,1,0:T(8,128)} %copy-done.9), custom_call_target="tpu_custom_call" | custom-call | flops 1000000 | bytes 524288 | tf_op jit(solution)/shard_map/pallas_call | solution.py:22
  (48 shorter events, 0.2 us)
Async XLA Ops:
  0.6 8.0 %copy-start.20 = (f32[8,128]{1,0:T(8,128)S(1)}, f32[8,128]{1,0:T(8,128)}, u32[]{:S(2)}) copy-start(f32[8,128]{1,0:T(8,128)} %param.26) | copy-start | bytes 12292
  0.6 8.1 %copy-start.10 = (bf16[2,128,128]{2,1,0:T(8,128)(2,1)S(1)}, bf16[2,128,128]{2,1,0:T(8,128)(2,1)}, u32[]{:S(2)}) copy-start(bf16[2,128,128]{2,1,0:T(8,128)(2,1)} %param.29) | copy-start | bytes 196612
  2.7 6.0 %copy-start = (f32[2,128,128]{2,1,0:T(8,128)S(1)}, f32[2,128,128]{2,1,0:T(8,128)}, u32[]{:S(2)}) copy-start(f32[2,128,128]{2,1,0:T(8,128)} %get-tuple-element.58.refs_0_) | copy-start | bytes 393220
  2.7 8.5 %collective-permute-start = (f32[2,128,128]{2,1,0:T(8,128)}, f32[2,128,128]{2,1,0:T(8,128)S(1)}, u32[]{:S(2)}, u32[]{:S(2)}) collective-permute-start(f32[2,128,128]{2,1,0:T(8,128)} %get-tuple-element.59), channel_id=1, source_target_pairs={{0,8},{8,16},{16,24},{24,0},{1,9},{9,17},{17,25},{25,1},{2,10},{10... | collective-permute-start | bytes 393224 | tf_op jit(solution)/shard_map/ppermute | solution.py:440
  5.7 7.5 %collective-permute-start.1 = (f32[2,128,128]{2,1,0:T(8,128)}, f32[2,128,128]{2,1,0:T(8,128)S(1)}, u32[]{:S(2)}, u32[]{:S(2)}) collective-permute-start(f32[2,128,128]{2,1,0:T(8,128)} %get-tuple-element.60), channel_id=1, source_target_pairs={{0,16},{8,24},{16,0},{24,8},{1,17},{9,25},{17,1},{25,9},{2,18},{10... | collective-permute-start | bytes 393224 | tf_op jit(solution)/shard_map/ppermute | solution.py:440
  7.2 6.6 %collective-permute-start.2 = (f32[2,128,128]{2,1,0:T(8,128)}, f32[2,128,128]{2,1,0:T(8,128)S(1)}, u32[]{:S(2)}, u32[]{:S(2)}) collective-permute-start(f32[2,128,128]{2,1,0:T(8,128)} %get-tuple-element.61), channel_id=1, source_target_pairs={{0,24},{8,0},{16,8},{24,16},{1,25},{9,1},{17,9},{25,17},{2,26},{10... | collective-permute-start | bytes 393224 | tf_op jit(solution)/shard_map/ppermute | solution.py:440
  8.7 0.8 copy-start.11
  11.2 0.7 copy-start.1
  13.1 0.6 copy-start.2
  13.8 0.9 slice-start
  13.8 0.9 copy-start.3
  13.8 0.9 slice-start.1
  14.7 0.8 copy-start.12
  14.7 2.2 %collective-permute-start.3 = (f32[4,128,128]{2,1,0:T(8,128)S(1)}, f32[4,128,128]{2,1,0:T(8,128)S(1)}, u32[]{:S(2)}, u32[]{:S(2)}) collective-permute-start(f32[4,128,128]{2,1,0:T(8,128)S(1)} %pad_maximum_fusion), channel_id=1, source_target_pairs={{0,4},{4,0},{1,5},{5,1},{2,6},{6,2},{3,7},{7,3},{8,12},{12,8},{9,1... | collective-permute-start | bytes 786440 | tf_op jit(solution)/shard_map/ppermute | solution.py:446
  15.6 16.5 %copy-start.17 = (bf16[2,128,384]{2,1,0:T(8,128)(2,1)}, bf16[2,128,384]{2,1,0:T(8,128)(2,1)S(1)}, u32[]{:S(2)}) copy-start(bf16[2,128,384]{2,1,0:T(8,128)(2,1)S(1)} %constant_dynamic-update-slice_fusion.refs_5_) | copy-start | bytes 589828
  16.2 0.7 copy-start.19
  16.9 2.9 %copy-start.18 = (bf16[2,8,128]{2,1,0:T(8,128)(2,1)}, bf16[2,8,128]{2,1,0:T(8,128)(2,1)S(1)}, u32[]{:S(2)}) copy-start(bf16[2,8,128]{2,1,0:T(8,128)(2,1)S(1)} %constant_dynamic-update-slice_fusion.3.refs_9_) | copy-start | bytes 12292
  16.9 0.7 copy-start.4
  19.8 24.1 %collective-permute-start.4 = (f32[5,2,4,8,128]{4,3,2,1,0:T(8,128)}, f32[5,2,4,8,128]{4,3,2,1,0:T(8,128)S(1)}, u32[]{:S(2)}, u32[]{:S(2)}) collective-permute-start(f32[5,2,4,8,128]{4,3,2,1,0:T(8,128)} %get-tuple-element.62), channel_id=1, source_target_pairs={{0,4},{4,8},{8,12},{12,16},{16,20},{20,24},{24,28},{28,1},{1,5},{5... | collective-permute-start | bytes 491528 | tf_op jit(solution)/shard_map/ppermute | solution.py:514
  19.9 24.1 %collective-permute-start.5 = (f32[5,2,4,8,128]{4,3,2,1,0:T(8,128)}, f32[5,2,4,8,128]{4,3,2,1,0:T(8,128)S(1)}, u32[]{:S(2)}, u32[]{:S(2)}) collective-permute-start(f32[5,2,4,8,128]{4,3,2,1,0:T(8,128)} %get-tuple-element.64), channel_id=1, source_target_pairs={{0,31},{4,0},{8,4},{12,8},{16,12},{20,16},{24,20},{28,24},{1,28},{... | collective-permute-start | bytes 491528 | tf_op jit(solution)/shard_map/ppermute | solution.py:514
  43.9 0.7 copy-start.21
  44.6 0.7 copy-start.22
  56.4 29.6 %collective-permute-start.6 = (f32[2,64,128]{2,1,0:T(8,128)}, f32[2,64,128]{2,1,0:T(8,128)S(1)}, u32[]{:S(2)}, u32[]{:S(2)}) collective-permute-start(f32[2,64,128]{2,1,0:T(8,128)} %get-tuple-element.66), channel_id=1, source_target_pairs={{0,8},{8,16},{16,24},{24,0},{1,9},{9,17},{17,25},{25,1},{2,10},{10... | collective-permute-start | bytes 196616 | tf_op jit(solution)/shard_map/ppermute | solution.py:440
  56.4 30.2 %collective-permute-start.7 = (f32[2,64,128]{2,1,0:T(8,128)}, f32[2,64,128]{2,1,0:T(8,128)S(1)}, u32[]{:S(2)}, u32[]{:S(2)}) collective-permute-start(f32[2,64,128]{2,1,0:T(8,128)} %get-tuple-element.67), channel_id=1, source_target_pairs={{0,16},{8,24},{16,0},{24,8},{1,17},{9,25},{17,1},{25,9},{2,18},{10... | collective-permute-start | bytes 196616 | tf_op jit(solution)/shard_map/ppermute | solution.py:440
  56.4 30.9 %collective-permute-start.8 = (f32[2,64,128]{2,1,0:T(8,128)}, f32[2,64,128]{2,1,0:T(8,128)S(1)}, u32[]{:S(2)}, u32[]{:S(2)}) collective-permute-start(f32[2,64,128]{2,1,0:T(8,128)} %get-tuple-element.68), channel_id=1, source_target_pairs={{0,24},{8,0},{16,8},{24,16},{1,25},{9,1},{17,9},{25,17},{2,26},{10... | collective-permute-start | bytes 196616 | tf_op jit(solution)/shard_map/ppermute | solution.py:440
  59.3 23.3 %copy-start.5 = (f32[2,64,128]{2,1,0:T(8,128)S(1)}, f32[2,64,128]{2,1,0:T(8,128)}, u32[]{:S(2)}) copy-start(f32[2,64,128]{2,1,0:T(8,128)} %get-tuple-element.65.refs_0_) | copy-start | bytes 196612
  76.4 4.9 %collective-permute-start.10 = (bf16[2,48,128]{2,1,0:T(8,128)(2,1)}, bf16[2,48,128]{2,1,0:T(8,128)(2,1)S(1)}, u32[]{:S(2)}, u32[]{:S(2)}) collective-permute-start(bf16[2,48,128]{2,1,0:T(8,128)(2,1)} %get-tuple-element.71), channel_id=1, source_target_pairs={{0,8},{8,16},{16,24},{24,0},{1,9},{9,17},{17,25},{25,1},{2,10},{10... | collective-permute-start | bytes 73736 | tf_op jit(solution)/shard_map/ppermute | solution.py:440
  77.0 5.7 %collective-permute-start.11 = (bf16[2,48,128]{2,1,0:T(8,128)(2,1)}, bf16[2,48,128]{2,1,0:T(8,128)(2,1)S(1)}, u32[]{:S(2)}, u32[]{:S(2)}) collective-permute-start(bf16[2,48,128]{2,1,0:T(8,128)(2,1)} %get-tuple-element.72), channel_id=1, source_target_pairs={{0,16},{8,24},{16,0},{24,8},{1,17},{9,25},{17,1},{25,9},{2,18},{10... | collective-permute-start | bytes 73736 | tf_op jit(solution)/shard_map/ppermute | solution.py:440
  81.4 1.3 %copy-start.13 = (bf16[2,48,128]{2,1,0:T(8,128)(2,1)}, bf16[2,48,128]{2,1,0:T(8,128)(2,1)S(1)}, u32[]{:S(2)}) copy-start(bf16[2,48,128]{2,1,0:T(8,128)(2,1)S(1)} %collective-permute-done.10.refs_1_) | copy-start | bytes 73732
  81.4 4.0 %collective-permute-start.12 = (bf16[2,48,128]{2,1,0:T(8,128)(2,1)}, bf16[2,48,128]{2,1,0:T(8,128)(2,1)S(1)}, u32[]{:S(2)}, u32[]{:S(2)}) collective-permute-start(bf16[2,48,128]{2,1,0:T(8,128)(2,1)} %get-tuple-element.73), channel_id=1, source_target_pairs={{0,24},{8,0},{16,8},{24,16},{1,25},{9,1},{17,9},{25,17},{2,26},{10... | collective-permute-start | bytes 73736 | tf_op jit(solution)/shard_map/ppermute | solution.py:440
  82.7 0.6 copy-start.14
  85.4 0.6 copy-start.15
  86.0 0.6 copy-start.6
  86.6 0.6 copy-start.7
  87.3 0.8 slice-start.2
  87.3 0.8 copy-start.8
  87.3 0.8 slice-start.3
  88.1 0.7 slice-start.4
  88.1 0.7 slice-start.5
  88.1 0.7 slice-start.6
  88.1 4.9 %collective-permute-start.9 = (f32[4,64,128]{2,1,0:T(8,128)S(1)}, f32[4,64,128]{2,1,0:T(8,128)S(1)}, u32[]{:S(2)}, u32[]{:S(2)}) collective-permute-start(f32[4,64,128]{2,1,0:T(8,128)S(1)} %pad_maximum_fusion.1), channel_id=1, source_target_pairs={{0,4},{4,0},{1,5},{5,1},{2,6},{6,2},{3,7},{7,3},{8,12},{12,8},{9,1... | collective-permute-start | bytes 393224 | tf_op jit(solution)/shard_map/ppermute | solution.py:446
  88.8 1.3 %collective-permute-start.13 = (bf16[4,48,128]{2,1,0:T(8,128)(2,1)S(1)}, bf16[4,48,128]{2,1,0:T(8,128)(2,1)S(1)}, u32[]{:S(2)}, u32[]{:S(2)}) collective-permute-start(bf16[4,48,128]{2,1,0:T(8,128)(2,1)S(1)} %pad_maximum_fusion.2), channel_id=1, source_target_pairs={{0,4},{4,0},{1,5},{5,1},{2,6},{6,2},{3,7},{7,3},{8,12},{12,8},{9,1... | collective-permute-start | bytes 147464 | tf_op jit(solution)/shard_map/ppermute | solution.py:446
  90.1 0.6 copy-start.16
  93.0 0.7 copy-start.9
where the time goes:
time: 96.2 us; the launch traced here: 95.6 us
  Pallas kernels  55.4 us (58%)
  starting transfers between devices  17.1 us (18%)
  local copies, waits for them, and re-layouts  13 us (14%)
  waiting for transfers between devices  9.11 us (9%)
    pallas_call x8, Pallas kernels, call(): pl.pallas_call(body, out_shape=tuple((jax.ShapeDtypeStruct(s, d) for s, d...  55.4 us
    ppermute x9, starting transfers between devices, over_x(): lax.ppermute(messages[d], 'gx', [(i, (i + d) % nx) for i in range(nx)])  11.5 us
    unnamed x49, local copies, waits for them, and re-layouts  9.97 us
    ppermute x9, waiting for transfers between devices, over_x(): lax.ppermute(messages[d], 'gx', [(i, (i + d) % nx) for i in range(nx)])  7.88 us
    ppermute x2, starting transfers between devices, ring_step(): return lax.ppermute(value, ('gx', 'gy', 'gz'), pairs)  5.34 us
    slice x19, local copies, waits for them, and re-layouts, over_y(): away = jnp.stack([piece[1] for piece in received], axis=0)  3.03 us
  transfers between devices with their start and end apart: 14, of which 5 were waited for; matrix products, arithmetic and copies ran while one was open for 2% of the time, Pallas kernels for 40%

commit v1 on v0

--- a/solution.py
+++ b/solution.py
@@ -1,5 +1,4 @@
 import functools
-import math
 
 import jax
 import jax.numpy as jnp
@@ -18,7 +17,7 @@
 VMEM = pl.BlockSpec(memory_space=pltpu.VMEM)
 
 
-def call(body, outs, args, scratch=(), flops=0, moved=0):
+def call(body, outs, args, scratch=(), flops=0, moved=0, room=16):
     return pl.pallas_call(
         body,
         out_shape=tuple(jax.ShapeDtypeStruct(s, d) for s, d in outs),
@@ -26,6 +25,7 @@
         out_specs=tuple([VMEM] * len(outs)),
         scratch_shapes=list(scratch),
         cost_estimate=pl.CostEstimate(flops=flops, bytes_accessed=moved, transcendentals=0),
+        compiler_params=pltpu.CompilerParams(vmem_limit_bytes=min(room, 60) * 1048576),
     )(*args)
 
 
@@ -94,72 +94,74 @@
         return xp, xm, yp, ym
 
 
-def stencil_kernel(nx, ny, fields, yl, blocks, first_state, planes, send, *refs):
+def stencil_kernel(nx, ny, fields, yl, blocks, first_state, planes, inner, outer, *refs):
     ins, refs = refs[:blocks], refs[blocks:]
+    kept = ()
+    if outer and inner:
+        kept, refs = refs[:3], refs[3:]
     filtered, refs = refs[0], refs[1:]
-    if send:
+    if outer:
         outs, refs = refs[:nx], refs[nx:]
-    whole, coef, one, two, three = refs
+        whole, coef, one, two, three = refs
+    else:
+        one, two, three, whole, coef = refs
     position = 0
     for ref in ins:
         count = ref.shape[0]
         whole[position : position + count] = ref[...]
         position += count
     zz = position
+    zc = zz - 2 * first_state
     shape = whole.shape[2:]
     lanes = shape[-1]
     shifts = Shifts(shape, yl, fields)
     upper = iota(shape, 1) < fields
 
-    def coefficients(z, carry):
+    def planes_of(margin):
+        due = range(margin, zz - margin)
+        if kept:
+            own = range(first_state + margin, first_state + zc - margin)
+            due = [z for z in due if z not in own]
+        due = sorted(due, key=lambda z: min(z, zz - 1 - z))
+        return due
+
+    for z in sorted({z for margin in (1, 2, 3) for z in planes_of(margin)}):
         nu = whole[z, 1]
-        for k, other in enumerate(shifts.pairs(nu)):
-            coef[z, k] = 0.5 * (nu + other)
-        coef[z, 4] = 0.5 * (nu + whole[z + 1, 1])
-        coef[z, 5] = 0.5 * (nu + whole[z - 1, 1])
-        return carry
-
-    lax.fori_loop(1, zz - 1, coefficients, 0)
-
-    def half_velocity(load, d):
-        top = jnp.broadcast_to(load(d), shape)
-        bottom = jnp.broadcast_to(load(fields + d), shape)
-        return 0.5 * jnp.where(upper, top, bottom)
+        total = None
+        for k, other in enumerate((*shifts.pairs(nu), whole[z + 1, 1], whole[z - 1, 1])):
+            face = nu + other
+            coef[z, k] = face
+            total = face if total is None else total + face
+        coef[z, 6] = 1.0 - (0.5 * TIME_STEP) * total
 
     def advanced(load, row, z):
         c = load(z)
         xp, xm, yp, ym = shifts.pairs(c)
-        zp, zm = load(z + 1), load(z - 1)
         total = None
-        for d, (p, m) in enumerate(((xp, xm), (yp, ym), (zp, zm))):
-            h = half_velocity(lambda r: row(z, r), d)
-            term = (coef[z, 2 * d] - h) * (p - c) + (coef[z, 2 * d + 1] + h) * (m - c)
+        for d, (p, m) in enumerate(((xp, xm), (yp, ym), (load(z + 1), load(z - 1)))):
+            top = jnp.broadcast_to(row(z, d), shape)
+            velocity = jnp.where(upper, top, jnp.broadcast_to(row(z, fields + d), shape))
+            term = (coef[z, 2 * d] - velocity) * p + (coef[z, 2 * d + 1] + velocity) * m
             total = term if total is None else total + term
-        return c + TIME_STEP * total
-
-    def segment_one(z, carry):
-        one[z] = advanced(
-            lambda i: whole[i, 0], lambda i, r: whole[i, 0, :, r : r + 1, :], z
-        )
-        return carry
-
-    def segment_two(z, carry):
+        return c * coef[z, 6] + (0.5 * TIME_STEP) * total
+
+    for z in planes_of(1):
+        one[z] = advanced(lambda i: whole[i, 0], lambda i, r: whole[i, 0, :, r : r + 1, :], z)
+    if kept:
+        for z in (1, 2, zc - 3, zc - 2):
+            one[first_state + z] = kept[0][z]
+        for z in (2, 3, zc - 4, zc - 3):
+            two[first_state + z] = kept[1][z]
+        three[first_state + 3 : first_state + zc - 3] = kept[2][3 : zc - 3]
+    for z in planes_of(2):
         moved = advanced(lambda i: one[i], lambda i, r: one[i, :, r : r + 1, :], z)
         two[z] = 0.75 * whole[z, 0] + 0.25 * moved
-        return carry
-
-    def last_segment(z, carry):
+    for z in planes_of(3):
         moved = advanced(lambda i: two[i], lambda i, r: two[i, :, r : r + 1, :], z)
         three[z] = whole[z, 0] * (1.0 / 3.0) + (2.0 / 3.0) * moved
-        return carry
-
-    lax.fori_loop(1, zz - 1, segment_one, 0)
-    lax.fori_loop(2, zz - 2, segment_two, 0)
-    lax.fori_loop(3, zz - 3, last_segment, 0)
-
-    if send:
+
+    if outer:
         a, b = lax.axis_index("gx"), lax.axis_index("gy")
-        zc = outs[0].shape[1] // fields
         mask = iota((zc // 2, 2 * fields, lanes), 1) < fields
         first = jnp.full((zc // 2, 2 * fields, lanes), b) == 0
         for d in range(nx):
@@ -190,14 +192,14 @@
                 ] = rounded[k]
 
 
-def gelu(x):
+def twice_gelu(x):
     inner = x * (0.7978845608028654 + 0.035677408136300125 * (x * x))
-    half = 0.5 * x
-    return half + half * jnp.tanh(inner)
+    return x + x * jnp.tanh(inner)
 
 
 def rms_scale(v, gain):
-    return v * lax.rsqrt(jnp.mean(v * v, axis=-1, keepdims=True) + EPSILON) * gain
+    total = jnp.sum(v * v, axis=-1, keepdims=True)
+    return v * lax.rsqrt(total + EPSILON * v.shape[-1]) * gain
 
 
 def matmul(v, w):
@@ -208,33 +210,70 @@
     return lax.dot_general(v, w, (((1,), (1,)), ((), ())), preferred_element_type=F32)
 
 
-def mixer(section, groups, same, weights, gains):
-    qkv_w, out_w, up_w, down_w = weights
+def attend(section, groups, same, weights, gain):
+    qkv_w, out_w = weights
     channels = section.shape[1]
     carried = section.astype(F32)
-    normed = rms_scale(carried, gains[0]).astype(BF16)
+    normed = rms_scale(carried, gain).astype(BF16)
+    yield
     qkv = matmul(normed, qkv_w).astype(BF16)
-    scale = channels ** (-0.5)
-    pieces = {}
+    yield
+    scale = channels ** (-0.5) * 1.4426950408889634
+    values, scores = [], []
     for group in groups:
         rows = jnp.concatenate([qkv[s : s + n] for s, n in group], axis=0)
-        q = rows[:, :channels]
-        k = rows[:, channels : 2 * channels]
-        v = rows[:, 2 * channels :]
-        scores = jnp.where(same, against(q, k) * scale, MASKED)
-        exponent = jnp.exp(scores - jnp.max(scores, axis=-1, keepdims=True))
-        total = jnp.sum(exponent, axis=-1, keepdims=True)
-        attention = (exponent * (1.0 / total)).astype(BF16)
-        result = matmul(attention, v).astype(BF16)
+        q, k = rows[:, :channels], rows[:, channels : 2 * channels]
+        values.append(rows[:, 2 * channels :])
+        scores.append(jnp.where(same, against(q, k), MASKED))
+        yield
+    weighted = []
+    for score in scores:
+        exponent = jnp.exp2((score - jnp.max(score, axis=-1, keepdims=True)) * scale)
+        weighted.append(exponent.astype(BF16))
+        yield
+    pieces = {}
+    for group, exponent, v in zip(groups, weighted, values):
+        summed = matmul(exponent, jnp.concatenate([v, jnp.ones_like(v)], axis=1))
+        result = (summed[:, :channels] * (1.0 / summed[:, channels:])).astype(BF16)
         at = 0
         for s, n in group:
             pieces[s] = result[at : at + n]
             at += n
+        yield
     attended = jnp.concatenate([pieces[s] for s in sorted(pieces)], axis=0)
-    residual = carried + matmul(attended, out_w)
-    again = rms_scale(residual, gains[1]).astype(BF16)
-    hidden = gelu(matmul(again, up_w)).astype(BF16)
-    return (residual + matmul(hidden, down_w)).astype(BF16)
+    return carried + matmul(attended, out_w)
+
+
+def feed(residual, weights, gain):
+    up_w, down_w = weights
+    again = rms_scale(residual, gain).astype(BF16)
+    yield
+    rows, hidden = residual.shape[0], up_w.shape[1]
+    wide, tall = min(256, hidden), min(64, rows)
+    total = None
+    for h in range(0, hidden, wide):
+        up = matmul(again, up_w[:, h : h + wide])
+        pieces = []
+        for r in range(0, rows, tall):
+            pieces.append(twice_gelu(up[r : r + tall]).astype(BF16))
+            yield
+        down = matmul(jnp.concatenate(pieces, axis=0), down_w[h : h + wide])
+        total = down if total is None else total + down
+        yield
+    return (residual + 0.5 * total).astype(BF16)
+
+
+def together(tasks):
+    results = [None] * len(tasks)
+    alive = dict(enumerate(tasks))
+    while alive:
+        for i in list(alive):
+            try:
+                next(alive[i])
+            except StopIteration as stop:
+                results[i] = stop.value
+                del alive[i]
+    return results
 
 
 def attention_kernel(nx, ny, fields, cells, step, last, earlier, *refs):
@@ -246,83 +285,78 @@
         if earlier:
             before, refs = refs[0], refs[1:]
         spread, refs = refs[0], refs[1:]
-        outs, coefficient = refs[:nx], refs[nx]
-    else:
-        coefficient = refs[0]
+        outs, refs = refs[:nx], refs[nx:]
+    coefficient = refs[0]
     xc, yc = cells
     channels = bias.shape[1]
     planes, height, wide = filtered.shape
     side = nx * xc * yc
     per_plane = ny * side
-    span = sel.shape[0]
-    cut = sel.shape[1]
-    along_x = [[(p * per_plane + b * side, side)] for p in range(step) for b in range(ny)]
-    together = max(1, 128 // (ny * xc * yc))
-    piece = together * xc * yc
+    cut, span = sel.shape
+    along_x = [[(b * side, side)] for b in range(ny)]
+    count = max(1, 128 // (ny * xc * yc))
+    piece = count * xc * yc
     along_y = [
-        [(p * per_plane + b * side + g * piece, piece) for b in range(ny)]
-        for p in range(step)
-        for g in range(nx // together)
+        [(b * side + g * piece, piece) for b in range(ny)] for g in range(nx // count)
     ]
     row, column = iota((side, side), 0), iota((side, side), 1)
     same_x_line = lax.rem(row, yc) == lax.rem(column, yc)
     count = ny * piece
     row, column = iota((count, count), 0), iota((count, count), 1)
     same_y_line = lax.rem(row, piece) // yc == lax.rem(column, piece) // yc
+    gain = [gains[i : i + 1] * channels**0.5 for i in range(6)]
+
+    def lift_and_first(block):
+        by_core = [[] for _ in range(ny)]
+        for g in range(wide // span):
+            parts = block[:, g * span : (g + 1) * span]
+            picked = against(sel[...], jnp.concatenate([parts] * 3, axis=0)).astype(BF16)
+            yield
+            both = matmul(picked, lift_w[...])
+            for b in range(ny):
+                by_core[b].append(both[:, b * channels : (b + 1) * channels])
+        yield
+        features = []
+        for rows in sum(by_core, []):
+            lifted = rows + bias[...]
+            features.append((0.5 * twice_gelu(rms_scale(lifted, gain[0]))).astype(BF16))
+            yield
+        features = jnp.concatenate(features, axis=0)
+        weights = qkv_w[0], out_w[0]
+        return (yield from attend(features, along_x, same_x_line, weights, gain[1]))
+
+    def first_feed(residual):
+        return feed(residual, (up_w[0], down_w[0]), gain[2])
+
+    def second(value):
+        return attend(value, along_y, same_y_line, (qkv_w[1], out_w[1]), gain[3])
+
+    def second_feed_and_head(residual, turned, plus):
+        value = yield from feed(residual, (up_w[1], down_w[1]), gain[4])
+        final = rms_scale(value.astype(F32), gain[5]).astype(BF16)
+        yield
+        logits = against(turned, final)
+        return logits if plus is None else logits + plus
+
+    def coefficient_of(logits):
+        return 0.05 + 0.45 * jax.nn.sigmoid(logits)
+
+    def chain(plane, turned):
+        value = yield from lift_and_first(plane)
+        value = yield from first_feed(value)
+        value = yield from second(value)
+        return (yield from second_feed_and_head(value, turned, None))
 
     def some_planes(i, carry):
-        block = filtered[pl.ds(i * step, step)].reshape(step * height, wide)
-        found = []
-        for g in range(wide // span):
-            picked = matmul(block[:, g * span : (g + 1) * span], sel[...])
-            third = height // 3
-            found.append(
-                [
-                    picked[p * height : p * height + third]
-                    + picked[p * height + third : p * height + 2 * third]
-                    + picked[p * height + 2 * third : (p + 1) * height]
-                    for p in range(step)
-                ]
-            )
-        lifted = []
-        for p in range(step):
-            by_core = [[] for _ in range(ny)]
-            for g in range(wide // span):
-                both = lax.dot_general(
-                    found[g][p],
-                    lift_w[...],
-                    (((0,), (0,)), ((), ())),
-                    precision=lax.Precision.HIGHEST,
-                    preferred_element_type=F32,
-                )
-                for b in range(ny):
-                    by_core[b].append(both[:, b * channels : (b + 1) * channels])
-            for b in range(ny):
-                lifted += by_core[b]
-        lifted = jnp.concatenate(lifted, axis=0) + bias[...]
-        features = gelu(rms_scale(lifted, gains[0:1])).astype(BF16)
-        first = mixer(
-            features,
-            along_x,
-            same_x_line,
-            (qkv_w[0], out_w[0], up_w[0], down_w[0]),
-            (gains[1:2], gains[2:3]),
-        )
-        second = mixer(
-            first,
-            along_y,
-            same_y_line,
-            (qkv_w[1], out_w[1], up_w[1], down_w[1]),
-            (gains[3:4], gains[4:5]),
-        )
-        final = rms_scale(second.astype(F32), gains[5:6]).astype(BF16)
-        logits = against(head[0], final[:per_plane])
-        for p in range(1, step):
-            logits = logits + against(head[p], final[p * per_plane : (p + 1) * per_plane])
-        coefficient[i] = 0.05 + 0.45 * jax.nn.sigmoid(logits)
+        tasks = [chain(filtered[i * width + p], head[p % step]) for p in range(width)]
+        found = together(tasks)
+        for p in range(0, width, step):
+            row = i * (width // step) + p // step
+            coefficient[row] = coefficient_of(sum(found[p + 1 : p + step], found[p]))
         return carry
 
-    lax.fori_loop(0, planes // step, some_planes, 0)
+    width = planes if planes * per_plane <= 2048 else step
+    lax.fori_loop(0, planes // width, some_planes, 0)
 
     if last:
         a, b = lax.axis_index("gx"), lax.axis_index("gy")
@@ -476,10 +510,16 @@
 
     eye = jnp.eye(ny, dtype=F32)
     lift_w = lift_weight.reshape(2, 1, fields, 1, channels) * eye.reshape(1, ny, 1, ny, 1)
-    lift_w = lift_w.reshape(2 * ny * fields, ny * channels)
+    rest = lift_w.reshape(2 * ny * fields, ny * channels)
+    stacked = []
+    for _ in range(3):
+        rounded = lax.reduce_precision(rest, 8, 7)
+        rest = rest - rounded
+        stacked += [rounded] * 3
+    lift_w = jnp.concatenate(stacked, axis=0).astype(BF16)
     qkv_w = jnp.concatenate([query_weight, key_weight, value_weight], axis=-1)
     group = max(1, 512 // lanes)
-    sel = jnp.asarray(pick_matrix(group, xl, yl), BF16)
+    sel = jnp.asarray(pick_matrix(group, xl, yl).T, BF16)
     turned_head = head_weight.T
 
     packed = call(
@@ -519,27 +559,31 @@
     inner = list(range(2, half - 2))
     outer = [p for p in range(-1, half + 1) if p not in inner]
 
-    def stencil(inputs, first_state, planes, send):
+    def stencil(inputs, first_state, planes, kept, last):
         zz = sum(v.shape[0] for v in inputs)
-        size = (zz,) + block[1:]
+        size = ((zz,) + block[1:], F32)
         outs = [((len(planes), 3 * 2 * ny * fields, nx * lanes), BF16)]
-        if send:
-            outs += [((ny, zc * fields, lanes), F32)] * nx
+        outs += [((ny, zc * fields, lanes), F32)] * nx if last else [size] * 3
         return call(
             functools.partial(
-                stencil_kernel, nx, ny, fields, yl, len(inputs), first_state, planes, send
+                stencil_kernel,
+                nx,
+                ny,
+                fields,
+                yl,
+                len(inputs),
+                first_state,
+                planes,
+                bool(kept) or not last,
+                last,
             ),
             outs,
-            inputs,
-            [
-                pltpu.VMEM((zz,) + block, F32),
-                pltpu.VMEM((zz, 6) + block[1:], F32),
-                pltpu.VMEM(size, F32),
-                pltpu.VMEM(size, F32),
-                pltpu.VMEM(size, F32),
-            ],
+            [*inputs, *kept],
+            [pltpu.VMEM((zz,) + block, F32), pltpu.VMEM((zz, 7) + block[1:], F32)]
+            + ([pltpu.VMEM(*size)] * 3 if last else []),
             flops=300000000,
             moved=8 * zz * nx * 8 * lanes,
+            room=16 * (nx // 4) ** 2,
         )
 
     def pairing(planes):
@@ -573,9 +617,10 @@
             ),
             outs if last else [(size, F32)],
             args,
-            [pltpu.VMEM(size, F32)] if last else [],
+            ([pltpu.VMEM(size, F32)] if last else []),
             flops=3 * work,
             moved=1000000,
+            room=16 * (nx // 4) ** 2,
         )
 
     place = {}
@@ -587,13 +632,13 @@
         depth += len(planes) // step * 8
     depth = -(-depth // 16) * 16
 
-    more = []
+    more, kept = [], []
     if inner:
-        (filtered,) = stencil([own], 0, inner, False)
+        filtered, *kept = stencil([own], 0, inner, [], False)
         more = list(attention(filtered, inner, [], None, False))
 
     ordered = below[::-1] + [own] + above
-    second = stencil(ordered, HALO, outer, True)
+    second = stencil(ordered, HALO, outer, kept, True)
     filtered, state_messages = second[0], list(second[1:])
     state_received = over_x(state_messages, nx)
 

time: 96.2 us -> 53.8 us (0.56)
  Pallas kernels: 55.4 us -> 16 us
  local copies, waits for them, and re-layouts: 13 us -> 8.89 us
  starting transfers between devices: 17.1 us -> 18.2 us
    pallas_call x8, Pallas kernels: 55.4 us -> 16 us  [call(): pl.pallas_call(body, out_shape=tuple((jax.ShapeDtypeStruct(s, d) for s, d...]
    unnamed x49 -> x54, local copies, waits for them, and re-layouts: 9.97 us -> 7.4 us
    slice x19 -> x17, local copies, waits for them, and re-layouts: 3.03 us -> 1.46 us  [over_y(): away = jnp.stack([piece[1] for piece in received], axis=0)]
    ppermute x9, starting transfers between devices: 11.5 us -> 12.6 us  [over_x(): lax.ppermute(messages[d], 'gx', [(i, (i + d) % nx) for i in range(nx)])]
  transfers between devices with their start and end apart: 14 -> 14, of which waited for: 5 -> 5; matrix products, arithmetic and copies ran while one was open for 2% -> 0% of each run, Pallas kernels for 40% -> 25%
where the time goes in v1:
time: 53.8 us; the launch traced here: 53.4 us
  starting transfers between devices  18.2 us (34%)
  Pallas kernels  16 us (30%)
  waiting for transfers between devices  9.07 us (17%)
  local copies, waits for them, and re-layouts  8.89 us (17%)
  between operations  1.09 us (2%)
    pallas_call x8, Pallas kernels, call(): pl.pallas_call(body, out_shape=tuple((jax.ShapeDtypeStruct(s, d) for s, d...  16 us
    ppermute x9, starting transfers between devices, over_x(): lax.ppermute(messages[d], 'gx', [(i, (i + d) % nx) for i in range(nx)])  12.6 us
    unnamed x54, local copies, waits for them, and re-layouts  7.4 us
    ppermute x9, waiting for transfers between devices, over_x(): lax.ppermute(messages[d], 'gx', [(i, (i + d) % nx) for i in range(nx)])  7.09 us
    ppermute x2, starting transfers between devices, ring_step(): return lax.ppermute(value, ('gx', 'gy', 'gz'), pairs)  5.39 us
    ppermute x3, waiting for transfers between devices, over_y(): return lax.ppermute(away, 'gy', [(i, (i + 1) % ny) for i in range(ny)])  1.98 us
    slice x17, local copies, waits for them, and re-layouts, over_y(): away = jnp.stack([piece[1] for piece in received], axis=0)  1.46 us
  transfers between devices with their start and end apart: 14, of which 5 were waited for; matrix products, arithmetic and copies ran while one was open for 0% of the time, Pallas kernels for 25%

profile of v1, /device:TPU:0, one launch (start us, length us, event | category | flops | bytes accessed | tf_op | source)
XLA Modules:
  0.0 53.4 jit_solution(10139555828259758004)
XLA Ops:
  0.6 0.9 %copy-done.5 = f32[4,4,32,128]{3,2,1,0:T(8,128)S(1)} copy-done((f32[4,4,32,128]{3,2,1,0:T(8,128)S(1)}, f32[4,4,32,128]{3,2,1,0:T(8,128)}, u32[]{:S(2)}) %copy-start.5) | copy-done | bytes 262168
  1.6 0.9 %copy-done.6 = f32[4,4,32,128]{3,2,1,0:T(8,128)S(1)} copy-done((f32[4,4,32,128]{3,2,1,0:T(8,128)S(1)}, f32[4,4,32,128]{3,2,1,0:T(8,128)}, u32[]{:S(2)}) %copy-start.6) | copy-done | bytes 262168
  2.5 0.2 shard_map.167
  2.8 0.0 copy-start.25
  2.8 3.0 %collective-permute-start = (f32[2,128,128]{2,1,0:T(8,128)S(1)}, f32[2,128,128]{2,1,0:T(8,128)S(1)}, u32[]{:S(2)}, u32[]{:S(2)}) collective-permute-start(f32[2,128,128]{2,1,0:T(8,128)S(1)} %get-tuple-element.63), channel_id=1, source_target_pairs={{0,8},{8,16},{16,24},{24,0},{1,9},{9,17},{17,25},{25,1},{2,10},{10... | collective-permute-start | bytes 393224 | tf_op jit(solution)/shard_map/ppermute | solution.py:474
  5.8 1.5 %collective-permute-start.1 = (f32[2,128,128]{2,1,0:T(8,128)S(1)}, f32[2,128,128]{2,1,0:T(8,128)S(1)}, u32[]{:S(2)}, u32[]{:S(2)}) collective-permute-start(f32[2,128,128]{2,1,0:T(8,128)S(1)} %get-tuple-element.64), channel_id=1, source_target_pairs={{0,16},{8,24},{16,0},{24,8},{1,17},{9,25},{17,1},{25,9},{2,18},{10... | collective-permute-start | bytes 393224 | tf_op jit(solution)/shard_map/ppermute | solution.py:474
  7.3 1.4 %collective-permute-start.2 = (f32[2,128,128]{2,1,0:T(8,128)S(1)}, f32[2,128,128]{2,1,0:T(8,128)S(1)}, u32[]{:S(2)}, u32[]{:S(2)}) collective-permute-start(f32[2,128,128]{2,1,0:T(8,128)S(1)} %get-tuple-element.65), channel_id=1, source_target_pairs={{0,24},{8,0},{16,8},{24,16},{1,25},{9,1},{17,9},{25,17},{2,26},{10... | collective-permute-start | bytes 393224 | tf_op jit(solution)/shard_map/ppermute | solution.py:474
  8.8 0.1 broadcast_multiply_fusion
  8.9 0.0 copy-start.21
  9.0 0.0 copy-start.24
  9.0 0.7 %copy-done.24 = bf16[128,4]{0,1:T(4,128)(2,1)S(1)} copy-done((bf16[128,4]{0,1:T(4,128)(2,1)S(1)}, bf16[128,4]{0,1:T(4,128)(2,1)}, u32[]{:S(2)}) %copy-start.24) | copy-done | bytes 1048
  9.7 0.1 copy-done.21
  9.7 0.0 copy-start.22
  9.8 0.8 %copy-done.22 = bf16[2,128,128]{2,1,0:T(8,128)(2,1)S(1)} copy-done((bf16[2,128,128]{2,1,0:T(8,128)(2,1)S(1)}, bf16[2,128,128]{2,1,0:T(8,128)(2,1)}, u32[]{:S(2)}) %copy-start.22) | copy-done | bytes 65560
  10.6 2.7 %collective-permute-done.2.refs_3_ = f32[2,128,128]{2,1,0:T(8,128)S(1)} collective-permute-done((f32[2,128,128]{2,1,0:T(8,128)S(1)}, f32[2,128,128]{2,1,0:T(8,128)S(1)}, u32[]{:S(2)}, u32[]{:S(2)}) %collective-permute-start.2) | collective-permute-done | bytes 131104 | tf_op jit(solution)/shard_map/ppermute | solution.py:474
  13.3 0.7 %copy-done.3 = f32[2,128,128]{2,1,0:T(8,128)} copy-done((f32[2,128,128]{2,1,0:T(8,128)}, f32[2,128,128]{2,1,0:T(8,128)S(1)}, u32[]{:S(2)}) %copy-start.3) | copy-done | bytes 131096
  14.0 0.0 collective-permute-done.1.refs_2_
  14.0 0.7 %copy-done.1 = f32[2,128,128]{2,1,0:T(8,128)} copy-done((f32[2,128,128]{2,1,0:T(8,128)}, f32[2,128,128]{2,1,0:T(8,128)S(1)}, u32[]{:S(2)}) %copy-start.1) | copy-done | bytes 131096
  14.6 0.0 collective-permute-done.refs_1_
  14.6 0.8 %slice-done.1 = f32[1,128,128]{2,1,0:T(8,128)S(1)} async-done(((f32[2,128,128]{2,1,0:T(8,128)}), f32[1,128,128]{2,1,0:T(8,128)S(1)}, s32[]{:S(2)}) %slice-start.1) | async-done | bytes 65560 | tf_op jit(solution)/shard_map/slice | solution.py:479
  15.5 0.0 slice-done
  15.5 0.0 copy-start.2
  15.5 0.1 collective-permute-start.3
  15.6 0.7 %copy-done.23 = bf16[2,128,128]{2,1,0:T(8,128)(2,1)S(1)} copy-done((bf16[2,128,128]{2,1,0:T(8,128)(2,1)S(1)}, bf16[2,128,128]{2,1,0:T(8,128)(2,1)}, u32[]{:S(2)}) %copy-start.23) | copy-done | bytes 65560
  16.4 0.8 %collective-permute-done.3.refs_4_ = f32[4,128,128]{2,1,0:T(8,128)S(1)} collective-permute-done((f32[4,128,128]{2,1,0:T(8,128)S(1)}, f32[4,128,128]{2,1,0:T(8,128)S(1)}, u32[]{:S(2)}, u32[]{:S(2)}) %collective-permute-start.3) | collective-permute-done | bytes 262176 | tf_op jit(solution)/shard_map/ppermute | solution.py:480
  17.1 0.1 shard_map.168
  17.3 0.2 collective-permute-start.4
  17.5 5.2 %collective-permute-start.5 = (f32[5,2,4,8,128]{4,3,2,1,0:T(8,128)S(1)}, f32[5,2,4,8,128]{4,3,2,1,0:T(8,128)S(1)}, u32[]{:S(2)}, u32[]{:S(2)}) collective-permute-start(f32[5,2,4,8,128]{4,3,2,1,0:T(8,128)S(1)} %get-tuple-element.68), channel_id=1, source_target_pairs={{0,31},{4,0},{8,4},{12,8},{16,12},{20,16},{24,20},{28,24},{1,28},{... | collective-permute-start | bytes 491528 | tf_op jit(solution)/shard_map/ppermute | solution.py:554
  22.7 0.0 copy-start.19
  22.7 1.5 %shard_map.169 = (bf16[4,48,512]{2,1,0:T(8,128)(2,1)S(1)}, f32[16,4,8,128]{3,2,1,0:T(8,128)S(1)}, f32[16,4,8,128]{3,2,1,0:T(8,128)S(1)}, f32[16,4,8,128]{3,2,1,0:T(8,128)S(1)}) custom-call(f32[16,2,4,8,128]{4,3,2,1,0:T(8,128)S(1)} %get-tuple-element.67.refs_0_.refs_1_), custom_call_target="tpu_custom_call" | custom-call | flops 300000000 | bytes 524288 | tf_op jit(solution)/shard_map/pallas_call | solution.py:21
  24.2 0.0 copy-start.18
  24.3 0.6 %copy-done.18 = f32[128]{0:T(128)S(1)} copy-done((f32[128]{0:T(128)S(1)}, f32[128]{0:T(128)}, u32[]{:S(2)}) %copy-start.18) | copy-done | bytes 536
  24.9 4.5 %shard_map.172.refs_10_ = f32[2,8,256]{2,1,0:T(8,128)S(1)} custom-call(bf16[4,48,512]{2,1,0:T(8,128)(2,1)S(1)} %get-tuple-element.77.refs_0_, bf16[128,512]{1,0:T(8,128)(2,1)S(1)} %copy-done.19, bf16[144,256]{1,0:T(8,128)(2,1)S(1)} %constant_dynamic-update-slice_fusion.refs_2_, f32[1,128]{1,0:T(1,128)S(1)} %bitcast.33, f32[6,128]{1,0:T(8,128)S(1)} %copy-done.17, ...), custom_call_target="tpu_custom_call" | custom-call | flops 2415919104 | bytes 1000000 | tf_op jit(solution)/shard_map/pallas_call | solution.py:21
  29.4 0.0 collective-permute-done.5.refs_2_
  29.4 0.0 copy-start.20
  29.4 1.6 %shard_map.170 = (bf16[6,48,512]{2,1,0:T(8,128)(2,1)S(1)}, f32[2,64,128]{2,1,0:T(8,128)S(1)}, f32[2,64,128]{2,1,0:T(8,128)S(1)}, f32[2,64,128]{2,1,0:T(8,128)S(1)}, f32[2,64,128]{2,1,0:T(8,128)S(1)}) custom-call(f32[5,2,4,8,128]{4,3,2,1,0:T(8,128)S(1)} %collective-permute-done.4.refs_0_, f32[16,2,4,8,128]{4,3,2,1,0:T(8,128)S(1)} %get-tuple-element.67.refs_0_.refs_1_, ...), custom_call_target="tpu_custom_call" | custom-call | flops 300000000 | bytes 851968 | tf_op jit(solution)/shard_map/pallas_call | solution.py:21
  31.0 0.1 collective-permute-start.6
  31.0 0.1 collective-permute-start.7
  31.1 2.8 %collective-permute-start.8 = (f32[2,64,128]{2,1,0:T(8,128)S(1)}, f32[2,64,128]{2,1,0:T(8,128)S(1)}, u32[]{:S(2)}, u32[]{:S(2)}) collective-permute-start(f32[2,64,128]{2,1,0:T(8,128)S(1)} %get-tuple-element.75), channel_id=1, source_target_pairs={{0,24},{8,0},{16,8},{24,16},{1,25},{9,1},{17,9},{25,17},{2,26},{10... | collective-permute-start | bytes 196616 | tf_op jit(solution)/shard_map/ppermute | solution.py:474
  34.0 6.0 %shard_map.173 = (bf16[2,48,128]{2,1,0:T(8,128)(2,1)S(1)}, bf16[2,48,128]{2,1,0:T(8,128)(2,1)S(1)}, bf16[2,48,128]{2,1,0:T(8,128)(2,1)S(1)}, bf16[2,48,128]{2,1,0:T(8,128)(2,1)S(1)}) custom-call(bf16[6,48,512]{2,1,0:T(8,128)(2,1)S(1)} %get-tuple-element.76.refs_0_, bf16[128,512]{1,0:T(8,128)(2,1)S(1)} %copy-done.19, ...), custom_call_target="tpu_custom_call" | custom-call | flops 3623878656 | bytes 1000000 | tf_op jit(solution)/shard_map/pallas_call | solution.py:21
  40.0 0.0 copy-start
  40.0 0.7 %collective-permute-start.12 = (bf16[2,48,128]{2,1,0:T(8,128)(2,1)S(1)}, bf16[2,48,128]{2,1,0:T(8,128)(2,1)S(1)}, u32[]{:S(2)}, u32[]{:S(2)}) collective-permute-start(bf16[2,48,128]{2,1,0:T(8,128)(2,1)S(1)} %get-tuple-element.81), channel_id=1, source_target_pairs={{0,24},{8,0},{16,8},{24,16},{1,25},{9,1},{17,9},{25,17},{2,26},{10... | collective-permute-start | bytes 73736 | tf_op jit(solution)/shard_map/ppermute | solution.py:474
  40.7 1.5 %collective-permute-start.11 = (bf16[2,48,128]{2,1,0:T(8,128)(2,1)S(1)}, bf16[2,48,128]{2,1,0:T(8,128)(2,1)S(1)}, u32[]{:S(2)}, u32[]{:S(2)}) collective-permute-start(bf16[2,48,128]{2,1,0:T(8,128)(2,1)S(1)} %get-tuple-element.80), channel_id=1, source_target_pairs={{0,16},{8,24},{16,0},{24,8},{1,17},{9,25},{17,1},{25,9},{2,18},{10... | collective-permute-start | bytes 73736 | tf_op jit(solution)/shard_map/ppermute | solution.py:474
  42.1 1.7 %collective-permute-done.12.refs_3_ = bf16[2,48,128]{2,1,0:T(8,128)(2,1)S(1)} collective-permute-done((bf16[2,48,128]{2,1,0:T(8,128)(2,1)S(1)}, bf16[2,48,128]{2,1,0:T(8,128)(2,1)S(1)}, u32[]{:S(2)}, u32[]{:S(2)}) %collective-permute-start.12) | collective-permute-done | bytes 24608 | tf_op jit(solution)/shard_map/ppermute | solution.py:474
  43.9 1.5 %collective-permute-start.10 = (bf16[2,48,128]{2,1,0:T(8,128)(2,1)S(1)}, bf16[2,48,128]{2,1,0:T(8,128)(2,1)S(1)}, u32[]{:S(2)}, u32[]{:S(2)}) collective-permute-start(bf16[2,48,128]{2,1,0:T(8,128)(2,1)S(1)} %get-tuple-element.79), channel_id=1, source_target_pairs={{0,8},{8,16},{16,24},{24,0},{1,9},{9,17},{17,25},{25,1},{2,10},{10... | collective-permute-start | bytes 73736 | tf_op jit(solution)/shard_map/ppermute | solution.py:474
  45.4 0.0 copy-start.9
  45.4 0.6 %copy-done.9 = bf16[2,48,128]{2,1,0:T(8,128)(2,1)} copy-done((bf16[2,48,128]{2,1,0:T(8,128)(2,1)}, bf16[2,48,128]{2,1,0:T(8,128)(2,1)S(1)}, u32[]{:S(2)}) %copy-start.9) | copy-done | bytes 24600
  46.0 2.6 %collective-permute-done.10.refs_1_ = bf16[2,48,128]{2,1,0:T(8,128)(2,1)S(1)} collective-permute-done((bf16[2,48,128]{2,1,0:T(8,128)(2,1)S(1)}, bf16[2,48,128]{2,1,0:T(8,128)(2,1)S(1)}, u32[]{:S(2)}, u32[]{:S(2)}) %collective-permute-start.10) | collective-permute-done | bytes 24608 | tf_op jit(solution)/shard_map/ppermute | solution.py:474
  48.6 0.6 %copy-done.11 = bf16[2,48,128]{2,1,0:T(8,128)(2,1)} copy-done((bf16[2,48,128]{2,1,0:T(8,128)(2,1)}, bf16[2,48,128]{2,1,0:T(8,128)(2,1)S(1)}, u32[]{:S(2)}) %copy-start.11) | copy-done | bytes 24600
  49.2 0.0 collective-permute-done.8.refs_3_
  49.2 0.0 collective-permute-done.7.refs_2_
  49.3 0.0 slice-start.3
  49.3 0.0 slice-start.4
  49.3 0.0 copy-start.13
  49.3 0.0 copy-start.10
  49.3 0.0 copy-start.12
  49.3 0.1 collective-permute-start.9
  49.4 0.5 slice-done.2
  50.0 0.0 slice-done.3
  50.0 0.0 slice-done.4
  50.0 0.1 collective-permute-start.13
  50.1 1.2 %collective-permute-done.13.refs_4_ = bf16[4,48,128]{2,1,0:T(8,128)(2,1)S(1)} collective-permute-done((bf16[4,48,128]{2,1,0:T(8,128)(2,1)S(1)}, bf16[4,48,128]{2,1,0:T(8,128)(2,1)S(1)}, u32[]{:S(2)}, u32[]{:S(2)}) %collective-permute-start.13) | collective-permute-done | bytes 49184 | tf_op jit(solution)/shard_map/ppermute | solution.py:480
  51.3 1.2 %shard_map.174 = f32[4,4,32,128]{3,2,1,0:T(8,128)} custom-call(bf16[2,48,128]{2,1,0:T(8,128)(2,1)S(1)} %get-tuple-element.78.refs_0_, bf16[2,48,128]{2,1,0:T(8,128)(2,1)S(1)} %copy-done.12, bf16[2,48,128]{2,1,0:T(8,128)(2,1)S(1)} %copy-done.10, bf16[2,48,128]{2,1,0:T(8,128)(2,1)S(1)} %copy-done.8, bf16[4,48,128]{2,1,0:T(8,128)(2,1)S(1)} %collective-permute-done.13.refs_4_, ...), custom_call_target="tpu_custom_call" | custom-call | flops 1000000 | bytes 524288 | tf_op jit(solution)/shard_map/pallas_call | solution.py:21
  52.6 0.9 %shard_map.171 = f32[4,4,32,128]{3,2,1,0:T(8,128)} custom-call(f32[2,64,128]{2,1,0:T(8,128)S(1)} %get-tuple-element.72.refs_0_, f32[2,64,128]{2,1,0:T(8,128)S(1)} %collective-permute-done.6.refs_1_, f32[2,64,128]{2,1,0:T(8,128)S(1)} %collective-permute-done.7.refs_2_, f32[2,64,128]{2,1,0:T(8,128)S(1)} %collective-permute-done.8.refs_3_, ...), custom_call_target="tpu_custom_call" | custom-call | flops 1000000 | bytes 524288 | tf_op jit(solution)/shard_map/pallas_call | solution.py:21
  (60 shorter events, 0.3 us)
Async XLA Ops:
  0.6 1.0 %copy-start.5 = (f32[4,4,32,128]{3,2,1,0:T(8,128)S(1)}, f32[4,4,32,128]{3,2,1,0:T(8,128)}, u32[]{:S(2)}) copy-start(f32[4,4,32,128]{3,2,1,0:T(8,128)} %flow.1) | copy-start | bytes 786436
  1.6 0.9 %copy-start.6 = (f32[4,4,32,128]{3,2,1,0:T(8,128)S(1)}, f32[4,4,32,128]{3,2,1,0:T(8,128)}, u32[]{:S(2)}) copy-start(f32[4,4,32,128]{3,2,1,0:T(8,128)} %visc.1) | copy-start | bytes 786436
  2.8 6.0 %copy-start.25 = (f32[8,128]{1,0:T(8,128)S(1)}, f32[8,128]{1,0:T(8,128)}, u32[]{:S(2)}) copy-start(f32[8,128]{1,0:T(8,128)} %param.26) | copy-start | bytes 12292
  2.8 11.9 %collective-permute-start = (f32[2,128,128]{2,1,0:T(8,128)S(1)}, f32[2,128,128]{2,1,0:T(8,128)S(1)}, u32[]{:S(2)}, u32[]{:S(2)}) collective-permute-start(f32[2,128,128]{2,1,0:T(8,128)S(1)} %get-tuple-element.63), channel_id=1, source_target_pairs={{0,8},{8,16},{16,24},{24,0},{1,9},{9,17},{17,25},{25,1},{2,10},{10... | collective-permute-start | bytes 393224 | tf_op jit(solution)/shard_map/ppermute | solution.py:474
  5.8 8.2 %collective-permute-start.1 = (f32[2,128,128]{2,1,0:T(8,128)S(1)}, f32[2,128,128]{2,1,0:T(8,128)S(1)}, u32[]{:S(2)}, u32[]{:S(2)}) collective-permute-start(f32[2,128,128]{2,1,0:T(8,128)S(1)} %get-tuple-element.64), channel_id=1, source_target_pairs={{0,16},{8,24},{16,0},{24,8},{1,17},{9,25},{17,1},{25,9},{2,18},{10... | collective-permute-start | bytes 393224 | tf_op jit(solution)/shard_map/ppermute | solution.py:474
  7.3 6.0 %collective-permute-start.2 = (f32[2,128,128]{2,1,0:T(8,128)S(1)}, f32[2,128,128]{2,1,0:T(8,128)S(1)}, u32[]{:S(2)}, u32[]{:S(2)}) collective-permute-start(f32[2,128,128]{2,1,0:T(8,128)S(1)} %get-tuple-element.65), channel_id=1, source_target_pairs={{0,24},{8,0},{16,8},{24,16},{1,25},{9,1},{17,9},{25,17},{2,26},{10... | collective-permute-start | bytes 393224 | tf_op jit(solution)/shard_map/ppermute | solution.py:474
  8.9 0.8 %copy-start.21 = (bf16[2,128,128]{2,1,0:T(8,128)(2,1)S(1)}, bf16[2,128,128]{2,1,0:T(8,128)(2,1)}, u32[]{:S(2)}) copy-start(bf16[2,128,128]{2,1,0:T(8,128)(2,1)} %param.29) | copy-start | bytes 196612
  9.0 0.7 %copy-start.24 = (bf16[128,4]{0,1:T(4,128)(2,1)S(1)}, bf16[128,4]{0,1:T(4,128)(2,1)}, u32[]{:S(2)}) copy-start(bf16[128,4]{0,1:T(4,128)(2,1)} %param.35) | copy-start | bytes 3076
  9.7 0.8 %copy-start.22 = (bf16[2,128,128]{2,1,0:T(8,128)(2,1)S(1)}, bf16[2,128,128]{2,1,0:T(8,128)(2,1)}, u32[]{:S(2)}) copy-start(bf16[2,128,128]{2,1,0:T(8,128)(2,1)} %param.30) | copy-start | bytes 196612
  13.3 0.7 %copy-start.3 = (f32[2,128,128]{2,1,0:T(8,128)}, f32[2,128,128]{2,1,0:T(8,128)S(1)}, u32[]{:S(2)}) copy-start(f32[2,128,128]{2,1,0:T(8,128)S(1)} %collective-permute-done.2.refs_3_) | copy-start | bytes 393220
  14.0 0.7 %copy-start.1 = (f32[2,128,128]{2,1,0:T(8,128)}, f32[2,128,128]{2,1,0:T(8,128)S(1)}, u32[]{:S(2)}) copy-start(f32[2,128,128]{2,1,0:T(8,128)S(1)} %collective-permute-done.1.refs_2_) | copy-start | bytes 393220
  14.6 0.8 %slice-start.1 = ((f32[2,128,128]{2,1,0:T(8,128)}), f32[1,128,128]{2,1,0:T(8,128)S(1)}, s32[]{:S(2)}) async-start(f32[2,128,128]{2,1,0:T(8,128)} %copy-done.3), calls=%async_computation.1 | async-start | bytes 131072 | tf_op jit(solution)/shard_map/slice | solution.py:479
  14.6 0.9 %slice-start = ((f32[2,128,128]{2,1,0:T(8,128)}), f32[1,128,128]{2,1,0:T(8,128)S(1)}, s32[]{:S(2)}) async-start(f32[2,128,128]{2,1,0:T(8,128)} %copy-done.1), calls=%async_computation | async-start | bytes 131072 | tf_op jit(solution)/shard_map/slice | solution.py:479
  15.5 0.8 %copy-start.23 = (bf16[2,128,128]{2,1,0:T(8,128)(2,1)S(1)}, bf16[2,128,128]{2,1,0:T(8,128)(2,1)}, u32[]{:S(2)}) copy-start(bf16[2,128,128]{2,1,0:T(8,128)(2,1)} %param.31) | copy-start | bytes 196612
  15.5 1.6 %copy-start.4 = (f32[2,128,128]{2,1,0:T(8,128)S(1)}, f32[2,128,128]{2,1,0:T(8,128)}, u32[]{:S(2)}) copy-start(f32[2,128,128]{2,1,0:T(8,128)} %copy-done.3) | copy-start | bytes 393220
  15.5 1.6 %copy-start.2 = (f32[2,128,128]{2,1,0:T(8,128)S(1)}, f32[2,128,128]{2,1,0:T(8,128)}, u32[]{:S(2)}) copy-start(f32[2,128,128]{2,1,0:T(8,128)} %copy-done.1) | copy-start | bytes 393220
  15.5 1.6 %collective-permute-start.3 = (f32[4,128,128]{2,1,0:T(8,128)S(1)}, f32[4,128,128]{2,1,0:T(8,128)S(1)}, u32[]{:S(2)}, u32[]{:S(2)}) collective-permute-start(f32[4,128,128]{2,1,0:T(8,128)S(1)} %pad_maximum_fusion), channel_id=1, source_target_pairs={{0,4},{4,0},{1,5},{5,1},{2,6},{6,2},{3,7},{7,3},{8,12},{12,8},{9,1... | collective-permute-start | bytes 786440 | tf_op jit(solution)/shard_map/ppermute | solution.py:480
  17.3 12.1 %collective-permute-start.4 = (f32[5,2,4,8,128]{4,3,2,1,0:T(8,128)S(1)}, f32[5,2,4,8,128]{4,3,2,1,0:T(8,128)S(1)}, u32[]{:S(2)}, u32[]{:S(2)}) collective-permute-start(f32[5,2,4,8,128]{4,3,2,1,0:T(8,128)S(1)} %get-tuple-element.66), channel_id=1, source_target_pairs={{0,4},{4,8},{8,12},{12,16},{16,20},{20,24},{24,28},{28,1},{1,5},{5... | collective-permute-start | bytes 491528 | tf_op jit(solution)/shard_map/ppermute | solution.py:554
  17.5 11.9 %collective-permute-start.5 = (f32[5,2,4,8,128]{4,3,2,1,0:T(8,128)S(1)}, f32[5,2,4,8,128]{4,3,2,1,0:T(8,128)S(1)}, u32[]{:S(2)}, u32[]{:S(2)}) collective-permute-start(f32[5,2,4,8,128]{4,3,2,1,0:T(8,128)S(1)} %get-tuple-element.68), channel_id=1, source_target_pairs={{0,31},{4,0},{8,4},{12,8},{16,12},{20,16},{24,20},{28,24},{1,28},{... | collective-permute-start | bytes 491528 | tf_op jit(solution)/shard_map/ppermute | solution.py:554
  22.7 1.6 %copy-start.14 = (bf16[2,128,512]{2,1,0:T(8,128)(2,1)S(1)}, bf16[2,128,512]{2,1,0:T(8,128)(2,1)}, u32[]{:S(2)}) copy-start(bf16[2,128,512]{2,1,0:T(8,128)(2,1)} %refs_7_.3) | copy-start | bytes 786436
  22.7 1.6 %copy-start.15 = (bf16[2,512,128]{2,1,0:T(8,128)(2,1)S(1)}, bf16[2,512,128]{2,1,0:T(8,128)(2,1)}, u32[]{:S(2)}) copy-start(bf16[2,512,128]{2,1,0:T(8,128)(2,1)} %refs_8_.3) | copy-start | bytes 786436
  22.7 1.6 %copy-start.16 = (bf16[2,128,128]{2,1,0:T(8,128)(2,1)S(1)}, bf16[2,128,128]{2,1,0:T(8,128)(2,1)}, u32[]{:S(2)}) copy-start(bf16[2,128,128]{2,1,0:T(8,128)(2,1)} %refs_6_.4) | copy-start | bytes 196612
  22.7 1.6 %copy-start.17 = (f32[6,128]{1,0:T(8,128)S(1)}, f32[6,128]{1,0:T(8,128)}, u32[]{:S(2)}) copy-start(f32[6,128]{1,0:T(8,128)} %refs_4_.3) | copy-start | bytes 9220
  22.7 1.6 %copy-start.19 = (bf16[128,512]{1,0:T(8,128)(2,1)S(1)}, bf16[128,512]{1,0:T(8,128)(2,1)}, u32[]{:S(2)}) copy-start(bf16[128,512]{1,0:T(8,128)(2,1)} %constant.100.clone.refs_1_) | copy-start | bytes 393220
  24.2 0.7 %copy-start.18 = (f32[128]{0:T(128)S(1)}, f32[128]{0:T(128)}, u32[]{:S(2)}) copy-start(f32[128]{0:T(128)} %param.27) | copy-start | bytes 1540
  29.4 4.6 %copy-start.20 = (bf16[256,256]{1,0:T(8,128)(2,1)S(1)}, bf16[256,256]{1,0:T(8,128)(2,1)}, u32[]{:S(2)}) copy-start(bf16[256,256]{1,0:T(8,128)(2,1)} %constant.101.clone.refs_11_) | copy-start | bytes 393220
  31.0 18.3 %collective-permute-start.6 = (f32[2,64,128]{2,1,0:T(8,128)S(1)}, f32[2,64,128]{2,1,0:T(8,128)S(1)}, u32[]{:S(2)}, u32[]{:S(2)}) collective-permute-start(f32[2,64,128]{2,1,0:T(8,128)S(1)} %get-tuple-element.73), channel_id=1, source_target_pairs={{0,8},{8,16},{16,24},{24,0},{1,9},{9,17},{17,25},{25,1},{2,10},{10... | collective-permute-start | bytes 196616 | tf_op jit(solution)/shard_map/ppermute | solution.py:474
  31.0 18.2 %collective-permute-start.7 = (f32[2,64,128]{2,1,0:T(8,128)S(1)}, f32[2,64,128]{2,1,0:T(8,128)S(1)}, u32[]{:S(2)}, u32[]{:S(2)}) collective-permute-start(f32[2,64,128]{2,1,0:T(8,128)S(1)} %get-tuple-element.74), channel_id=1, source_target_pairs={{0,16},{8,24},{16,0},{24,8},{1,17},{9,25},{17,1},{25,9},{2,18},{10... | collective-permute-start | bytes 196616 | tf_op jit(solution)/shard_map/ppermute | solution.py:474
  31.1 18.1 %collective-permute-start.8 = (f32[2,64,128]{2,1,0:T(8,128)S(1)}, f32[2,64,128]{2,1,0:T(8,128)S(1)}, u32[]{:S(2)}, u32[]{:S(2)}) collective-permute-start(f32[2,64,128]{2,1,0:T(8,128)S(1)} %get-tuple-element.75), channel_id=1, source_target_pairs={{0,24},{8,0},{16,8},{24,16},{1,25},{9,1},{17,9},{25,17},{2,26},{10... | collective-permute-start | bytes 196616 | tf_op jit(solution)/shard_map/ppermute | solution.py:474
  40.0 11.3 %copy-start = (bf16[384,512]{1,0:T(8,128)(2,1)S(1)}, bf16[384,512]{1,0:T(8,128)(2,1)}, u32[]{:S(2)}) copy-start(bf16[384,512]{1,0:T(8,128)(2,1)} %constant.102.clone.refs_5_) | copy-start | bytes 1179652
  40.0 3.9 %collective-permute-start.12 = (bf16[2,48,128]{2,1,0:T(8,128)(2,1)S(1)}, bf16[2,48,128]{2,1,0:T(8,128)(2,1)S(1)}, u32[]{:S(2)}, u32[]{:S(2)}) collective-permute-start(bf16[2,48,128]{2,1,0:T(8,128)(2,1)S(1)} %get-tuple-element.81), channel_id=1, source_target_pairs={{0,24},{8,0},{16,8},{24,16},{1,25},{9,1},{17,9},{25,17},{2,26},{10... | collective-permute-start | bytes 73736 | tf_op jit(solution)/shard_map/ppermute | solution.py:474
  40.7 4.7 %collective-permute-start.11 = (bf16[2,48,128]{2,1,0:T(8,128)(2,1)S(1)}, bf16[2,48,128]{2,1,0:T(8,128)(2,1)S(1)}, u32[]{:S(2)}, u32[]{:S(2)}) collective-permute-start(bf16[2,48,128]{2,1,0:T(8,128)(2,1)S(1)} %get-tuple-element.80), channel_id=1, source_target_pairs={{0,16},{8,24},{16,0},{24,8},{1,17},{9,25},{17,1},{25,9},{2,18},{10... | collective-permute-start | bytes 73736 | tf_op jit(solution)/shard_map/ppermute | solution.py:474
  43.9 1.5 %copy-start.7 = (bf16[2,48,128]{2,1,0:T(8,128)(2,1)}, bf16[2,48,128]{2,1,0:T(8,128)(2,1)S(1)}, u32[]{:S(2)}) copy-start(bf16[2,48,128]{2,1,0:T(8,128)(2,1)S(1)} %collective-permute-done.12.refs_3_) | copy-start | bytes 73732
  43.9 4.7 %collective-permute-start.10 = (bf16[2,48,128]{2,1,0:T(8,128)(2,1)S(1)}, bf16[2,48,128]{2,1,0:T(8,128)(2,1)S(1)}, u32[]{:S(2)}, u32[]{:S(2)}) collective-permute-start(bf16[2,48,128]{2,1,0:T(8,128)(2,1)S(1)} %get-tuple-element.79), channel_id=1, source_target_pairs={{0,8},{8,16},{16,24},{24,0},{1,9},{9,17},{17,25},{25,1},{2,10},{10... | collective-permute-start | bytes 73736 | tf_op jit(solution)/shard_map/ppermute | solution.py:474
  45.4 0.6 %copy-start.9 = (bf16[2,48,128]{2,1,0:T(8,128)(2,1)}, bf16[2,48,128]{2,1,0:T(8,128)(2,1)S(1)}, u32[]{:S(2)}) copy-start(bf16[2,48,128]{2,1,0:T(8,128)(2,1)S(1)} %collective-permute-done.11.refs_2_) | copy-start | bytes 73732
  48.6 0.6 %copy-start.11 = (bf16[2,48,128]{2,1,0:T(8,128)(2,1)}, bf16[2,48,128]{2,1,0:T(8,128)(2,1)S(1)}, u32[]{:S(2)}) copy-start(bf16[2,48,128]{2,1,0:T(8,128)(2,1)S(1)} %collective-permute-done.10.refs_1_) | copy-start | bytes 73732
  49.2 0.7 %slice-start.2 = ((bf16[2,48,128]{2,1,0:T(8,128)(2,1)}), bf16[1,48,128]{2,1,0:T(8,128)(2,1)S(1)}, s32[]{:S(2)}) async-start(bf16[2,48,128]{2,1,0:T(8,128)(2,1)} %copy-done.7), calls=%async_computation.2 | async-start | bytes 24576 | tf_op jit(solution)/shard_map/slice | solution.py:479
  49.3 0.7 %slice-start.3 = ((bf16[2,48,128]{2,1,0:T(8,128)(2,1)}), bf16[1,48,128]{2,1,0:T(8,128)(2,1)S(1)}, s32[]{:S(2)}) async-start(bf16[2,48,128]{2,1,0:T(8,128)(2,1)} %copy-done.9), calls=%async_computation.3 | async-start | bytes 24576 | tf_op jit(solution)/shard_map/slice | solution.py:479
  49.3 0.7 %slice-start.4 = ((bf16[2,48,128]{2,1,0:T(8,128)(2,1)}), bf16[1,48,128]{2,1,0:T(8,128)(2,1)S(1)}, s32[]{:S(2)}) async-start(bf16[2,48,128]{2,1,0:T(8,128)(2,1)} %copy-done.11), calls=%async_computation.4 | async-start | bytes 24576 | tf_op jit(solution)/shard_map/slice | solution.py:479
  49.3 2.0 %copy-start.13 = (bf16[128,128]{1,0:T(8,128)(2,1)S(1)}, bf16[128,128]{1,0:T(8,128)(2,1)}, u32[]{:S(2)}) copy-start(bf16[128,128]{1,0:T(8,128)(2,1)} %constant.103.clone.refs_6_) | copy-start | bytes 98308
  49.3 2.0 %copy-start.8 = (bf16[2,48,128]{2,1,0:T(8,128)(2,1)S(1)}, bf16[2,48,128]{2,1,0:T(8,128)(2,1)}, u32[]{:S(2)}) copy-start(bf16[2,48,128]{2,1,0:T(8,128)(2,1)} %copy-done.7) | copy-start | bytes 73732
  49.3 2.0 %copy-start.10 = (bf16[2,48,128]{2,1,0:T(8,128)(2,1)S(1)}, bf16[2,48,128]{2,1,0:T(8,128)(2,1)}, u32[]{:S(2)}) copy-start(bf16[2,48,128]{2,1,0:T(8,128)(2,1)} %copy-done.9) | copy-start | bytes 73732
  49.3 2.0 %copy-start.12 = (bf16[2,48,128]{2,1,0:T(8,128)(2,1)S(1)}, bf16[2,48,128]{2,1,0:T(8,128)(2,1)}, u32[]{:S(2)}) copy-start(bf16[2,48,128]{2,1,0:T(8,128)(2,1)} %copy-done.11) | copy-start | bytes 73732
  49.3 3.2 %collective-permute-start.9 = (f32[4,64,128]{2,1,0:T(8,128)S(1)}, f32[4,64,128]{2,1,0:T(8,128)S(1)}, u32[]{:S(2)}, u32[]{:S(2)}) collective-permute-start(f32[4,64,128]{2,1,0:T(8,128)S(1)} %pad_maximum_fusion.1), channel_id=1, source_target_pairs={{0,4},{4,0},{1,5},{5,1},{2,6},{6,2},{3,7},{7,3},{8,12},{12,8},{9,1... | collective-permute-start | bytes 393224 | tf_op jit(solution)/shard_map/ppermute | solution.py:480
  50.0 1.3 %collective-permute-start.13 = (bf16[4,48,128]{2,1,0:T(8,128)(2,1)S(1)}, bf16[4,48,128]{2,1,0:T(8,128)(2,1)S(1)}, u32[]{:S(2)}, u32[]{:S(2)}) collective-permute-start(bf16[4,48,128]{2,1,0:T(8,128)(2,1)S(1)} %pad_maximum_fusion.2), channel_id=1, source_target_pairs={{0,4},{4,0},{1,5},{5,1},{2,6},{6,2},{3,7},{7,3},{8,12},{12,8},{9,1... | collective-permute-start | bytes 147464 | tf_op jit(solution)/shard_map/ppermute | solution.py:480

commit v2 on v1

--- a/solution.py
+++ b/solution.py
@@ -1,4 +1,5 @@
 import functools
+import math
 
 import jax
 import jax.numpy as jnp
@@ -15,17 +16,18 @@
 F32 = jnp.float32
 BF16 = jnp.bfloat16
 VMEM = pl.BlockSpec(memory_space=pltpu.VMEM)
-
-
-def call(body, outs, args, scratch=(), flops=0, moved=0, room=16):
+HBM = pl.BlockSpec(memory_space=pltpu.HBM)
+
+
+def call(body, outs, args, scratch=(), flops=0, moved=0, room=16, where=(VMEM, VMEM)):
     return pl.pallas_call(
         body,
         out_shape=tuple(jax.ShapeDtypeStruct(s, d) for s, d in outs),
-        in_specs=[VMEM] * len(args),
-        out_specs=tuple([VMEM] * len(outs)),
+        in_specs=[where[0]] * len(args),
+        out_specs=tuple([where[1]] * len(outs)),
         scratch_shapes=list(scratch),
         cost_estimate=pl.CostEstimate(flops=flops, bytes_accessed=moved, transcendentals=0),
-        compiler_params=pltpu.CompilerParams(vmem_limit_bytes=min(room, 60) * 1048576),
+        compiler_params=pltpu.CompilerParams(vmem_limit_bytes=int(min(room, 63.93) * 1048576)),
     )(*args)
 
 
@@ -33,40 +35,94 @@
     return lax.broadcasted_iota(jnp.int32, shape, dim)
 
 
+def halves(v):
+    high = v.astype(BF16)
+    return high, (v - high.astype(F32)).astype(BF16)
+
+
 def pack_kernel(nx, ny, flow, visc, *rest):
-    outs, turned = rest[:nx], rest[nx]
+    outs, (turned, blocks, sems) = rest[:nx], rest[nx:]
     fields, xl, yl, zl = flow.shape
     lanes = xl * yl
     both = 2 * fields
+    copies = []
     for f in range(both):
-        source = flow[f] if f < fields else visc[f - fields]
-        turned[pl.ds(f, zl, stride=both), :] = source.reshape(lanes, zl).T
-    rows = zl * both // (nx * ny)
+        source = flow.at[f] if f < fields else visc.at[f - fields]
+        copies.append(pltpu.make_async_copy(source, blocks.at[f], sems.at[f]))
+        copies[f].start()
+    for f in range(both):
+        copies[f].wait()
+        kind, row = divmod(f, fields)
+        turned[kind, pl.ds(row, zl, stride=fields), :] = blocks[f].reshape(lanes, zl).T
+    rows = zl * fields // (nx * ny)
     a, b = lax.axis_index("gx"), lax.axis_index("gy")
     for d in range(nx):
         for e in range(ny):
             chunk = lax.rem(a + d, nx) * ny + lax.rem(b + e, ny)
             start = pl.multiple_of(chunk * rows, 8)
-            outs[d][e] = turned[pl.ds(start, rows), :]
-
-
-def unify_kernel(nx, fields, ring, *refs):
-    parts, got = refs[:nx], refs[nx]
-    whole = refs[nx + 1]
-    ends = refs[nx + 2 :]
+            high, low = halves(turned[0, pl.ds(start, rows), :])
+            outs[d][e, 0] = high
+            outs[d][e, 1] = low
+            outs[d][e, 2] = turned[1, pl.ds(start, rows), :].astype(BF16)
+
+
+def small_kernel(ny, fields, lift, bias, gains, head, small, lift_w, head_w):
+    channels = gains.shape[1]
+    small[:6] = gains[...] * channels**0.5
+    small[6:7] = bias[...]
+    small[7:8] = bias[...]
+    rest = lift[...]
+    rows = rest.shape[0]
+    upper = lax.rem(iota((rows, channels), 0), 2 * fields) < fields
+    for part in range(3):
+        rounded = rest.astype(BF16)
+        rest = rest - rounded.astype(F32)
+        exact = rounded.astype(F32)
+        swapped = pltpu.roll(exact, fields, 0)
+        for b in range(ny):
+            first = exact if b == 0 else swapped
+            second = swapped if b == 0 else exact
+            keep = upper if b == 0 else jnp.logical_not(upper)
+            both = jnp.concatenate(
+                [jnp.where(keep, first, 0.0), jnp.where(keep, second, 0.0)], axis=0
+            ).astype(BF16)
+            for again in range(3):
+                at = (part * 3 + again) * 2 * rows
+                lift_w[at : at + 2 * rows, b * channels : (b + 1) * channels] = both
+    turned = head[...].astype(F32).T
+    turned = jnp.concatenate([turned, jnp.zeros_like(turned)], axis=0)
+    head_w[0] = turned.astype(BF16)
+    head_w[1] = pltpu.roll(turned, fields, 0).astype(BF16)
+
+
+def sort_kernel(nx, *refs):
+    parts, (mine, away) = refs[:nx], refs[-2:]
+    for d in range(nx):
+        mine[d] = parts[d][0]
+        away[d] = parts[d][1]
+
+
+def unify_kernel(nx, fields, ring, mine, got, whole, *ends):
     a, b = lax.axis_index("gx"), lax.axis_index("gy")
-    rows, lanes = got.shape[1:]
-    zc = rows // (2 * fields)
-    low = iota((zc, 2 * fields, lanes), 1) < fields
-    first = jnp.full((zc, 2 * fields, lanes), b) == 0
+    rows, lanes = got.shape[2:]
+    zc = rows // fields
+    shape = zc // 2, 2 * fields, lanes
+    low = iota(shape, 1) < fields
+    first = jnp.full(shape, b) == 0
     for d in range(nx):
-        mine = parts[d][0].reshape(zc, 2 * fields, lanes)
-        theirs = got[d].reshape(zc, 2 * fields, lanes)
-        p = jnp.where(first, mine, theirs)
-        q = jnp.where(first, theirs, mine)
         where_from = lax.rem(a + nx - d, nx)
-        whole[:, 0, where_from] = jnp.where(low, p, pltpu.roll(q, fields, 1))
-        whole[:, 1, where_from] = jnp.where(low, pltpu.roll(p, fields, 1), q)
+        near = mine[d].astype(F32)
+        far = got[d].astype(F32)
+        for kind in range(2):
+            m = (near[2] if kind else near[0] + near[1]).reshape(shape)
+            t = (far[2] if kind else far[0] + far[1]).reshape(shape)
+            p = jnp.where(first, m, t)
+            q = jnp.where(first, t, m)
+            even = jnp.where(low, p, pltpu.roll(q, fields, 1))
+            odd = jnp.where(low, pltpu.roll(p, fields, 1), q)
+            for z in range(zc // 2):
+                whole[2 * z, kind, where_from] = even[z]
+                whole[2 * z + 1, kind, where_from] = odd[z]
     for s, count in enumerate(ring):
         ends[2 * s][...] = whole[:count]
         ends[2 * s + 1][...] = whole[zc - count :]
@@ -255,7 +311,7 @@
         up = matmul(again, up_w[:, h : h + wide])
         pieces = []
         for r in range(0, rows, tall):
-            pieces.append(twice_gelu(up[r : r + tall]).astype(BF16))
+            pieces.append(twice_gelu(up[r : r + tall].astype(BF16)))
             yield
         down = matmul(jnp.concatenate(pieces, axis=0), down_w[h : h + wide])
         total = down if total is None else total + down
@@ -277,18 +333,18 @@
 
 
 def attention_kernel(nx, ny, fields, cells, step, last, earlier, *refs):
-    (filtered, sel, lift_w, bias, gains, qkv_w, out_w, up_w, down_w, head), refs = (
-        refs[:10],
-        refs[10:],
-    )
+    filtered, sel, lift_w, gains, query_w, key_w, value_w = refs[:7]
+    (out_w, up_w, down_w, head), refs = refs[7:11], refs[11:]
     if last:
         if earlier:
             before, refs = refs[0], refs[1:]
         spread, refs = refs[0], refs[1:]
+        states, refs = refs[:nx], refs[nx:]
         outs, refs = refs[:nx], refs[nx:]
     coefficient = refs[0]
     xc, yc = cells
-    channels = bias.shape[1]
+    channels = gains.shape[1]
+    bias = gains[6:7]
     planes, height, wide = filtered.shape
     side = nx * xc * yc
     per_plane = ny * side
@@ -304,7 +360,10 @@
     count = ny * piece
     row, column = iota((count, count), 0), iota((count, count), 1)
     same_y_line = lax.rem(row, piece) // yc == lax.rem(column, piece) // yc
-    gain = [gains[i : i + 1] * channels**0.5 for i in range(6)]
+    gain = [gains[i : i + 1] for i in range(6)]
+    qkv_w = [
+        jnp.concatenate([query_w[i], key_w[i], value_w[i]], axis=1) for i in range(2)
+    ]
 
     def lift_and_first(block):
         by_core = [[] for _ in range(ny)]
@@ -318,7 +377,7 @@
         yield
         features = []
         for rows in sum(by_core, []):
-            lifted = rows + bias[...]
+            lifted = rows + bias
             features.append((0.5 * twice_gelu(rms_scale(lifted, gain[0]))).astype(BF16))
             yield
         features = jnp.concatenate(features, axis=0)
@@ -363,7 +422,8 @@
         every = coefficient[...].reshape(-1, per_plane)
         if earlier:
             every = jnp.concatenate([before[...].reshape(-1, per_plane), every], axis=0)
-        depth = outs[0].shape[1]
+        kept = 2 * states[0].shape[1]
+        depth = outs[0].shape[1] - kept
         if every.shape[0] < depth:
             blank = jnp.zeros((depth - every.shape[0], per_plane), F32)
             every = jnp.concatenate([every, blank], axis=0)
@@ -380,46 +440,55 @@
             near = jnp.concatenate(near, axis=1).astype(BF16)
             found = matmul(near, spread[...])
             zero, other = found[:, :width], found[:, width:]
-            outs[d][0] = jnp.where(first, zero, other).astype(BF16)
-            outs[d][1] = jnp.where(first, other, zero).astype(BF16)
-
-
-def state_kernel(nx, ny, *refs):
-    parts, got, out, rows = refs[:nx], refs[nx], refs[nx + 1], refs[nx + 2]
-    fields, xl, yl, zl = out.shape
+            high, low = halves(states[d][...])
+            outs[d][:, : kept // 2] = high
+            outs[d][:, kept // 2 : kept] = low
+            outs[d][0, kept:] = jnp.where(first, zero, other).astype(BF16)
+            outs[d][1, kept:] = jnp.where(first, other, zero).astype(BF16)
+
+
+def return_kernel(nx, ny, mine, got, along_z, across, *refs):
+    state_out, eddy_out, state_rows, coarse_rows, state, eddy, sems = refs
+    fields, xl, yl, zl = state_out.shape
     a, b = lax.axis_index("gx"), lax.axis_index("gy")
-    size = got.shape[1]
+    size = state_rows.shape[0] // (nx * ny)
     for d in range(nx):
-        source = lax.rem(a + nx - d, nx)
-        mine = pl.multiple_of((source * ny + b) * size, 8)
-        theirs = pl.multiple_of((source * ny + lax.rem(b + 1, ny)) * size, 8)
-        rows[pl.ds(mine, size), :] = parts[d][0]
-        rows[pl.ds(theirs, size), :] = got[d]
+        for piece, core in ((mine, b), (got, lax.rem(b + 1, ny))):
+            chunk = lax.rem(a + nx - d, nx) * ny + core
+            start = pl.multiple_of(chunk * size, 8)
+            high, low = piece[d, :size].astype(F32), piece[d, size : 2 * size].astype(F32)
+            state_rows[pl.ds(start, size), :] = high + low
+            coarse_rows[chunk] = piece[d, 2 * size :]
+    copies = []
+
+    def send(buffer, out, f):
+        copy = pltpu.make_async_copy(buffer.at[f], out.at[f], sems.at[len(copies)])
+        copy.start()
+        copies.append(copy)
+
     for f in range(fields):
-        out[f] = rows[pl.ds(f, zl, stride=fields), :].T.reshape(xl, yl, zl)
-
-
-def refine_kernel(nx, ny, *refs):
-    parts, (got, along_z, across, out, rows) = refs[:nx], refs[nx:]
-    fields, xl, yl, zl = out.shape
-    a, b = lax.axis_index("gx"), lax.axis_index("gy")
-    for d in range(nx):
-        source = lax.rem(a + nx - d, nx)
-        rows[source * ny + b] = parts[d][0]
-        rows[source * ny + lax.rem(b + 1, ny)] = got[d]
-    count, depth, width = rows.shape
-    coarse = rows[...].reshape(count * depth, width)
-    spread = lax.dot_general(
-        coarse, along_z[...], (((0,), (0,)), ((), ())), preferred_element_type=F32
-    )
-    total = None
-    for part in range(3):
-        rounded = spread.astype(BF16)
-        spread = spread - rounded.astype(F32)
-        product = matmul(across[...], rounded)
-        total = product if total is None else total + product
+        rows = state_rows[pl.ds(f, zl, stride=fields), :]
+        state[f] = rows.T.reshape(xl, yl, zl)
+        send(state, state_out, f)
+    count, depth, width = coarse_rows.shape
+    coarse = coarse_rows[...].reshape(count * depth, width)
     for f in range(fields):
-        out[f] = total[:, f * zl : (f + 1) * zl].reshape(xl, yl, zl)
+        spread = lax.dot_general(
+            coarse,
+            along_z[:, f * zl : (f + 1) * zl],
+            (((0,), (0,)), ((), ())),
+            preferred_element_type=F32,
+        )
+        total = None
+        for part in range(3):
+            rounded = spread.astype(BF16)
+            spread = spread - rounded.astype(F32)
+            product = matmul(across[...], rounded)
+            total = product if total is None else total + product
+        eddy[f] = total.reshape(xl, yl, zl)
+        send(eddy, eddy_out, f)
+    for copy in copies:
+        copy.wait()
 
 
 def pick_matrix(group, xl, yl):
@@ -468,16 +537,19 @@
     return table.reshape(chunks * depth, fields * chunks * zc)
 
 
-def over_x(messages, nx):
-    received = [messages[0]]
-    for d in range(1, nx):
-        received.append(lax.ppermute(messages[d], "gx", [(i, (i + d) % nx) for i in range(nx)]))
-    return received
-
-
-def over_y(received, ny):
-    away = jnp.stack([piece[1] for piece in received], axis=0)
-    return lax.ppermute(away, "gy", [(i, (i + 1) % ny) for i in range(ny)])
+def exchange(messages, nx, ny, meanwhile=()):
+    received = [messages[0]] + [None] * (nx - 1)
+    for d in sorted(range(1, nx), key=lambda d: abs(2 * d - nx)):
+        received[d] = lax.ppermute(messages[d], "gx", [(i, (i + d) % nx) for i in range(nx)])
+    shape = (nx,) + messages[0].shape[1:]
+    mine, away = call(
+        functools.partial(sort_kernel, nx),
+        [(shape, messages[0].dtype)] * 2,
+        [*received, *meanwhile],
+        flops=1000,
+        moved=8 * math.prod(shape),
+    )
+    return mine, lax.ppermute(away, "gy", [(i, (i + 1) % ny) for i in range(ny)])
 
 
 def per_device(
@@ -508,30 +580,35 @@
     both = 2 * fields
     per_plane = chunks * xc * yc
 
-    eye = jnp.eye(ny, dtype=F32)
-    lift_w = lift_weight.reshape(2, 1, fields, 1, channels) * eye.reshape(1, ny, 1, ny, 1)
-    rest = lift_w.reshape(2 * ny * fields, ny * channels)
-    stacked = []
-    for _ in range(3):
-        rounded = lax.reduce_precision(rest, 8, 7)
-        rest = rest - rounded
-        stacked += [rounded] * 3
-    lift_w = jnp.concatenate(stacked, axis=0).astype(BF16)
-    qkv_w = jnp.concatenate([query_weight, key_weight, value_weight], axis=-1)
     group = max(1, 512 // lanes)
     sel = jnp.asarray(pick_matrix(group, xl, yl).T, BF16)
-    turned_head = head_weight.T
+    small, lift_w, head_w = call(
+        functools.partial(small_kernel, ny, fields),
+        [
+            ((8, channels), F32),
+            ((9 * 2 * ny * fields, ny * channels), BF16),
+            ((2, 8, channels), BF16),
+        ],
+        [lift_weight, lift_bias.reshape(1, channels), norm_gains, head_weight],
+        flops=1000000,
+        moved=200000,
+    )
 
     packed = call(
         functools.partial(pack_kernel, nx, ny),
-        [((ny, zc * both, lanes), F32)] * nx,
+        [((ny, 3, zc * fields, lanes), BF16)] * nx,
         [flow_state, viscosity],
-        [pltpu.VMEM((zl * both, lanes), F32)],
+        [
+            pltpu.VMEM((2, zl * fields, lanes), F32),
+            pltpu.VMEM((both, xl, yl, zl), F32),
+            pltpu.SemaphoreType.DMA((both,)),
+        ],
         flops=1000000,
         moved=4 * zl * both * lanes,
+        room=53.5,
+        where=(HBM, VMEM),
     )
-    received = over_x(packed, nx)
-    got = over_y(received, ny)
+    mine, got = exchange(packed, nx, ny, [small])
     ring = []
     while sum(ring) < HALO:
         ring.append(min(zc, HALO - sum(ring)))
@@ -539,7 +616,7 @@
     unified = call(
         functools.partial(unify_kernel, nx, fields, ring),
         [((zc,) + block, F32)] + [((n,) + block, F32) for n in ring for _ in range(2)],
-        [*received, got],
+        [mine, got],
         flops=1000000,
         moved=8 * zl * both * lanes,
     )
@@ -589,31 +666,26 @@
     def pairing(planes):
         return 2 if len(planes) % 2 == 0 else 1
 
-    def heads(step):
-        out = jnp.zeros((step, 8, channels), BF16)
-        for p in range(step):
-            out = out.at[p, p * fields : (p + 1) * fields].set(turned_head)
-        return out
-
     def attention(filtered, planes, more, outs, last):
         step = pairing(planes)
         args = [
             filtered,
             sel,
             lift_w,
-            lift_bias.reshape(1, channels),
-            norm_gains,
-            qkv_w,
+            small,
+            query_weight,
+            key_weight,
+            value_weight,
             output_weight,
             up_weight,
             down_weight,
-            heads(step),
+            head_w,
         ] + more
         size = (len(planes) // step, 8, per_plane)
         work = len(planes) * per_plane * channels * (8 * channels + 4 * hidden) * 2
         return call(
             functools.partial(
-                attention_kernel, nx, ny, fields, (xc, yc), step, last, len(more) > 1
+                attention_kernel, nx, ny, fields, (xc, yc), step, last, bool(last and inner)
             ),
             outs if last else [(size, F32)],
             args,
@@ -640,34 +712,35 @@
     ordered = below[::-1] + [own] + above
     second = stencil(ordered, HALO, outer, kept, True)
     filtered, state_messages = second[0], list(second[1:])
-    state_received = over_x(state_messages, nx)
 
     width = -(-(xc + 2) * (yc + 2) // 128) * 128
     near = 128 // (xc * yc)
     spread = jnp.asarray(spread_matrix(ny, near, xc, yc, width), BF16)
+    rows = zc * fields
     messages = attention(
-        filtered, outer, more + [spread], [((ny, depth, width), BF16)] * nx, True
+        filtered,
+        outer,
+        more + [spread] + state_messages,
+        [((ny, 2 * rows + depth, width), BF16)] * nx,
+        True,
     )
-    coarse_received = over_x(list(messages), nx)
-    state_got = over_y(state_received, ny)
-    (state_next,) = call(
-        functools.partial(state_kernel, nx, ny),
-        [(flow_state.shape, F32)],
-        [*state_received, state_got],
-        [pltpu.VMEM((zl * fields, lanes), F32)],
+    mine, got = exchange(list(messages), nx, ny)
+    along_z = jnp.asarray(along_z_matrix(chunks, depth, place, fields, zc), BF16)
+    across = jnp.asarray(across_matrix(xl, yl, width), BF16)
+    state_next, eddy_field = call(
+        functools.partial(return_kernel, nx, ny),
+        [(flow_state.shape, F32)] * 2,
+        [mine, got, along_z, across],
+        [
+            pltpu.VMEM((zl * fields, lanes), F32),
+            pltpu.VMEM((chunks, depth, width), BF16),
+            pltpu.VMEM(flow_state.shape, F32),
+            pltpu.VMEM(flow_state.shape, F32),
+            pltpu.SemaphoreType.DMA((2 * fields,)),
+        ],
         flops=1000000,
         moved=8 * zl * fields * lanes,
-    )
-    coarse_got = over_y(coarse_received, ny)
-    along_z = jnp.asarray(along_z_matrix(chunks, depth, place, fields, zc), BF16)
-    across = jnp.asarray(across_matrix(xl, yl, width), BF16)
-    (eddy_field,) = call(
-        functools.partial(refine_kernel, nx, ny),
-        [(flow_state.shape, F32)],
-        [*coarse_received, coarse_got, along_z, across],
-        [pltpu.VMEM((chunks, depth, width), BF16)],
-        flops=1000000,
-        moved=8 * zl * fields * lanes,
+        where=(VMEM, HBM),
     )
     return (state_next, eddy_field)
 

time: 53.8 us -> 40.9 us (0.76)
  local copies, waits for them, and re-layouts: 8.89 us -> 0.85 us
  starting transfers between devices: 18.2 us -> 14.5 us
  waiting for transfers between devices: 9.07 us -> 8.27 us
    unnamed x54 -> x29, local copies, waits for them, and re-layouts: 7.4 us -> 0.85 us
    ppermute x12 -> x8, starting transfers between devices: 12.8 us -> 9.08 us  [the longest x6 8.94 us: exchange(): lax.ppermute(messages[d], 'gx', [(i, (i + d) % nx) for i in range(nx)])]
    slice x17 -> x0, local copies, waits for them, and re-layouts: 1.46 us -> none  [over_y(): away = jnp.stack([piece[1] for piece in received], axis=0)]
    ppermute x12 -> x8, waiting for transfers between devices: 9.07 us -> 8.27 us  [the longest x6 5.43 us: exchange(): lax.ppermute(messages[d], 'gx', [(i, (i + d) % nx) for i in range(nx)])]
    pallas_call x8 -> x10, Pallas kernels: 16 us -> 16 us  [call(): pl.pallas_call(body, out_shape=tuple((jax.ShapeDtypeStruct(s, d) for s, d...]
  transfers between devices with their start and end apart: 14 -> 10, of which waited for: 5 -> 7; matrix products, arithmetic and copies ran while one was open for 0% -> 0% of each run, Pallas kernels for 25% -> 14%
where the time goes in v2:
time: 40.9 us; the launch traced here: 40.4 us
  Pallas kernels  16 us (39%)
  starting transfers between devices  14.5 us (35%)
  waiting for transfers between devices  8.27 us (20%)
  local copies, waits for them, and re-layouts  0.85 us (2%)
  between operations  0.85 us (2%)
    pallas_call x10, Pallas kernels, call(): pl.pallas_call(body, out_shape=tuple((jax.ShapeDtypeStruct(s, d) for s, d...  16 us
    ppermute x6, starting transfers between devices, exchange(): lax.ppermute(messages[d], 'gx', [(i, (i + d) % nx) for i in range(nx)])  8.94 us
    ppermute x6, waiting for transfers between devices, exchange(): lax.ppermute(messages[d], 'gx', [(i, (i + d) % nx) for i in range(nx)])  5.43 us
    ppermute x2, starting transfers between devices, ring_step(): return lax.ppermute(value, ('gx', 'gy', 'gz'), pairs)  5.39 us
    ppermute x2, waiting for transfers between devices, exchange(): lax.ppermute(away, 'gy', [(i, (i + 1) % ny) for i in range(ny)])  2.83 us
    unnamed x29, local copies, waits for them, and re-layouts  0.85 us
  transfers between devices with their start and end apart: 10, of which 7 were waited for; matrix products, arithmetic and copies ran while one was open for 0% of the time, Pallas kernels for 14%

profile of v2, /device:TPU:0, one launch (start us, length us, event | category | flops | bytes accessed | tf_op | source)
XLA Modules:
  0.0 40.4 jit_solution(10821844902014834134)
XLA Ops:
  0.6 1.8 %shard_map.167 = (bf16[2,3,64,128]{3,2,1,0:T(8,128)(2,1)S(1)}, bf16[2,3,64,128]{3,2,1,0:T(8,128)(2,1)S(1)}, bf16[2,3,64,128]{3,2,1,0:T(8,128)(2,1)S(1)}, bf16[2,3,64,128]{3,2,1,0:T(8,128)(2,1)S(1)}) custom-call(f32[4,4,32,128]{3,2,1,0:T(8,128)} %flow.1, f32[4,4,32,128]{3,2,1,0:T(8,128)} %visc.1), custom_call_target="tpu_custom_call" | custom-call | flops 1000000 | bytes 524288 | tf_op jit(solution)/shard_map/pallas_call | solution.py:23
  2.4 3.0 %collective-permute-start = (bf16[2,3,64,128]{3,2,1,0:T(8,128)(2,1)S(1)}, bf16[2,3,64,128]{3,2,1,0:T(8,128)(2,1)S(1)}, u32[]{:S(2)}, u32[]{:S(2)}) collective-permute-start(bf16[2,3,64,128]{3,2,1,0:T(8,128)(2,1)S(1)} %get-tuple-element.30), channel_id=1, source_target_pairs={{0,8},{8,16},{16,24},{24,0},{1,9},{9,17},{17,25},{25,1},{2,10},{10... | collective-permute-start | bytes 294920 | tf_op jit(solution)/shard_map/ppermute | solution.py:543
  5.4 0.0 copy-start.13
  5.4 1.5 %collective-permute-start.1 = (bf16[2,3,64,128]{3,2,1,0:T(8,128)(2,1)S(1)}, bf16[2,3,64,128]{3,2,1,0:T(8,128)(2,1)S(1)}, u32[]{:S(2)}, u32[]{:S(2)}) collective-permute-start(bf16[2,3,64,128]{3,2,1,0:T(8,128)(2,1)S(1)} %get-tuple-element.31), channel_id=1, source_target_pairs={{0,16},{8,24},{16,0},{24,8},{1,17},{9,25},{17,1},{25,9},{2,18},{10... | collective-permute-start | bytes 294920 | tf_op jit(solution)/shard_map/ppermute | solution.py:543
  6.9 1.4 %collective-permute-start.2 = (bf16[2,3,64,128]{3,2,1,0:T(8,128)(2,1)S(1)}, bf16[2,3,64,128]{3,2,1,0:T(8,128)(2,1)S(1)}, u32[]{:S(2)}, u32[]{:S(2)}) collective-permute-start(bf16[2,3,64,128]{3,2,1,0:T(8,128)(2,1)S(1)} %get-tuple-element.32), channel_id=1, source_target_pairs={{0,24},{8,0},{16,8},{24,16},{1,25},{9,1},{17,9},{25,17},{2,26},{10... | collective-permute-start | bytes 294920 | tf_op jit(solution)/shard_map/ppermute | solution.py:543
  8.4 0.0 copy-done.13
  8.4 0.0 copy-start.2
  8.4 0.0 copy-start.3
  8.4 0.1 copy.18.head
  8.5 0.0 copy-start.4
  8.5 0.5 %copy-done.2 = f32[8,128]{1,0:T(8,128)S(1)} copy-done((f32[8,128]{1,0:T(8,128)S(1)}, f32[8,128]{1,0:T(8,128)}, u32[]{:S(2)}) %copy-start.2) | copy-done | bytes 4120
  9.1 0.0 copy-done.3
  9.1 0.1 copy-done.4
  9.2 0.1 shard_map.168
  9.2 0.4 collective-permute-done.refs_1_
  9.6 1.7 %collective-permute-done.1.refs_2_ = bf16[2,3,64,128]{3,2,1,0:T(8,128)(2,1)S(1)} collective-permute-done((bf16[2,3,64,128]{3,2,1,0:T(8,128)(2,1)S(1)}, bf16[2,3,64,128]{3,2,1,0:T(8,128)(2,1)S(1)}, u32[]{:S(2)}, u32[]{:S(2)}) %collective-permute-start.1) | collective-permute-done | bytes 98336 | tf_op jit(solution)/shard_map/ppermute | solution.py:543
  11.3 0.3 collective-permute-done.2.refs_3_
  11.6 0.1 collective-permute-start.3
  11.7 1.4 %collective-permute-done.3.got = bf16[4,3,64,128]{3,2,1,0:T(8,128)(2,1)S(1)} collective-permute-done((bf16[4,3,64,128]{3,2,1,0:T(8,128)(2,1)S(1)}, bf16[4,3,64,128]{3,2,1,0:T(8,128)(2,1)S(1)}, u32[]{:S(2)}, u32[]{:S(2)}) %collective-permute-start.3) | collective-permute-done | bytes 196640 | tf_op jit(solution)/shard_map/ppermute | solution.py:552
  13.1 0.1 shard_map.170
  13.3 0.2 collective-permute-start.4
  13.5 5.2 %collective-permute-start.5 = (f32[5,2,4,8,128]{4,3,2,1,0:T(8,128)S(1)}, f32[5,2,4,8,128]{4,3,2,1,0:T(8,128)S(1)}, u32[]{:S(2)}, u32[]{:S(2)}) collective-permute-start(f32[5,2,4,8,128]{4,3,2,1,0:T(8,128)S(1)} %get-tuple-element.38), channel_id=1, source_target_pairs={{0,31},{4,0},{8,4},{12,8},{16,12},{20,16},{24,20},{28,24},{1,28},{... | collective-permute-start | bytes 491528 | tf_op jit(solution)/shard_map/ppermute | solution.py:631
  18.7 0.0 copy-start.5
  18.7 0.0 copy-start.6
  18.7 0.0 copy-start.7
  18.7 0.0 copy-start.8
  18.7 0.0 copy-start.9
  18.7 0.0 copy-start.10
  18.7 0.0 copy-start.11
  18.7 1.5 %shard_map.171 = (bf16[4,48,512]{2,1,0:T(8,128)(2,1)S(1)}, f32[16,4,8,128]{3,2,1,0:T(8,128)S(1)}, f32[16,4,8,128]{3,2,1,0:T(8,128)S(1)}, f32[16,4,8,128]{3,2,1,0:T(8,128)S(1)}) custom-call(f32[16,2,4,8,128]{4,3,2,1,0:T(8,128)S(1)} %get-tuple-element.37.refs_0_.refs_1_), custom_call_target="tpu_custom_call" | custom-call | flops 300000000 | bytes 524288 | tf_op jit(solution)/shard_map/pallas_call | solution.py:23
  20.3 0.0 copy-done.5
  20.3 0.0 copy-done.6
  20.3 0.0 copy-done.7
  20.3 0.0 copy-done.8
  20.3 0.0 copy-done.9
  20.3 0.0 copy-done.10
  20.3 0.0 copy-done.11
  20.3 4.1 %shard_map.173.refs_11_ = f32[2,8,256]{2,1,0:T(8,128)S(1)} custom-call(bf16[4,48,512]{2,1,0:T(8,128)(2,1)S(1)} %get-tuple-element.45.refs_0_, bf16[128,512]{1,0:T(8,128)(2,1)S(1)} %copy-done.11, bf16[144,256]{1,0:T(8,128)(2,1)S(1)} %get-tuple-element.43.refs_2_, f32[8,128]{1,0:T(8,128)S(1)} %get-tuple-element.33.refs_4_.refs_3_, ...), custom_call_target="tpu_custom_call" | custom-call | flops 2415919104 | bytes 1000000 | tf_op jit(solution)/shard_map/pallas_call | solution.py:23
  24.4 0.0 collective-permute-done.4.refs_0_
  24.4 0.0 collective-permute-done.5.refs_2_
  24.5 0.0 copy-start.12
  24.5 1.6 %shard_map.172 = (bf16[6,48,512]{2,1,0:T(8,128)(2,1)S(1)}, f32[2,64,128]{2,1,0:T(8,128)S(1)}, f32[2,64,128]{2,1,0:T(8,128)S(1)}, f32[2,64,128]{2,1,0:T(8,128)S(1)}, f32[2,64,128]{2,1,0:T(8,128)S(1)}) custom-call(f32[5,2,4,8,128]{4,3,2,1,0:T(8,128)S(1)} %collective-permute-done.4.refs_0_, f32[16,2,4,8,128]{4,3,2,1,0:T(8,128)S(1)} %get-tuple-element.37.refs_0_.refs_1_, ...), custom_call_target="tpu_custom_call" | custom-call | flops 300000000 | bytes 851968 | tf_op jit(solution)/shard_map/pallas_call | solution.py:23
  26.0 0.0 copy-done.12
  26.1 0.0 copy-start
  26.1 5.5 %shard_map.174 = (bf16[2,176,128]{2,1,0:T(8,128)(2,1)S(1)}, bf16[2,176,128]{2,1,0:T(8,128)(2,1)S(1)}, bf16[2,176,128]{2,1,0:T(8,128)(2,1)S(1)}, bf16[2,176,128]{2,1,0:T(8,128)(2,1)S(1)}) custom-call(bf16[6,48,512]{2,1,0:T(8,128)(2,1)S(1)} %get-tuple-element.42.refs_0_, bf16[128,512]{1,0:T(8,128)(2,1)S(1)} %copy-done.11, ...), custom_call_target="tpu_custom_call" | custom-call | flops 3623878656 | bytes 1000000 | tf_op jit(solution)/shard_map/pallas_call | solution.py:23
  31.6 0.1 collective-permute-start.6
  31.7 0.1 collective-permute-start.7
  31.7 2.8 %collective-permute-start.8 = (bf16[2,176,128]{2,1,0:T(8,128)(2,1)S(1)}, bf16[2,176,128]{2,1,0:T(8,128)(2,1)S(1)}, u32[]{:S(2)}, u32[]{:S(2)}) collective-permute-start(bf16[2,176,128]{2,1,0:T(8,128)(2,1)S(1)} %get-tuple-element.53), channel_id=1, source_target_pairs={{0,24},{8,0},{16,8},{24,16},{1,25},{9,1},{17,9},{25,17},{2,26},{10... | collective-permute-start | bytes 270344 | tf_op jit(solution)/shard_map/ppermute | solution.py:543
  34.6 2.6 %collective-permute-done.6.refs_1_ = bf16[2,176,128]{2,1,0:T(8,128)(2,1)S(1)} collective-permute-done((bf16[2,176,128]{2,1,0:T(8,128)(2,1)S(1)}, bf16[2,176,128]{2,1,0:T(8,128)(2,1)S(1)}, u32[]{:S(2)}, u32[]{:S(2)}) %collective-permute-start.6) | collective-permute-done | bytes 90144 | tf_op jit(solution)/shard_map/ppermute | solution.py:543
  37.2 0.0 collective-permute-done.7.refs_2_
  37.2 0.4 %collective-permute-done.8.refs_3_ = bf16[2,176,128]{2,1,0:T(8,128)(2,1)S(1)} collective-permute-done((bf16[2,176,128]{2,1,0:T(8,128)(2,1)S(1)}, bf16[2,176,128]{2,1,0:T(8,128)(2,1)S(1)}, u32[]{:S(2)}, u32[]{:S(2)}) %collective-permute-start.8) | collective-permute-done | bytes 90144 | tf_op jit(solution)/shard_map/ppermute | solution.py:543
  37.6 0.0 copy-start.1
  37.7 0.1 collective-permute-start.9
  37.8 1.4 %collective-permute-done.9.got = bf16[4,176,128]{2,1,0:T(8,128)(2,1)S(1)} collective-permute-done((bf16[4,176,128]{2,1,0:T(8,128)(2,1)S(1)}, bf16[4,176,128]{2,1,0:T(8,128)(2,1)S(1)}, u32[]{:S(2)}, u32[]{:S(2)}) %collective-permute-start.9) | collective-permute-done | bytes 180256 | tf_op jit(solution)/shard_map/ppermute | solution.py:552
  39.2 0.0 copy-done
  39.2 0.0 copy-done.1
  39.2 1.3 %shard_map.176 = (f32[4,4,32,128]{3,2,1,0:T(8,128)}, f32[4,4,32,128]{3,2,1,0:T(8,128)}) custom-call(bf16[4,176,128]{2,1,0:T(8,128)(2,1)S(1)} %get-tuple-element.54.mine, bf16[4,176,128]{2,1,0:T(8,128)(2,1)S(1)} %collective-permute-done.9.got, bf16[384,512]{1,0:T(8,128)(2,1)S(1)} %copy-done, bf16[128,128]{1,0:T(8,128)(2,1)S(1)} %copy-done.1), custom_call_target="tpu_custom_call" | custom-call | flops 1000000 | bytes 524288 | tf_op jit(solution)/shard_map/pallas_call | solution.py:23
  (2 shorter events, 0.1 us)
Async XLA Ops:
  2.4 7.2 %collective-permute-start = (bf16[2,3,64,128]{3,2,1,0:T(8,128)(2,1)S(1)}, bf16[2,3,64,128]{3,2,1,0:T(8,128)(2,1)S(1)}, u32[]{:S(2)}, u32[]{:S(2)}) collective-permute-start(bf16[2,3,64,128]{3,2,1,0:T(8,128)(2,1)S(1)} %get-tuple-element.30), channel_id=1, source_target_pairs={{0,8},{8,16},{16,24},{24,0},{1,9},{9,17},{17,25},{25,1},{2,10},{10... | collective-permute-start | bytes 294920 | tf_op jit(solution)/shard_map/ppermute | solution.py:543
  5.4 3.0 %copy-start.13 = (bf16[128,4]{0,1:T(4,128)(2,1)S(1)}, bf16[128,4]{0,1:T(4,128)(2,1)}, u32[]{:S(2)}) copy-start(bf16[128,4]{0,1:T(4,128)(2,1)} %param.27) | copy-start | bytes 3076
  5.4 5.9 %collective-permute-start.1 = (bf16[2,3,64,128]{3,2,1,0:T(8,128)(2,1)S(1)}, bf16[2,3,64,128]{3,2,1,0:T(8,128)(2,1)S(1)}, u32[]{:S(2)}, u32[]{:S(2)}) collective-permute-start(bf16[2,3,64,128]{3,2,1,0:T(8,128)(2,1)S(1)} %get-tuple-element.31), channel_id=1, source_target_pairs={{0,16},{8,24},{16,0},{24,8},{1,17},{9,25},{17,1},{25,9},{2,18},{10... | collective-permute-start | bytes 294920 | tf_op jit(solution)/shard_map/ppermute | solution.py:543
  6.9 4.7 %collective-permute-start.2 = (bf16[2,3,64,128]{3,2,1,0:T(8,128)(2,1)S(1)}, bf16[2,3,64,128]{3,2,1,0:T(8,128)(2,1)S(1)}, u32[]{:S(2)}, u32[]{:S(2)}) collective-permute-start(bf16[2,3,64,128]{3,2,1,0:T(8,128)(2,1)S(1)} %get-tuple-element.32), channel_id=1, source_target_pairs={{0,24},{8,0},{16,8},{24,16},{1,25},{9,1},{17,9},{25,17},{2,26},{10... | collective-permute-start | bytes 294920 | tf_op jit(solution)/shard_map/ppermute | solution.py:543
  8.4 0.7 %copy-start.2 = (f32[8,128]{1,0:T(8,128)S(1)}, f32[8,128]{1,0:T(8,128)}, u32[]{:S(2)}) copy-start(f32[8,128]{1,0:T(8,128)} %lift.1) | copy-start | bytes 12292
  8.4 0.7 %copy-start.3 = (f32[6,128]{1,0:T(8,128)S(1)}, f32[6,128]{1,0:T(8,128)}, u32[]{:S(2)}) copy-start(f32[6,128]{1,0:T(8,128)} %gains.1) | copy-start | bytes 9220
  8.5 0.7 %copy-start.4 = (f32[128]{0:T(128)S(1)}, f32[128]{0:T(128)}, u32[]{:S(2)}) copy-start(f32[128]{0:T(128)} %param.19) | copy-start | bytes 1540
  11.6 1.5 %collective-permute-start.3 = (bf16[4,3,64,128]{3,2,1,0:T(8,128)(2,1)S(1)}, bf16[4,3,64,128]{3,2,1,0:T(8,128)(2,1)S(1)}, u32[]{:S(2)}, u32[]{:S(2)}) collective-permute-start(bf16[4,3,64,128]{3,2,1,0:T(8,128)(2,1)S(1)} %get-tuple-element.35), channel_id=1, source_target_pairs={{0,4},{4,0},{1,5},{5,1},{2,6},{6,2},{3,7},{7,3},{8,12},{12,8},{9,1... | collective-permute-start | bytes 589832 | tf_op jit(solution)/shard_map/ppermute | solution.py:552
  13.3 11.2 %collective-permute-start.4 = (f32[5,2,4,8,128]{4,3,2,1,0:T(8,128)S(1)}, f32[5,2,4,8,128]{4,3,2,1,0:T(8,128)S(1)}, u32[]{:S(2)}, u32[]{:S(2)}) collective-permute-start(f32[5,2,4,8,128]{4,3,2,1,0:T(8,128)S(1)} %get-tuple-element.36), channel_id=1, source_target_pairs={{0,4},{4,8},{8,12},{12,16},{16,20},{20,24},{24,28},{28,1},{1,5},{5... | collective-permute-start | bytes 491528 | tf_op jit(solution)/shard_map/ppermute | solution.py:631
  13.5 11.0 %collective-permute-start.5 = (f32[5,2,4,8,128]{4,3,2,1,0:T(8,128)S(1)}, f32[5,2,4,8,128]{4,3,2,1,0:T(8,128)S(1)}, u32[]{:S(2)}, u32[]{:S(2)}) collective-permute-start(f32[5,2,4,8,128]{4,3,2,1,0:T(8,128)S(1)} %get-tuple-element.38), channel_id=1, source_target_pairs={{0,31},{4,0},{8,4},{12,8},{16,12},{20,16},{24,20},{28,24},{1,28},{... | collective-permute-start | bytes 491528 | tf_op jit(solution)/shard_map/ppermute | solution.py:631
  18.7 1.6 %copy-start.5 = (bf16[2,128,512]{2,1,0:T(8,128)(2,1)S(1)}, bf16[2,128,512]{2,1,0:T(8,128)(2,1)}, u32[]{:S(2)}) copy-start(bf16[2,128,512]{2,1,0:T(8,128)(2,1)} %refs_8_.3) | copy-start | bytes 786436
  18.7 1.6 %copy-start.6 = (bf16[2,512,128]{2,1,0:T(8,128)(2,1)S(1)}, bf16[2,512,128]{2,1,0:T(8,128)(2,1)}, u32[]{:S(2)}) copy-start(bf16[2,512,128]{2,1,0:T(8,128)(2,1)} %refs_9_.3) | copy-start | bytes 786436
  18.7 1.6 %copy-start.7 = (bf16[2,128,128]{2,1,0:T(8,128)(2,1)S(1)}, bf16[2,128,128]{2,1,0:T(8,128)(2,1)}, u32[]{:S(2)}) copy-start(bf16[2,128,128]{2,1,0:T(8,128)(2,1)} %refs_4_.3) | copy-start | bytes 196612
  18.7 1.6 %copy-start.8 = (bf16[2,128,128]{2,1,0:T(8,128)(2,1)S(1)}, bf16[2,128,128]{2,1,0:T(8,128)(2,1)}, u32[]{:S(2)}) copy-start(bf16[2,128,128]{2,1,0:T(8,128)(2,1)} %refs_5_.3) | copy-start | bytes 196612
  18.7 1.6 %copy-start.9 = (bf16[2,128,128]{2,1,0:T(8,128)(2,1)S(1)}, bf16[2,128,128]{2,1,0:T(8,128)(2,1)}, u32[]{:S(2)}) copy-start(bf16[2,128,128]{2,1,0:T(8,128)(2,1)} %refs_6_.3) | copy-start | bytes 196612
  18.7 1.6 %copy-start.10 = (bf16[2,128,128]{2,1,0:T(8,128)(2,1)S(1)}, bf16[2,128,128]{2,1,0:T(8,128)(2,1)}, u32[]{:S(2)}) copy-start(bf16[2,128,128]{2,1,0:T(8,128)(2,1)} %refs_7_.3) | copy-start | bytes 196612
  18.7 1.6 %copy-start.11 = (bf16[128,512]{1,0:T(8,128)(2,1)S(1)}, bf16[128,512]{1,0:T(8,128)(2,1)}, u32[]{:S(2)}) copy-start(bf16[128,512]{1,0:T(8,128)(2,1)} %constant.8.clone.refs_1_) | copy-start | bytes 393220
  24.5 1.6 %copy-start.12 = (bf16[256,256]{1,0:T(8,128)(2,1)S(1)}, bf16[256,256]{1,0:T(8,128)(2,1)}, u32[]{:S(2)}) copy-start(bf16[256,256]{1,0:T(8,128)(2,1)} %constant.9.clone.refs_12_) | copy-start | bytes 393220
  26.1 13.1 %copy-start = (bf16[384,512]{1,0:T(8,128)(2,1)S(1)}, bf16[384,512]{1,0:T(8,128)(2,1)}, u32[]{:S(2)}) copy-start(bf16[384,512]{1,0:T(8,128)(2,1)} %constant.10.clone.along_z) | copy-start | bytes 1179652
  31.6 5.6 %collective-permute-start.6 = (bf16[2,176,128]{2,1,0:T(8,128)(2,1)S(1)}, bf16[2,176,128]{2,1,0:T(8,128)(2,1)S(1)}, u32[]{:S(2)}, u32[]{:S(2)}) collective-permute-start(bf16[2,176,128]{2,1,0:T(8,128)(2,1)S(1)} %get-tuple-element.51), channel_id=1, source_target_pairs={{0,8},{8,16},{16,24},{24,0},{1,9},{9,17},{17,25},{25,1},{2,10},{10... | collective-permute-start | bytes 270344 | tf_op jit(solution)/shard_map/ppermute | solution.py:543
  31.7 5.6 %collective-permute-start.7 = (bf16[2,176,128]{2,1,0:T(8,128)(2,1)S(1)}, bf16[2,176,128]{2,1,0:T(8,128)(2,1)S(1)}, u32[]{:S(2)}, u32[]{:S(2)}) collective-permute-start(bf16[2,176,128]{2,1,0:T(8,128)(2,1)S(1)} %get-tuple-element.52), channel_id=1, source_target_pairs={{0,16},{8,24},{16,0},{24,8},{1,17},{9,25},{17,1},{25,9},{2,18},{10... | collective-permute-start | bytes 270344 | tf_op jit(solution)/shard_map/ppermute | solution.py:543
  31.7 5.9 %collective-permute-start.8 = (bf16[2,176,128]{2,1,0:T(8,128)(2,1)S(1)}, bf16[2,176,128]{2,1,0:T(8,128)(2,1)S(1)}, u32[]{:S(2)}, u32[]{:S(2)}) collective-permute-start(bf16[2,176,128]{2,1,0:T(8,128)(2,1)S(1)} %get-tuple-element.53), channel_id=1, source_target_pairs={{0,24},{8,0},{16,8},{24,16},{1,25},{9,1},{17,9},{25,17},{2,26},{10... | collective-permute-start | bytes 270344 | tf_op jit(solution)/shard_map/ppermute | solution.py:543
  37.6 1.5 %copy-start.1 = (bf16[128,128]{1,0:T(8,128)(2,1)S(1)}, bf16[128,128]{1,0:T(8,128)(2,1)}, u32[]{:S(2)}) copy-start(bf16[128,128]{1,0:T(8,128)(2,1)} %constant.11.clone.across) | copy-start | bytes 98308
  37.7 1.5 %collective-permute-start.9 = (bf16[4,176,128]{2,1,0:T(8,128)(2,1)S(1)}, bf16[4,176,128]{2,1,0:T(8,128)(2,1)S(1)}, u32[]{:S(2)}, u32[]{:S(2)}) collective-permute-start(bf16[4,176,128]{2,1,0:T(8,128)(2,1)S(1)} %get-tuple-element.55), channel_id=1, source_target_pairs={{0,4},{4,0},{1,5},{5,1},{2,6},{6,2},{3,7},{7,3},{8,12},{12,8},{9,1... | collective-permute-start | bytes 540680 | tf_op jit(solution)/shard_map/ppermute | solution.py:552

commit v3 on v2

--- a/solution.py
+++ b/solution.py
@@ -12,7 +12,9 @@
 EPSILON = 1e-06
 TIME_STEP = 0.3
 HALO = 5
+EXTRA = 1000
 MASKED = -1e30
+MIDDLE, REACH, OCTAVES = 0.275, 0.225, 118.0
 F32 = jnp.float32
 BF16 = jnp.bfloat16
 VMEM = pl.BlockSpec(memory_space=pltpu.VMEM)
@@ -38,6 +40,17 @@
 def halves(v):
     high = v.astype(BF16)
     return high, (v - high.astype(F32)).astype(BF16)
+
+
+def coded(nu):
+    place = (nu - MIDDLE) * (OCTAVES / REACH)
+    size = jnp.exp2(2.0 * jnp.abs(place) - OCTAVES)
+    return jnp.where(place < 0.0, -size, size).astype(BF16)
+
+
+def decoded(code):
+    size = (jnp.log2(jnp.abs(code)) + OCTAVES) * (0.5 * REACH / OCTAVES)
+    return MIDDLE + jnp.where(code < 0.0, -size, size)
 
 
 def pack_kernel(nx, ny, flow, visc, *rest):
@@ -63,7 +76,7 @@
             high, low = halves(turned[0, pl.ds(start, rows), :])
             outs[d][e, 0] = high
             outs[d][e, 1] = low
-            outs[d][e, 2] = turned[1, pl.ds(start, rows), :].astype(BF16)
+            outs[d][e, 2] = coded(turned[1, pl.ds(start, rows), :])
 
 
 def small_kernel(ny, fields, lift, bias, gains, head, small, lift_w, head_w):
@@ -114,8 +127,8 @@
         near = mine[d].astype(F32)
         far = got[d].astype(F32)
         for kind in range(2):
-            m = (near[2] if kind else near[0] + near[1]).reshape(shape)
-            t = (far[2] if kind else far[0] + far[1]).reshape(shape)
+            m = (decoded(near[2]) if kind else near[0] + near[1]).reshape(shape)
+            t = (decoded(far[2]) if kind else far[0] + far[1]).reshape(shape)
             p = jnp.where(first, m, t)
             q = jnp.where(first, t, m)
             even = jnp.where(low, p, pltpu.roll(q, fields, 1))
@@ -230,8 +243,11 @@
             outs[d][0] = jnp.where(first, zero, other).reshape(zc * fields, lanes)
             outs[d][1] = jnp.where(first, other, zero).reshape(zc * fields, lanes)
 
+    chunk = lax.axis_index("gx") * ny + lax.axis_index("gy")
     for i, plane in enumerate(planes):
         z = first_state + 2 * plane
+        if plane == EXTRA:
+            z = first_state + jnp.where(chunk < nx * ny // 2, -2, zc)
         s0, s1 = three[z], three[z + 1]
         rows = []
         for value in (s0 + s1, s0 * s0 + s1 * s1):
@@ -528,12 +544,16 @@
 
 
 def along_z_matrix(chunks, depth, place, fields, zc):
-    table = np.zeros((chunks, depth, fields, chunks, zc), np.float32)
-    for c in range(chunks):
-        for z in range(zc):
-            for i, u in taps(z):
-                for f in range(fields):
-                    table[c, place[i] + f, f, c, z] += u
+    half = zc // 2
+    table = np.zeros((chunks, depth, fields, chunks * zc), np.float32)
+    for z in range(chunks * zc):
+        for i, u in taps(z):
+            if 0 <= i < chunks * half:
+                c, row = i // half, place[i % half]
+            else:
+                c, row = (0 if i < 0 else chunks - 1), place[EXTRA]
+            for f in range(fields):
+                table[c, row + f, f, z] += u
     return table.reshape(chunks * depth, fields * chunks * zc)
 
 
@@ -634,7 +654,7 @@
     below = [ring_step(ends[2 * s + 1], s + 1) for s in range(len(ring))]
 
     inner = list(range(2, half - 2))
-    outer = [p for p in range(-1, half + 1) if p not in inner]
+    outer = [p for p in range(half) if p not in inner] + [EXTRA]
 
     def stencil(inputs, first_state, planes, kept, last):
         zz = sum(v.shape[0] for v in inputs)
@@ -663,11 +683,9 @@
             room=16 * (nx // 4) ** 2,
         )
 
-    def pairing(planes):
-        return 2 if len(planes) % 2 == 0 else 1
+    step = 2 if per_plane <= 256 else 1
 
     def attention(filtered, planes, more, outs, last):
-        step = pairing(planes)
         args = [
             filtered,
             sel,
@@ -681,7 +699,7 @@
             down_weight,
             head_w,
         ] + more
-        size = (len(planes) // step, 8, per_plane)
+        size = (-(-len(planes) // step), 8, per_plane)
         work = len(planes) * per_plane * channels * (8 * channels + 4 * hidden) * 2
         return call(
             functools.partial(
@@ -698,10 +716,9 @@
     place = {}
     depth = 0
     for planes in (inner, outer):
-        step = pairing(planes)
         for i, p in enumerate(planes):
             place[p] = depth + (i // step) * 8 + (i % step) * fields
-        depth += len(planes) // step * 8
+        depth += -(-len(planes) // step) * 8
     depth = -(-depth // 16) * 16
 
     more, kept = [], []

time: 40.9 us -> 40.1 us (0.980)
  Pallas kernels: 16 us -> 15.2 us
    pallas_call x10, Pallas kernels: 16 us -> 15.2 us  [call(): pl.pallas_call(body, out_shape=tuple((jax.ShapeDtypeStruct(s, d) for s, d...]
where the time goes in v3:
time: 40.1 us; the launch traced here: 39.6 us
  Pallas kernels  15.2 us (38%)
  starting transfers between devices  14.5 us (36%)
  waiting for transfers between devices  8.27 us (21%)
  local copies, waits for them, and re-layouts  0.85 us (2%)
  between operations  0.85 us (2%)
    pallas_call x10, Pallas kernels, call(): pl.pallas_call(body, out_shape=tuple((jax.ShapeDtypeStruct(s, d) for s, d...  15.2 us
    ppermute x6, starting transfers between devices, exchange(): lax.ppermute(messages[d], 'gx', [(i, (i + d) % nx) for i in range(nx)])  8.93 us
    ppermute x6, waiting for transfers between devices, exchange(): lax.ppermute(messages[d], 'gx', [(i, (i + d) % nx) for i in range(nx)])  5.43 us
    ppermute x2, starting transfers between devices, ring_step(): return lax.ppermute(value, ('gx', 'gy', 'gz'), pairs)  5.39 us
    ppermute x2, waiting for transfers between devices, exchange(): lax.ppermute(away, 'gy', [(i, (i + 1) % ny) for i in range(ny)])  2.83 us
    unnamed x29, local copies, waits for them, and re-layouts  0.85 us
  transfers between devices with their start and end apart: 10, of which 7 were waited for; matrix products, arithmetic and copies ran while one was open for 0% of the time, Pallas kernels for 14%

profile of v3, /device:TPU:0, one launch (start us, length us, event | category | flops | bytes accessed | tf_op | source)
XLA Modules:
  0.0 39.6 jit_solution(17078765827797931151)
XLA Ops:
  0.6 1.8 %shard_map.167 = (bf16[2,3,64,128]{3,2,1,0:T(8,128)(2,1)S(1)}, bf16[2,3,64,128]{3,2,1,0:T(8,128)(2,1)S(1)}, bf16[2,3,64,128]{3,2,1,0:T(8,128)(2,1)S(1)}, bf16[2,3,64,128]{3,2,1,0:T(8,128)(2,1)S(1)}) custom-call(f32[4,4,32,128]{3,2,1,0:T(8,128)} %flow.1, f32[4,4,32,128]{3,2,1,0:T(8,128)} %visc.1), custom_call_target="tpu_custom_call" | custom-call | flops 1000000 | bytes 524288 | tf_op jit(solution)/shard_map/pallas_call | solution.py:25
  2.5 3.0 %collective-permute-start = (bf16[2,3,64,128]{3,2,1,0:T(8,128)(2,1)S(1)}, bf16[2,3,64,128]{3,2,1,0:T(8,128)(2,1)S(1)}, u32[]{:S(2)}, u32[]{:S(2)}) collective-permute-start(bf16[2,3,64,128]{3,2,1,0:T(8,128)(2,1)S(1)} %get-tuple-element.30), channel_id=1, source_target_pairs={{0,8},{8,16},{16,24},{24,0},{1,9},{9,17},{17,25},{25,1},{2,10},{10... | collective-permute-start | bytes 294920 | tf_op jit(solution)/shard_map/ppermute | solution.py:563
  5.5 0.0 copy-start.13
  5.5 1.5 %collective-permute-start.1 = (bf16[2,3,64,128]{3,2,1,0:T(8,128)(2,1)S(1)}, bf16[2,3,64,128]{3,2,1,0:T(8,128)(2,1)S(1)}, u32[]{:S(2)}, u32[]{:S(2)}) collective-permute-start(bf16[2,3,64,128]{3,2,1,0:T(8,128)(2,1)S(1)} %get-tuple-element.31), channel_id=1, source_target_pairs={{0,16},{8,24},{16,0},{24,8},{1,17},{9,25},{17,1},{25,9},{2,18},{10... | collective-permute-start | bytes 294920 | tf_op jit(solution)/shard_map/ppermute | solution.py:563
  7.0 1.4 %collective-permute-start.2 = (bf16[2,3,64,128]{3,2,1,0:T(8,128)(2,1)S(1)}, bf16[2,3,64,128]{3,2,1,0:T(8,128)(2,1)S(1)}, u32[]{:S(2)}, u32[]{:S(2)}) collective-permute-start(bf16[2,3,64,128]{3,2,1,0:T(8,128)(2,1)S(1)} %get-tuple-element.32), channel_id=1, source_target_pairs={{0,24},{8,0},{16,8},{24,16},{1,25},{9,1},{17,9},{25,17},{2,26},{10... | collective-permute-start | bytes 294920 | tf_op jit(solution)/shard_map/ppermute | solution.py:563
  8.4 0.0 copy-done.13
  8.4 0.0 copy-start.2
  8.5 0.0 copy-start.3
  8.5 0.1 copy.18.head
  8.6 0.0 copy-start.4
  8.6 0.5 %copy-done.2 = f32[8,128]{1,0:T(8,128)S(1)} copy-done((f32[8,128]{1,0:T(8,128)S(1)}, f32[8,128]{1,0:T(8,128)}, u32[]{:S(2)}) %copy-start.2) | copy-done | bytes 4120
  9.1 0.0 copy-done.3
  9.2 0.1 copy-done.4
  9.2 0.1 shard_map.168
  9.3 0.4 collective-permute-done.refs_1_
  9.7 1.7 %collective-permute-done.1.refs_2_ = bf16[2,3,64,128]{3,2,1,0:T(8,128)(2,1)S(1)} collective-permute-done((bf16[2,3,64,128]{3,2,1,0:T(8,128)(2,1)S(1)}, bf16[2,3,64,128]{3,2,1,0:T(8,128)(2,1)S(1)}, u32[]{:S(2)}, u32[]{:S(2)}) %collective-permute-start.1) | collective-permute-done | bytes 98336 | tf_op jit(solution)/shard_map/ppermute | solution.py:563
  11.4 0.3 collective-permute-done.2.refs_3_
  11.7 0.1 collective-permute-start.3
  11.8 1.4 %collective-permute-done.3.got = bf16[4,3,64,128]{3,2,1,0:T(8,128)(2,1)S(1)} collective-permute-done((bf16[4,3,64,128]{3,2,1,0:T(8,128)(2,1)S(1)}, bf16[4,3,64,128]{3,2,1,0:T(8,128)(2,1)S(1)}, u32[]{:S(2)}, u32[]{:S(2)}) %collective-permute-start.3) | collective-permute-done | bytes 196640 | tf_op jit(solution)/shard_map/ppermute | solution.py:572
  13.2 0.2 shard_map.170
  13.4 0.2 collective-permute-start.4
  13.6 5.2 %collective-permute-start.5 = (f32[5,2,4,8,128]{4,3,2,1,0:T(8,128)S(1)}, f32[5,2,4,8,128]{4,3,2,1,0:T(8,128)S(1)}, u32[]{:S(2)}, u32[]{:S(2)}) collective-permute-start(f32[5,2,4,8,128]{4,3,2,1,0:T(8,128)S(1)} %get-tuple-element.38), channel_id=1, source_target_pairs={{0,31},{4,0},{8,4},{12,8},{16,12},{20,16},{24,20},{28,24},{1,28},{... | collective-permute-start | bytes 491528 | tf_op jit(solution)/shard_map/ppermute | solution.py:651
  18.8 0.0 copy-start.5
  18.8 0.0 copy-start.6
  18.8 0.0 copy-start.7
  18.8 0.0 copy-start.8
  18.8 0.0 copy-start.9
  18.8 0.0 copy-start.10
  18.8 0.0 copy-start.11
  18.9 1.5 %shard_map.171 = (bf16[4,48,512]{2,1,0:T(8,128)(2,1)S(1)}, f32[16,4,8,128]{3,2,1,0:T(8,128)S(1)}, f32[16,4,8,128]{3,2,1,0:T(8,128)S(1)}, f32[16,4,8,128]{3,2,1,0:T(8,128)S(1)}) custom-call(f32[16,2,4,8,128]{4,3,2,1,0:T(8,128)S(1)} %get-tuple-element.37.refs_0_.refs_1_), custom_call_target="tpu_custom_call" | custom-call | flops 300000000 | bytes 524288 | tf_op jit(solution)/shard_map/pallas_call | solution.py:25
  20.4 0.0 copy-done.5
  20.4 0.0 copy-done.6
  20.4 0.0 copy-done.7
  20.4 0.0 copy-done.8
  20.5 0.0 copy-done.9
  20.5 0.0 copy-done.10
  20.5 0.0 copy-done.11
  20.5 4.1 %shard_map.173.refs_11_ = f32[2,8,256]{2,1,0:T(8,128)S(1)} custom-call(bf16[4,48,512]{2,1,0:T(8,128)(2,1)S(1)} %get-tuple-element.45.refs_0_, bf16[128,512]{1,0:T(8,128)(2,1)S(1)} %copy-done.11, bf16[144,256]{1,0:T(8,128)(2,1)S(1)} %get-tuple-element.43.refs_2_, f32[8,128]{1,0:T(8,128)S(1)} %get-tuple-element.33.refs_4_.refs_3_, ...), custom_call_target="tpu_custom_call" | custom-call | flops 2415919104 | bytes 1000000 | tf_op jit(solution)/shard_map/pallas_call | solution.py:25
  24.6 0.0 collective-permute-done.4.refs_0_
  24.6 0.0 collective-permute-done.5.refs_2_
  24.6 0.0 copy-start.12
  24.6 1.4 %shard_map.172 = (bf16[5,48,512]{2,1,0:T(8,128)(2,1)S(1)}, f32[2,64,128]{2,1,0:T(8,128)S(1)}, f32[2,64,128]{2,1,0:T(8,128)S(1)}, f32[2,64,128]{2,1,0:T(8,128)S(1)}, f32[2,64,128]{2,1,0:T(8,128)S(1)}) custom-call(f32[5,2,4,8,128]{4,3,2,1,0:T(8,128)S(1)} %collective-permute-done.4.refs_0_, f32[16,2,4,8,128]{4,3,2,1,0:T(8,128)S(1)} %get-tuple-element.37.refs_0_.refs_1_, ...), custom_call_target="tpu_custom_call" | custom-call | flops 300000000 | bytes 851968 | tf_op jit(solution)/shard_map/pallas_call | solution.py:25
  26.1 0.0 copy-done.12
  26.1 0.0 copy-start
  26.1 4.7 %shard_map.174 = (bf16[2,176,128]{2,1,0:T(8,128)(2,1)S(1)}, bf16[2,176,128]{2,1,0:T(8,128)(2,1)S(1)}, bf16[2,176,128]{2,1,0:T(8,128)(2,1)S(1)}, bf16[2,176,128]{2,1,0:T(8,128)(2,1)S(1)}) custom-call(bf16[5,48,512]{2,1,0:T(8,128)(2,1)S(1)} %get-tuple-element.42.refs_0_, bf16[128,512]{1,0:T(8,128)(2,1)S(1)} %copy-done.11, ...), custom_call_target="tpu_custom_call" | custom-call | flops 3019898880 | bytes 1000000 | tf_op jit(solution)/shard_map/pallas_call | solution.py:25
  30.8 0.1 collective-permute-start.6
  30.9 0.1 collective-permute-start.7
  30.9 2.8 %collective-permute-start.8 = (bf16[2,176,128]{2,1,0:T(8,128)(2,1)S(1)}, bf16[2,176,128]{2,1,0:T(8,128)(2,1)S(1)}, u32[]{:S(2)}, u32[]{:S(2)}) collective-permute-start(bf16[2,176,128]{2,1,0:T(8,128)(2,1)S(1)} %get-tuple-element.53), channel_id=1, source_target_pairs={{0,24},{8,0},{16,8},{24,16},{1,25},{9,1},{17,9},{25,17},{2,26},{10... | collective-permute-start | bytes 270344 | tf_op jit(solution)/shard_map/ppermute | solution.py:563
  33.8 2.6 %collective-permute-done.6.refs_1_ = bf16[2,176,128]{2,1,0:T(8,128)(2,1)S(1)} collective-permute-done((bf16[2,176,128]{2,1,0:T(8,128)(2,1)S(1)}, bf16[2,176,128]{2,1,0:T(8,128)(2,1)S(1)}, u32[]{:S(2)}, u32[]{:S(2)}) %collective-permute-start.6) | collective-permute-done | bytes 90144 | tf_op jit(solution)/shard_map/ppermute | solution.py:563
  36.4 0.0 collective-permute-done.7.refs_2_
  36.4 0.4 %collective-permute-done.8.refs_3_ = bf16[2,176,128]{2,1,0:T(8,128)(2,1)S(1)} collective-permute-done((bf16[2,176,128]{2,1,0:T(8,128)(2,1)S(1)}, bf16[2,176,128]{2,1,0:T(8,128)(2,1)S(1)}, u32[]{:S(2)}, u32[]{:S(2)}) %collective-permute-start.8) | collective-permute-done | bytes 90144 | tf_op jit(solution)/shard_map/ppermute | solution.py:563
  36.8 0.0 copy-start.1
  36.9 0.1 collective-permute-start.9
  37.0 1.4 %collective-permute-done.9.got = bf16[4,176,128]{2,1,0:T(8,128)(2,1)S(1)} collective-permute-done((bf16[4,176,128]{2,1,0:T(8,128)(2,1)S(1)}, bf16[4,176,128]{2,1,0:T(8,128)(2,1)S(1)}, u32[]{:S(2)}, u32[]{:S(2)}) %collective-permute-start.9) | collective-permute-done | bytes 180256 | tf_op jit(solution)/shard_map/ppermute | solution.py:572
  38.4 0.0 copy-done
  38.4 0.0 copy-done.1
  38.4 1.3 %shard_map.176 = (f32[4,4,32,128]{3,2,1,0:T(8,128)}, f32[4,4,32,128]{3,2,1,0:T(8,128)}) custom-call(bf16[4,176,128]{2,1,0:T(8,128)(2,1)S(1)} %get-tuple-element.54.mine, bf16[4,176,128]{2,1,0:T(8,128)(2,1)S(1)} %collective-permute-done.9.got, bf16[384,512]{1,0:T(8,128)(2,1)S(1)} %copy-done, bf16[128,128]{1,0:T(8,128)(2,1)S(1)} %copy-done.1), custom_call_target="tpu_custom_call" | custom-call | flops 1000000 | bytes 524288 | tf_op jit(solution)/shard_map/pallas_call | solution.py:25
  (2 shorter events, 0.1 us)
Async XLA Ops:
  2.5 7.2 %collective-permute-start = (bf16[2,3,64,128]{3,2,1,0:T(8,128)(2,1)S(1)}, bf16[2,3,64,128]{3,2,1,0:T(8,128)(2,1)S(1)}, u32[]{:S(2)}, u32[]{:S(2)}) collective-permute-start(bf16[2,3,64,128]{3,2,1,0:T(8,128)(2,1)S(1)} %get-tuple-element.30), channel_id=1, source_target_pairs={{0,8},{8,16},{16,24},{24,0},{1,9},{9,17},{17,25},{25,1},{2,10},{10... | collective-permute-start | bytes 294920 | tf_op jit(solution)/shard_map/ppermute | solution.py:563
  5.5 3.0 %copy-start.13 = (bf16[128,4]{0,1:T(4,128)(2,1)S(1)}, bf16[128,4]{0,1:T(4,128)(2,1)}, u32[]{:S(2)}) copy-start(bf16[128,4]{0,1:T(4,128)(2,1)} %param.27) | copy-start | bytes 3076
  5.5 5.9 %collective-permute-start.1 = (bf16[2,3,64,128]{3,2,1,0:T(8,128)(2,1)S(1)}, bf16[2,3,64,128]{3,2,1,0:T(8,128)(2,1)S(1)}, u32[]{:S(2)}, u32[]{:S(2)}) collective-permute-start(bf16[2,3,64,128]{3,2,1,0:T(8,128)(2,1)S(1)} %get-tuple-element.31), channel_id=1, source_target_pairs={{0,16},{8,24},{16,0},{24,8},{1,17},{9,25},{17,1},{25,9},{2,18},{10... | collective-permute-start | bytes 294920 | tf_op jit(solution)/shard_map/ppermute | solution.py:563
  7.0 4.7 %collective-permute-start.2 = (bf16[2,3,64,128]{3,2,1,0:T(8,128)(2,1)S(1)}, bf16[2,3,64,128]{3,2,1,0:T(8,128)(2,1)S(1)}, u32[]{:S(2)}, u32[]{:S(2)}) collective-permute-start(bf16[2,3,64,128]{3,2,1,0:T(8,128)(2,1)S(1)} %get-tuple-element.32), channel_id=1, source_target_pairs={{0,24},{8,0},{16,8},{24,16},{1,25},{9,1},{17,9},{25,17},{2,26},{10... | collective-permute-start | bytes 294920 | tf_op jit(solution)/shard_map/ppermute | solution.py:563
  8.4 0.7 %copy-start.2 = (f32[8,128]{1,0:T(8,128)S(1)}, f32[8,128]{1,0:T(8,128)}, u32[]{:S(2)}) copy-start(f32[8,128]{1,0:T(8,128)} %lift.1) | copy-start | bytes 12292
  8.5 0.7 %copy-start.3 = (f32[6,128]{1,0:T(8,128)S(1)}, f32[6,128]{1,0:T(8,128)}, u32[]{:S(2)}) copy-start(f32[6,128]{1,0:T(8,128)} %gains.1) | copy-start | bytes 9220
  8.6 0.7 %copy-start.4 = (f32[128]{0:T(128)S(1)}, f32[128]{0:T(128)}, u32[]{:S(2)}) copy-start(f32[128]{0:T(128)} %param.19) | copy-start | bytes 1540
  11.7 1.5 %collective-permute-start.3 = (bf16[4,3,64,128]{3,2,1,0:T(8,128)(2,1)S(1)}, bf16[4,3,64,128]{3,2,1,0:T(8,128)(2,1)S(1)}, u32[]{:S(2)}, u32[]{:S(2)}) collective-permute-start(bf16[4,3,64,128]{3,2,1,0:T(8,128)(2,1)S(1)} %get-tuple-element.35), channel_id=1, source_target_pairs={{0,4},{4,0},{1,5},{5,1},{2,6},{6,2},{3,7},{7,3},{8,12},{12,8},{9,1... | collective-permute-start | bytes 589832 | tf_op jit(solution)/shard_map/ppermute | solution.py:572
  13.4 11.2 %collective-permute-start.4 = (f32[5,2,4,8,128]{4,3,2,1,0:T(8,128)S(1)}, f32[5,2,4,8,128]{4,3,2,1,0:T(8,128)S(1)}, u32[]{:S(2)}, u32[]{:S(2)}) collective-permute-start(f32[5,2,4,8,128]{4,3,2,1,0:T(8,128)S(1)} %get-tuple-element.36), channel_id=1, source_target_pairs={{0,4},{4,8},{8,12},{12,16},{16,20},{20,24},{24,28},{28,1},{1,5},{5... | collective-permute-start | bytes 491528 | tf_op jit(solution)/shard_map/ppermute | solution.py:651
  13.6 11.0 %collective-permute-start.5 = (f32[5,2,4,8,128]{4,3,2,1,0:T(8,128)S(1)}, f32[5,2,4,8,128]{4,3,2,1,0:T(8,128)S(1)}, u32[]{:S(2)}, u32[]{:S(2)}) collective-permute-start(f32[5,2,4,8,128]{4,3,2,1,0:T(8,128)S(1)} %get-tuple-element.38), channel_id=1, source_target_pairs={{0,31},{4,0},{8,4},{12,8},{16,12},{20,16},{24,20},{28,24},{1,28},{... | collective-permute-start | bytes 491528 | tf_op jit(solution)/shard_map/ppermute | solution.py:651
  18.8 1.6 %copy-start.5 = (bf16[2,128,512]{2,1,0:T(8,128)(2,1)S(1)}, bf16[2,128,512]{2,1,0:T(8,128)(2,1)}, u32[]{:S(2)}) copy-start(bf16[2,128,512]{2,1,0:T(8,128)(2,1)} %refs_8_.3) | copy-start | bytes 786436
  18.8 1.6 %copy-start.6 = (bf16[2,512,128]{2,1,0:T(8,128)(2,1)S(1)}, bf16[2,512,128]{2,1,0:T(8,128)(2,1)}, u32[]{:S(2)}) copy-start(bf16[2,512,128]{2,1,0:T(8,128)(2,1)} %refs_9_.3) | copy-start | bytes 786436
  18.8 1.6 %copy-start.7 = (bf16[2,128,128]{2,1,0:T(8,128)(2,1)S(1)}, bf16[2,128,128]{2,1,0:T(8,128)(2,1)}, u32[]{:S(2)}) copy-start(bf16[2,128,128]{2,1,0:T(8,128)(2,1)} %refs_4_.3) | copy-start | bytes 196612
  18.8 1.6 %copy-start.8 = (bf16[2,128,128]{2,1,0:T(8,128)(2,1)S(1)}, bf16[2,128,128]{2,1,0:T(8,128)(2,1)}, u32[]{:S(2)}) copy-start(bf16[2,128,128]{2,1,0:T(8,128)(2,1)} %refs_5_.3) | copy-start | bytes 196612
  18.8 1.6 %copy-start.9 = (bf16[2,128,128]{2,1,0:T(8,128)(2,1)S(1)}, bf16[2,128,128]{2,1,0:T(8,128)(2,1)}, u32[]{:S(2)}) copy-start(bf16[2,128,128]{2,1,0:T(8,128)(2,1)} %refs_6_.3) | copy-start | bytes 196612
  18.8 1.6 %copy-start.10 = (bf16[2,128,128]{2,1,0:T(8,128)(2,1)S(1)}, bf16[2,128,128]{2,1,0:T(8,128)(2,1)}, u32[]{:S(2)}) copy-start(bf16[2,128,128]{2,1,0:T(8,128)(2,1)} %refs_7_.3) | copy-start | bytes 196612
  18.8 1.6 %copy-start.11 = (bf16[128,512]{1,0:T(8,128)(2,1)S(1)}, bf16[128,512]{1,0:T(8,128)(2,1)}, u32[]{:S(2)}) copy-start(bf16[128,512]{1,0:T(8,128)(2,1)} %constant.8.clone.refs_1_) | copy-start | bytes 393220
  24.6 1.5 %copy-start.12 = (bf16[256,256]{1,0:T(8,128)(2,1)S(1)}, bf16[256,256]{1,0:T(8,128)(2,1)}, u32[]{:S(2)}) copy-start(bf16[256,256]{1,0:T(8,128)(2,1)} %constant.9.clone.refs_12_) | copy-start | bytes 393220
  26.1 12.3 %copy-start = (bf16[384,512]{1,0:T(8,128)(2,1)S(1)}, bf16[384,512]{1,0:T(8,128)(2,1)}, u32[]{:S(2)}) copy-start(bf16[384,512]{1,0:T(8,128)(2,1)} %constant.10.clone.along_z) | copy-start | bytes 1179652
  30.8 5.6 %collective-permute-start.6 = (bf16[2,176,128]{2,1,0:T(8,128)(2,1)S(1)}, bf16[2,176,128]{2,1,0:T(8,128)(2,1)S(1)}, u32[]{:S(2)}, u32[]{:S(2)}) collective-permute-start(bf16[2,176,128]{2,1,0:T(8,128)(2,1)S(1)} %get-tuple-element.51), channel_id=1, source_target_pairs={{0,8},{8,16},{16,24},{24,0},{1,9},{9,17},{17,25},{25,1},{2,10},{10... | collective-permute-start | bytes 270344 | tf_op jit(solution)/shard_map/ppermute | solution.py:563
  30.9 5.6 %collective-permute-start.7 = (bf16[2,176,128]{2,1,0:T(8,128)(2,1)S(1)}, bf16[2,176,128]{2,1,0:T(8,128)(2,1)S(1)}, u32[]{:S(2)}, u32[]{:S(2)}) collective-permute-start(bf16[2,176,128]{2,1,0:T(8,128)(2,1)S(1)} %get-tuple-element.52), channel_id=1, source_target_pairs={{0,16},{8,24},{16,0},{24,8},{1,17},{9,25},{17,1},{25,9},{2,18},{10... | collective-permute-start | bytes 270344 | tf_op jit(solution)/shard_map/ppermute | solution.py:563
  30.9 5.9 %collective-permute-start.8 = (bf16[2,176,128]{2,1,0:T(8,128)(2,1)S(1)}, bf16[2,176,128]{2,1,0:T(8,128)(2,1)S(1)}, u32[]{:S(2)}, u32[]{:S(2)}) collective-permute-start(bf16[2,176,128]{2,1,0:T(8,128)(2,1)S(1)} %get-tuple-element.53), channel_id=1, source_target_pairs={{0,24},{8,0},{16,8},{24,16},{1,25},{9,1},{17,9},{25,17},{2,26},{10... | collective-permute-start | bytes 270344 | tf_op jit(solution)/shard_map/ppermute | solution.py:563
  36.8 1.5 %copy-start.1 = (bf16[128,128]{1,0:T(8,128)(2,1)S(1)}, bf16[128,128]{1,0:T(8,128)(2,1)}, u32[]{:S(2)}) copy-start(bf16[128,128]{1,0:T(8,128)(2,1)} %constant.11.clone.across) | copy-start | bytes 98308
  36.9 1.5 %collective-permute-start.9 = (bf16[4,176,128]{2,1,0:T(8,128)(2,1)S(1)}, bf16[4,176,128]{2,1,0:T(8,128)(2,1)S(1)}, u32[]{:S(2)}, u32[]{:S(2)}) collective-permute-start(bf16[4,176,128]{2,1,0:T(8,128)(2,1)S(1)} %get-tuple-element.55), channel_id=1, source_target_pairs={{0,4},{4,0},{1,5},{5,1},{2,6},{6,2},{3,7},{7,3},{8,12},{12,8},{9,1... | collective-permute-start | bytes 540680 | tf_op jit(solution)/shard_map/ppermute | solution.py:572

commit v4 on v3

--- a/solution.py
+++ b/solution.py
@@ -31,6 +31,13 @@
         cost_estimate=pl.CostEstimate(flops=flops, bytes_accessed=moved, transcendentals=0),
         compiler_params=pltpu.CompilerParams(vmem_limit_bytes=int(min(room, 63.93) * 1048576)),
     )(*args)
+
+
+def chunk_of(nx, ny, a, b, slab):
+    if nx & (nx - 1) == 0:
+        a = a ^ (a >> 1)
+    chunk = a * ny + b
+    return chunk + slab % 2 * (nx * ny - 1 - 2 * chunk)
 
 
 def iota(shape, dim):
@@ -69,9 +76,10 @@
         turned[kind, pl.ds(row, zl, stride=fields), :] = blocks[f].reshape(lanes, zl).T
     rows = zl * fields // (nx * ny)
     a, b = lax.axis_index("gx"), lax.axis_index("gy")
+    slab = lax.axis_index("gz")
     for d in range(nx):
         for e in range(ny):
-            chunk = lax.rem(a + d, nx) * ny + lax.rem(b + e, ny)
+            chunk = chunk_of(nx, ny, lax.rem(a + d, nx), lax.rem(b + e, ny), slab)
             start = pl.multiple_of(chunk * rows, 8)
             high, low = halves(turned[0, pl.ds(start, rows), :])
             outs[d][e, 0] = high
@@ -243,7 +251,7 @@
             outs[d][0] = jnp.where(first, zero, other).reshape(zc * fields, lanes)
             outs[d][1] = jnp.where(first, other, zero).reshape(zc * fields, lanes)
 
-    chunk = lax.axis_index("gx") * ny + lax.axis_index("gy")
+    chunk = chunk_of(nx, ny, *(lax.axis_index(name) for name in ("gx", "gy", "gz")))
     for i, plane in enumerate(planes):
         z = first_state + 2 * plane
         if plane == EXTRA:
@@ -467,10 +475,11 @@
     state_out, eddy_out, state_rows, coarse_rows, state, eddy, sems = refs
     fields, xl, yl, zl = state_out.shape
     a, b = lax.axis_index("gx"), lax.axis_index("gy")
+    slab = lax.axis_index("gz")
     size = state_rows.shape[0] // (nx * ny)
     for d in range(nx):
         for piece, core in ((mine, b), (got, lax.rem(b + 1, ny))):
-            chunk = lax.rem(a + nx - d, nx) * ny + core
+            chunk = chunk_of(nx, ny, lax.rem(a + nx - d, nx), core, slab)
             start = pl.multiple_of(chunk * size, 8)
             high, low = piece[d, :size].astype(F32), piece[d, size : 2 * size].astype(F32)
             state_rows[pl.ds(start, size), :] = high + low
@@ -643,11 +652,15 @@
     own, ends = unified[0], unified[1:]
     total = nz * chunks
 
+    devices = {}
+    for a in range(nx):
+        for b in range(ny):
+            for slab in range(nz):
+                position = slab * chunks + chunk_of(nx, ny, a, b, slab)
+                devices[position] = (a * ny + b) * nz + slab
+
     def ring_step(value, move):
-        pairs = []
-        for k in range(total):
-            t = (k + move) % total
-            pairs.append(((k % chunks) * nz + k // chunks, (t % chunks) * nz + t // chunks))
+        pairs = [(devices[k], devices[(k + move) % total]) for k in range(total)]
         return lax.ppermute(value, ("gx", "gy", "gz"), pairs)
 
     above = [ring_step(ends[2 * s], -(s + 1)) for s in range(len(ring))]

time: 40.1 us -> 38.6 us (0.963)
  starting transfers between devices: 14.5 us -> 13 us
    ppermute x2, starting transfers between devices: 5.39 us -> 3.88 us  [ring_step(): return lax.ppermute(value, ('gx', 'gy', 'gz'), pairs)]
  transfers between devices with their start and end apart: 10 -> 10, of which waited for: 7 -> 7; matrix products, arithmetic and copies ran while one was open for 0% -> 0% of each run, Pallas kernels for 14% -> 15%
where the time goes in v4:
time: 38.6 us; the launch traced here: 38.2 us
  Pallas kernels  15.2 us (39%)
  starting transfers between devices  13 us (34%)
  waiting for transfers between devices  8.27 us (21%)
  local copies, waits for them, and re-layouts  0.85 us (2%)
  between operations  0.84 us (2%)
    pallas_call x10, Pallas kernels, call(): pl.pallas_call(body, out_shape=tuple((jax.ShapeDtypeStruct(s, d) for s, d...  15.2 us
    ppermute x6, starting transfers between devices, exchange(): lax.ppermute(messages[d], 'gx', [(i, (i + d) % nx) for i in range(nx)])  8.94 us
    ppermute x6, waiting for transfers between devices, exchange(): lax.ppermute(messages[d], 'gx', [(i, (i + d) % nx) for i in range(nx)])  5.43 us
    ppermute x2, starting transfers between devices, ring_step(): return lax.ppermute(value, ('gx', 'gy', 'gz'), pairs)  3.88 us
    ppermute x2, waiting for transfers between devices, exchange(): lax.ppermute(away, 'gy', [(i, (i + 1) % ny) for i in range(ny)])  2.83 us
    unnamed x29, local copies, waits for them, and re-layouts  0.85 us
  transfers between devices with their start and end apart: 10, of which 7 were waited for; matrix products, arithmetic and copies ran while one was open for 0% of the time, Pallas kernels for 15%

profile of v4, /device:TPU:0, one launch (start us, length us, event | category | flops | bytes accessed | tf_op | source)
XLA Modules:
  0.0 38.2 jit_solution(14074825233778326116)
XLA Ops:
  0.6 1.8 %shard_map.167 = (bf16[2,3,64,128]{3,2,1,0:T(8,128)(2,1)S(1)}, bf16[2,3,64,128]{3,2,1,0:T(8,128)(2,1)S(1)}, bf16[2,3,64,128]{3,2,1,0:T(8,128)(2,1)S(1)}, bf16[2,3,64,128]{3,2,1,0:T(8,128)(2,1)S(1)}) custom-call(f32[4,4,32,128]{3,2,1,0:T(8,128)} %flow.1, f32[4,4,32,128]{3,2,1,0:T(8,128)} %visc.1), custom_call_target="tpu_custom_call" | custom-call | flops 1000000 | bytes 524288 | tf_op jit(solution)/shard_map/pallas_call | solution.py:25
  2.5 3.0 %collective-permute-start = (bf16[2,3,64,128]{3,2,1,0:T(8,128)(2,1)S(1)}, bf16[2,3,64,128]{3,2,1,0:T(8,128)(2,1)S(1)}, u32[]{:S(2)}, u32[]{:S(2)}) collective-permute-start(bf16[2,3,64,128]{3,2,1,0:T(8,128)(2,1)S(1)} %get-tuple-element.30), channel_id=1, source_target_pairs={{0,8},{8,16},{16,24},{24,0},{1,9},{9,17},{17,25},{25,1},{2,10},{10... | collective-permute-start | bytes 294920 | tf_op jit(solution)/shard_map/ppermute | solution.py:572
  5.5 0.0 copy-start.13
  5.5 1.5 %collective-permute-start.1 = (bf16[2,3,64,128]{3,2,1,0:T(8,128)(2,1)S(1)}, bf16[2,3,64,128]{3,2,1,0:T(8,128)(2,1)S(1)}, u32[]{:S(2)}, u32[]{:S(2)}) collective-permute-start(bf16[2,3,64,128]{3,2,1,0:T(8,128)(2,1)S(1)} %get-tuple-element.31), channel_id=1, source_target_pairs={{0,16},{8,24},{16,0},{24,8},{1,17},{9,25},{17,1},{25,9},{2,18},{10... | collective-permute-start | bytes 294920 | tf_op jit(solution)/shard_map/ppermute | solution.py:572
  7.0 1.4 %collective-permute-start.2 = (bf16[2,3,64,128]{3,2,1,0:T(8,128)(2,1)S(1)}, bf16[2,3,64,128]{3,2,1,0:T(8,128)(2,1)S(1)}, u32[]{:S(2)}, u32[]{:S(2)}) collective-permute-start(bf16[2,3,64,128]{3,2,1,0:T(8,128)(2,1)S(1)} %get-tuple-element.32), channel_id=1, source_target_pairs={{0,24},{8,0},{16,8},{24,16},{1,25},{9,1},{17,9},{25,17},{2,26},{10... | collective-permute-start | bytes 294920 | tf_op jit(solution)/shard_map/ppermute | solution.py:572
  8.4 0.0 copy-done.13
  8.4 0.0 copy-start.2
  8.5 0.0 copy-start.3
  8.5 0.1 copy.18.head
  8.6 0.0 copy-start.4
  8.6 0.5 %copy-done.2 = f32[8,128]{1,0:T(8,128)S(1)} copy-done((f32[8,128]{1,0:T(8,128)S(1)}, f32[8,128]{1,0:T(8,128)}, u32[]{:S(2)}) %copy-start.2) | copy-done | bytes 4120
  9.1 0.0 copy-done.3
  9.2 0.1 copy-done.4
  9.2 0.1 shard_map.168
  9.3 0.3 collective-permute-done.refs_1_
  9.7 1.7 %collective-permute-done.1.refs_2_ = bf16[2,3,64,128]{3,2,1,0:T(8,128)(2,1)S(1)} collective-permute-done((bf16[2,3,64,128]{3,2,1,0:T(8,128)(2,1)S(1)}, bf16[2,3,64,128]{3,2,1,0:T(8,128)(2,1)S(1)}, u32[]{:S(2)}, u32[]{:S(2)}) %collective-permute-start.1) | collective-permute-done | bytes 98336 | tf_op jit(solution)/shard_map/ppermute | solution.py:572
  11.3 0.3 collective-permute-done.2.refs_3_
  11.7 0.1 collective-permute-start.3
  11.8 1.4 %collective-permute-done.3.got = bf16[4,3,64,128]{3,2,1,0:T(8,128)(2,1)S(1)} collective-permute-done((bf16[4,3,64,128]{3,2,1,0:T(8,128)(2,1)S(1)}, bf16[4,3,64,128]{3,2,1,0:T(8,128)(2,1)S(1)}, u32[]{:S(2)}, u32[]{:S(2)}) %collective-permute-start.3) | collective-permute-done | bytes 196640 | tf_op jit(solution)/shard_map/ppermute | solution.py:581
  13.2 0.2 shard_map.170
  13.4 0.2 collective-permute-start.4
  13.6 3.7 %collective-permute-start.5 = (f32[5,2,4,8,128]{4,3,2,1,0:T(8,128)S(1)}, f32[5,2,4,8,128]{4,3,2,1,0:T(8,128)S(1)}, u32[]{:S(2)}, u32[]{:S(2)}) collective-permute-start(f32[5,2,4,8,128]{4,3,2,1,0:T(8,128)S(1)} %get-tuple-element.38), channel_id=1, source_target_pairs={{0,3},{4,0},{8,4},{12,8},{24,12},{28,24},{16,28},{20,16},{21,20},{... | collective-permute-start | bytes 491528 | tf_op jit(solution)/shard_map/ppermute | solution.py:664
  17.3 0.0 copy-start.5
  17.3 0.0 copy-start.6
  17.3 0.0 copy-start.7
  17.3 0.0 copy-start.8
  17.3 0.0 copy-start.9
  17.3 0.0 copy-start.10
  17.3 0.0 copy-start.11
  17.4 1.5 %shard_map.171 = (bf16[4,48,512]{2,1,0:T(8,128)(2,1)S(1)}, f32[16,4,8,128]{3,2,1,0:T(8,128)S(1)}, f32[16,4,8,128]{3,2,1,0:T(8,128)S(1)}, f32[16,4,8,128]{3,2,1,0:T(8,128)S(1)}) custom-call(f32[16,2,4,8,128]{4,3,2,1,0:T(8,128)S(1)} %get-tuple-element.37.refs_0_.refs_1_), custom_call_target="tpu_custom_call" | custom-call | flops 300000000 | bytes 524288 | tf_op jit(solution)/shard_map/pallas_call | solution.py:25
  18.9 0.0 copy-done.5
  18.9 0.0 copy-done.6
  18.9 0.0 copy-done.7
  18.9 0.0 copy-done.8
  18.9 0.0 copy-done.9
  19.0 0.0 copy-done.10
  19.0 0.0 copy-done.11
  19.0 4.1 %shard_map.173.refs_11_ = f32[2,8,256]{2,1,0:T(8,128)S(1)} custom-call(bf16[4,48,512]{2,1,0:T(8,128)(2,1)S(1)} %get-tuple-element.45.refs_0_, bf16[128,512]{1,0:T(8,128)(2,1)S(1)} %copy-done.11, bf16[144,256]{1,0:T(8,128)(2,1)S(1)} %get-tuple-element.43.refs_2_, f32[8,128]{1,0:T(8,128)S(1)} %get-tuple-element.33.refs_4_.refs_3_, ...), custom_call_target="tpu_custom_call" | custom-call | flops 2415919104 | bytes 1000000 | tf_op jit(solution)/shard_map/pallas_call | solution.py:25
  23.1 0.0 collective-permute-done.4.refs_0_
  23.1 0.0 collective-permute-done.5.refs_2_
  23.1 0.0 copy-start.12
  23.1 1.4 %shard_map.172 = (bf16[5,48,512]{2,1,0:T(8,128)(2,1)S(1)}, f32[2,64,128]{2,1,0:T(8,128)S(1)}, f32[2,64,128]{2,1,0:T(8,128)S(1)}, f32[2,64,128]{2,1,0:T(8,128)S(1)}, f32[2,64,128]{2,1,0:T(8,128)S(1)}) custom-call(f32[5,2,4,8,128]{4,3,2,1,0:T(8,128)S(1)} %collective-permute-done.4.refs_0_, f32[16,2,4,8,128]{4,3,2,1,0:T(8,128)S(1)} %get-tuple-element.37.refs_0_.refs_1_, ...), custom_call_target="tpu_custom_call" | custom-call | flops 300000000 | bytes 851968 | tf_op jit(solution)/shard_map/pallas_call | solution.py:25
  24.6 0.0 copy-done.12
  24.6 0.0 copy-start
  24.6 4.7 %shard_map.174 = (bf16[2,176,128]{2,1,0:T(8,128)(2,1)S(1)}, bf16[2,176,128]{2,1,0:T(8,128)(2,1)S(1)}, bf16[2,176,128]{2,1,0:T(8,128)(2,1)S(1)}, bf16[2,176,128]{2,1,0:T(8,128)(2,1)S(1)}) custom-call(bf16[5,48,512]{2,1,0:T(8,128)(2,1)S(1)} %get-tuple-element.42.refs_0_, bf16[128,512]{1,0:T(8,128)(2,1)S(1)} %copy-done.11, ...), custom_call_target="tpu_custom_call" | custom-call | flops 3019898880 | bytes 1000000 | tf_op jit(solution)/shard_map/pallas_call | solution.py:25
  29.3 0.1 collective-permute-start.6
  29.4 0.7 %collective-permute-start.7 = (bf16[2,176,128]{2,1,0:T(8,128)(2,1)S(1)}, bf16[2,176,128]{2,1,0:T(8,128)(2,1)S(1)}, u32[]{:S(2)}, u32[]{:S(2)}) collective-permute-start(bf16[2,176,128]{2,1,0:T(8,128)(2,1)S(1)} %get-tuple-element.52), channel_id=1, source_target_pairs={{0,16},{8,24},{16,0},{24,8},{1,17},{9,25},{17,1},{25,9},{2,18},{10... | collective-permute-start | bytes 270344 | tf_op jit(solution)/shard_map/ppermute | solution.py:572
  30.1 2.2 %collective-permute-start.8 = (bf16[2,176,128]{2,1,0:T(8,128)(2,1)S(1)}, bf16[2,176,128]{2,1,0:T(8,128)(2,1)S(1)}, u32[]{:S(2)}, u32[]{:S(2)}) collective-permute-start(bf16[2,176,128]{2,1,0:T(8,128)(2,1)S(1)} %get-tuple-element.53), channel_id=1, source_target_pairs={{0,24},{8,0},{16,8},{24,16},{1,25},{9,1},{17,9},{25,17},{2,26},{10... | collective-permute-start | bytes 270344 | tf_op jit(solution)/shard_map/ppermute | solution.py:572
  32.3 2.6 %collective-permute-done.6.refs_1_ = bf16[2,176,128]{2,1,0:T(8,128)(2,1)S(1)} collective-permute-done((bf16[2,176,128]{2,1,0:T(8,128)(2,1)S(1)}, bf16[2,176,128]{2,1,0:T(8,128)(2,1)S(1)}, u32[]{:S(2)}, u32[]{:S(2)}) %collective-permute-start.6) | collective-permute-done | bytes 90144 | tf_op jit(solution)/shard_map/ppermute | solution.py:572
  34.9 0.0 collective-permute-done.7.refs_2_
  34.9 0.4 %collective-permute-done.8.refs_3_ = bf16[2,176,128]{2,1,0:T(8,128)(2,1)S(1)} collective-permute-done((bf16[2,176,128]{2,1,0:T(8,128)(2,1)S(1)}, bf16[2,176,128]{2,1,0:T(8,128)(2,1)S(1)}, u32[]{:S(2)}, u32[]{:S(2)}) %collective-permute-start.8) | collective-permute-done | bytes 90144 | tf_op jit(solution)/shard_map/ppermute | solution.py:572
  35.3 0.0 copy-start.1
  35.4 0.1 collective-permute-start.9
  35.5 1.4 %collective-permute-done.9.got = bf16[4,176,128]{2,1,0:T(8,128)(2,1)S(1)} collective-permute-done((bf16[4,176,128]{2,1,0:T(8,128)(2,1)S(1)}, bf16[4,176,128]{2,1,0:T(8,128)(2,1)S(1)}, u32[]{:S(2)}, u32[]{:S(2)}) %collective-permute-start.9) | collective-permute-done | bytes 180256 | tf_op jit(solution)/shard_map/ppermute | solution.py:581
  36.9 0.0 copy-done
  36.9 0.0 copy-done.1
  36.9 1.3 %shard_map.176 = (f32[4,4,32,128]{3,2,1,0:T(8,128)}, f32[4,4,32,128]{3,2,1,0:T(8,128)}) custom-call(bf16[4,176,128]{2,1,0:T(8,128)(2,1)S(1)} %get-tuple-element.54.mine, bf16[4,176,128]{2,1,0:T(8,128)(2,1)S(1)} %collective-permute-done.9.got, bf16[384,512]{1,0:T(8,128)(2,1)S(1)} %copy-done, bf16[128,128]{1,0:T(8,128)(2,1)S(1)} %copy-done.1), custom_call_target="tpu_custom_call" | custom-call | flops 1000000 | bytes 524288 | tf_op jit(solution)/shard_map/pallas_call | solution.py:25
  (2 shorter events, 0.1 us)
Async XLA Ops:
  2.5 7.2 %collective-permute-start = (bf16[2,3,64,128]{3,2,1,0:T(8,128)(2,1)S(1)}, bf16[2,3,64,128]{3,2,1,0:T(8,128)(2,1)S(1)}, u32[]{:S(2)}, u32[]{:S(2)}) collective-permute-start(bf16[2,3,64,128]{3,2,1,0:T(8,128)(2,1)S(1)} %get-tuple-element.30), channel_id=1, source_target_pairs={{0,8},{8,16},{16,24},{24,0},{1,9},{9,17},{17,25},{25,1},{2,10},{10... | collective-permute-start | bytes 294920 | tf_op jit(solution)/shard_map/ppermute | solution.py:572
  5.5 3.0 %copy-start.13 = (bf16[128,4]{0,1:T(4,128)(2,1)S(1)}, bf16[128,4]{0,1:T(4,128)(2,1)}, u32[]{:S(2)}) copy-start(bf16[128,4]{0,1:T(4,128)(2,1)} %param.27) | copy-start | bytes 3076
  5.5 5.9 %collective-permute-start.1 = (bf16[2,3,64,128]{3,2,1,0:T(8,128)(2,1)S(1)}, bf16[2,3,64,128]{3,2,1,0:T(8,128)(2,1)S(1)}, u32[]{:S(2)}, u32[]{:S(2)}) collective-permute-start(bf16[2,3,64,128]{3,2,1,0:T(8,128)(2,1)S(1)} %get-tuple-element.31), channel_id=1, source_target_pairs={{0,16},{8,24},{16,0},{24,8},{1,17},{9,25},{17,1},{25,9},{2,18},{10... | collective-permute-start | bytes 294920 | tf_op jit(solution)/shard_map/ppermute | solution.py:572
  7.0 4.7 %collective-permute-start.2 = (bf16[2,3,64,128]{3,2,1,0:T(8,128)(2,1)S(1)}, bf16[2,3,64,128]{3,2,1,0:T(8,128)(2,1)S(1)}, u32[]{:S(2)}, u32[]{:S(2)}) collective-permute-start(bf16[2,3,64,128]{3,2,1,0:T(8,128)(2,1)S(1)} %get-tuple-element.32), channel_id=1, source_target_pairs={{0,24},{8,0},{16,8},{24,16},{1,25},{9,1},{17,9},{25,17},{2,26},{10... | collective-permute-start | bytes 294920 | tf_op jit(solution)/shard_map/ppermute | solution.py:572
  8.4 0.7 %copy-start.2 = (f32[8,128]{1,0:T(8,128)S(1)}, f32[8,128]{1,0:T(8,128)}, u32[]{:S(2)}) copy-start(f32[8,128]{1,0:T(8,128)} %lift.1) | copy-start | bytes 12292
  8.5 0.7 %copy-start.3 = (f32[6,128]{1,0:T(8,128)S(1)}, f32[6,128]{1,0:T(8,128)}, u32[]{:S(2)}) copy-start(f32[6,128]{1,0:T(8,128)} %gains.1) | copy-start | bytes 9220
  8.6 0.7 %copy-start.4 = (f32[128]{0:T(128)S(1)}, f32[128]{0:T(128)}, u32[]{:S(2)}) copy-start(f32[128]{0:T(128)} %param.19) | copy-start | bytes 1540
  11.7 1.5 %collective-permute-start.3 = (bf16[4,3,64,128]{3,2,1,0:T(8,128)(2,1)S(1)}, bf16[4,3,64,128]{3,2,1,0:T(8,128)(2,1)S(1)}, u32[]{:S(2)}, u32[]{:S(2)}) collective-permute-start(bf16[4,3,64,128]{3,2,1,0:T(8,128)(2,1)S(1)} %get-tuple-element.35), channel_id=1, source_target_pairs={{0,4},{4,0},{1,5},{5,1},{2,6},{6,2},{3,7},{7,3},{8,12},{12,8},{9,1... | collective-permute-start | bytes 589832 | tf_op jit(solution)/shard_map/ppermute | solution.py:581
  13.4 9.7 %collective-permute-start.4 = (f32[5,2,4,8,128]{4,3,2,1,0:T(8,128)S(1)}, f32[5,2,4,8,128]{4,3,2,1,0:T(8,128)S(1)}, u32[]{:S(2)}, u32[]{:S(2)}) collective-permute-start(f32[5,2,4,8,128]{4,3,2,1,0:T(8,128)S(1)} %get-tuple-element.36), channel_id=1, source_target_pairs={{0,4},{4,8},{8,12},{12,24},{24,28},{28,16},{16,20},{20,21},{21,17}... | collective-permute-start | bytes 491528 | tf_op jit(solution)/shard_map/ppermute | solution.py:664
  13.6 9.5 %collective-permute-start.5 = (f32[5,2,4,8,128]{4,3,2,1,0:T(8,128)S(1)}, f32[5,2,4,8,128]{4,3,2,1,0:T(8,128)S(1)}, u32[]{:S(2)}, u32[]{:S(2)}) collective-permute-start(f32[5,2,4,8,128]{4,3,2,1,0:T(8,128)S(1)} %get-tuple-element.38), channel_id=1, source_target_pairs={{0,3},{4,0},{8,4},{12,8},{24,12},{28,24},{16,28},{20,16},{21,20},{... | collective-permute-start | bytes 491528 | tf_op jit(solution)/shard_map/ppermute | solution.py:664
  17.3 1.6 %copy-start.5 = (bf16[2,128,512]{2,1,0:T(8,128)(2,1)S(1)}, bf16[2,128,512]{2,1,0:T(8,128)(2,1)}, u32[]{:S(2)}) copy-start(bf16[2,128,512]{2,1,0:T(8,128)(2,1)} %refs_8_.3) | copy-start | bytes 786436
  17.3 1.6 %copy-start.6 = (bf16[2,512,128]{2,1,0:T(8,128)(2,1)S(1)}, bf16[2,512,128]{2,1,0:T(8,128)(2,1)}, u32[]{:S(2)}) copy-start(bf16[2,512,128]{2,1,0:T(8,128)(2,1)} %refs_9_.3) | copy-start | bytes 786436
  17.3 1.6 %copy-start.7 = (bf16[2,128,128]{2,1,0:T(8,128)(2,1)S(1)}, bf16[2,128,128]{2,1,0:T(8,128)(2,1)}, u32[]{:S(2)}) copy-start(bf16[2,128,128]{2,1,0:T(8,128)(2,1)} %refs_4_.3) | copy-start | bytes 196612
  17.3 1.6 %copy-start.8 = (bf16[2,128,128]{2,1,0:T(8,128)(2,1)S(1)}, bf16[2,128,128]{2,1,0:T(8,128)(2,1)}, u32[]{:S(2)}) copy-start(bf16[2,128,128]{2,1,0:T(8,128)(2,1)} %refs_5_.3) | copy-start | bytes 196612
  17.3 1.6 %copy-start.9 = (bf16[2,128,128]{2,1,0:T(8,128)(2,1)S(1)}, bf16[2,128,128]{2,1,0:T(8,128)(2,1)}, u32[]{:S(2)}) copy-start(bf16[2,128,128]{2,1,0:T(8,128)(2,1)} %refs_6_.3) | copy-start | bytes 196612
  17.3 1.6 %copy-start.10 = (bf16[2,128,128]{2,1,0:T(8,128)(2,1)S(1)}, bf16[2,128,128]{2,1,0:T(8,128)(2,1)}, u32[]{:S(2)}) copy-start(bf16[2,128,128]{2,1,0:T(8,128)(2,1)} %refs_7_.3) | copy-start | bytes 196612
  17.3 1.6 %copy-start.11 = (bf16[128,512]{1,0:T(8,128)(2,1)S(1)}, bf16[128,512]{1,0:T(8,128)(2,1)}, u32[]{:S(2)}) copy-start(bf16[128,512]{1,0:T(8,128)(2,1)} %constant.8.clone.refs_1_) | copy-start | bytes 393220
  23.1 1.5 %copy-start.12 = (bf16[256,256]{1,0:T(8,128)(2,1)S(1)}, bf16[256,256]{1,0:T(8,128)(2,1)}, u32[]{:S(2)}) copy-start(bf16[256,256]{1,0:T(8,128)(2,1)} %constant.9.clone.refs_12_) | copy-start | bytes 393220
  24.6 12.3 %copy-start = (bf16[384,512]{1,0:T(8,128)(2,1)S(1)}, bf16[384,512]{1,0:T(8,128)(2,1)}, u32[]{:S(2)}) copy-start(bf16[384,512]{1,0:T(8,128)(2,1)} %constant.10.clone.along_z) | copy-start | bytes 1179652
  29.3 5.6 %collective-permute-start.6 = (bf16[2,176,128]{2,1,0:T(8,128)(2,1)S(1)}, bf16[2,176,128]{2,1,0:T(8,128)(2,1)S(1)}, u32[]{:S(2)}, u32[]{:S(2)}) collective-permute-start(bf16[2,176,128]{2,1,0:T(8,128)(2,1)S(1)} %get-tuple-element.51), channel_id=1, source_target_pairs={{0,8},{8,16},{16,24},{24,0},{1,9},{9,17},{17,25},{25,1},{2,10},{10... | collective-permute-start | bytes 270344 | tf_op jit(solution)/shard_map/ppermute | solution.py:572
  29.4 5.6 %collective-permute-start.7 = (bf16[2,176,128]{2,1,0:T(8,128)(2,1)S(1)}, bf16[2,176,128]{2,1,0:T(8,128)(2,1)S(1)}, u32[]{:S(2)}, u32[]{:S(2)}) collective-permute-start(bf16[2,176,128]{2,1,0:T(8,128)(2,1)S(1)} %get-tuple-element.52), channel_id=1, source_target_pairs={{0,16},{8,24},{16,0},{24,8},{1,17},{9,25},{17,1},{25,9},{2,18},{10... | collective-permute-start | bytes 270344 | tf_op jit(solution)/shard_map/ppermute | solution.py:572
  30.1 5.3 %collective-permute-start.8 = (bf16[2,176,128]{2,1,0:T(8,128)(2,1)S(1)}, bf16[2,176,128]{2,1,0:T(8,128)(2,1)S(1)}, u32[]{:S(2)}, u32[]{:S(2)}) collective-permute-start(bf16[2,176,128]{2,1,0:T(8,128)(2,1)S(1)} %get-tuple-element.53), channel_id=1, source_target_pairs={{0,24},{8,0},{16,8},{24,16},{1,25},{9,1},{17,9},{25,17},{2,26},{10... | collective-permute-start | bytes 270344 | tf_op jit(solution)/shard_map/ppermute | solution.py:572
  35.3 1.5 %copy-start.1 = (bf16[128,128]{1,0:T(8,128)(2,1)S(1)}, bf16[128,128]{1,0:T(8,128)(2,1)}, u32[]{:S(2)}) copy-start(bf16[128,128]{1,0:T(8,128)(2,1)} %constant.11.clone.across) | copy-start | bytes 98308
  35.4 1.5 %collective-permute-start.9 = (bf16[4,176,128]{2,1,0:T(8,128)(2,1)S(1)}, bf16[4,176,128]{2,1,0:T(8,128)(2,1)S(1)}, u32[]{:S(2)}, u32[]{:S(2)}) collective-permute-start(bf16[4,176,128]{2,1,0:T(8,128)(2,1)S(1)} %get-tuple-element.55), channel_id=1, source_target_pairs={{0,4},{4,0},{1,5},{5,1},{2,6},{6,2},{3,7},{7,3},{8,12},{12,8},{9,1... | collective-permute-start | bytes 540680 | tf_op jit(solution)/shard_map/ppermute | solution.py:581

commit v5 on v4

--- a/solution.py
+++ b/solution.py
@@ -15,6 +15,7 @@
 EXTRA = 1000
 MASKED = -1e30
 MIDDLE, REACH, OCTAVES = 0.275, 0.225, 118.0
+LOWEST, SPAN = -45.0, 64.0
 F32 = jnp.float32
 BF16 = jnp.bfloat16
 VMEM = pl.BlockSpec(memory_space=pltpu.VMEM)
@@ -58,6 +59,18 @@
 def decoded(code):
     size = (jnp.log2(jnp.abs(code)) + OCTAVES) * (0.5 * REACH / OCTAVES)
     return MIDDLE + jnp.where(code < 0.0, -size, size)
+
+
+def coded_state(v):
+    place = jnp.log2(jnp.maximum(jnp.abs(v), 2.0**LOWEST)) - LOWEST
+    size = jnp.exp2(place * (2.0 * OCTAVES / SPAN) - OCTAVES)
+    return jnp.where(v < 0.0, -size, size).astype(BF16)
+
+
+def decoded_state(code):
+    place = (jnp.log2(jnp.abs(code)) + OCTAVES) * (0.5 * SPAN / OCTAVES)
+    size = jnp.where(place < 0.0005, 0.0, jnp.exp2(place + LOWEST))
+    return jnp.where(code < 0.0, -size, size)
 
 
 def pack_kernel(nx, ny, flow, visc, *rest):
@@ -446,7 +459,7 @@
         every = coefficient[...].reshape(-1, per_plane)
         if earlier:
             every = jnp.concatenate([before[...].reshape(-1, per_plane), every], axis=0)
-        kept = 2 * states[0].shape[1]
+        kept = states[0].shape[1]
         depth = outs[0].shape[1] - kept
         if every.shape[0] < depth:
             blank = jnp.zeros((depth - every.shape[0], per_plane), F32)
@@ -464,9 +477,7 @@
             near = jnp.concatenate(near, axis=1).astype(BF16)
             found = matmul(near, spread[...])
             zero, other = found[:, :width], found[:, width:]
-            high, low = halves(states[d][...])
-            outs[d][:, : kept // 2] = high
-            outs[d][:, kept // 2 : kept] = low
+            outs[d][:, :kept] = coded_state(states[d][...])
             outs[d][0, kept:] = jnp.where(first, zero, other).astype(BF16)
             outs[d][1, kept:] = jnp.where(first, other, zero).astype(BF16)
 
@@ -481,9 +492,8 @@
         for piece, core in ((mine, b), (got, lax.rem(b + 1, ny))):
             chunk = chunk_of(nx, ny, lax.rem(a + nx - d, nx), core, slab)
             start = pl.multiple_of(chunk * size, 8)
-            high, low = piece[d, :size].astype(F32), piece[d, size : 2 * size].astype(F32)
-            state_rows[pl.ds(start, size), :] = high + low
-            coarse_rows[chunk] = piece[d, 2 * size :]
+            state_rows[pl.ds(start, size), :] = decoded_state(piece[d, :size].astype(F32))
+            coarse_rows[chunk] = piece[d, size:]
     copies = []
 
     def send(buffer, out, f):
@@ -751,7 +761,7 @@
         filtered,
         outer,
         more + [spread] + state_messages,
-        [((ny, 2 * rows + depth, width), BF16)] * nx,
+        [((ny, rows + depth, width), BF16)] * nx,
         True,
     )
     mine, got = exchange(list(messages), nx, ny)

time: 38.6 us -> 38.2 us (0.990)
  waiting for transfers between devices: 8.27 us -> 7.83 us
where the time goes in v5:
time: 38.2 us; the launch traced here: 37.8 us
  Pallas kernels  15.3 us (40%)
  starting transfers between devices  13 us (34%)
  waiting for transfers between devices  7.83 us (20%)
  local copies, waits for them, and re-layouts  0.85 us (2%)
  between operations  0.84 us (2%)
    pallas_call x10, Pallas kernels, call(): pl.pallas_call(body, out_shape=tuple((jax.ShapeDtypeStruct(s, d) for s, d...  15.3 us
    ppermute x6, starting transfers between devices, exchange(): lax.ppermute(messages[d], 'gx', [(i, (i + d) % nx) for i in range(nx)])  8.94 us
    ppermute x6, waiting for transfers between devices, exchange(): lax.ppermute(messages[d], 'gx', [(i, (i + d) % nx) for i in range(nx)])  5.08 us
    ppermute x2, starting transfers between devices, ring_step(): return lax.ppermute(value, ('gx', 'gy', 'gz'), pairs)  3.88 us
    ppermute x2, waiting for transfers between devices, exchange(): lax.ppermute(away, 'gy', [(i, (i + 1) % ny) for i in range(ny)])  2.74 us
    unnamed x29, local copies, waits for them, and re-layouts  0.85 us
  transfers between devices with their start and end apart: 10, of which 7 were waited for; matrix products, arithmetic and copies ran while one was open for 0% of the time, Pallas kernels for 15%

profile of v5, /device:TPU:0, one launch (start us, length us, event | category | flops | bytes accessed | tf_op | source)
XLA Modules:
  0.0 37.8 jit_solution(3434039904643492577)
XLA Ops:
  0.6 1.8 %shard_map.167 = (bf16[2,3,64,128]{3,2,1,0:T(8,128)(2,1)S(1)}, bf16[2,3,64,128]{3,2,1,0:T(8,128)(2,1)S(1)}, bf16[2,3,64,128]{3,2,1,0:T(8,128)(2,1)S(1)}, bf16[2,3,64,128]{3,2,1,0:T(8,128)(2,1)S(1)}) custom-call(f32[4,4,32,128]{3,2,1,0:T(8,128)} %flow.1, f32[4,4,32,128]{3,2,1,0:T(8,128)} %visc.1), custom_call_target="tpu_custom_call" | custom-call | flops 1000000 | bytes 524288 | tf_op jit(solution)/shard_map/pallas_call | solution.py:26
  2.5 3.0 %collective-permute-start = (bf16[2,3,64,128]{3,2,1,0:T(8,128)(2,1)S(1)}, bf16[2,3,64,128]{3,2,1,0:T(8,128)(2,1)S(1)}, u32[]{:S(2)}, u32[]{:S(2)}) collective-permute-start(bf16[2,3,64,128]{3,2,1,0:T(8,128)(2,1)S(1)} %get-tuple-element.30), channel_id=1, source_target_pairs={{0,8},{8,16},{16,24},{24,0},{1,9},{9,17},{17,25},{25,1},{2,10},{10... | collective-permute-start | bytes 294920 | tf_op jit(solution)/shard_map/ppermute | solution.py:582
  5.5 0.0 copy-start.13
  5.5 1.5 %collective-permute-start.1 = (bf16[2,3,64,128]{3,2,1,0:T(8,128)(2,1)S(1)}, bf16[2,3,64,128]{3,2,1,0:T(8,128)(2,1)S(1)}, u32[]{:S(2)}, u32[]{:S(2)}) collective-permute-start(bf16[2,3,64,128]{3,2,1,0:T(8,128)(2,1)S(1)} %get-tuple-element.31), channel_id=1, source_target_pairs={{0,16},{8,24},{16,0},{24,8},{1,17},{9,25},{17,1},{25,9},{2,18},{10... | collective-permute-start | bytes 294920 | tf_op jit(solution)/shard_map/ppermute | solution.py:582
  7.0 1.4 %collective-permute-start.2 = (bf16[2,3,64,128]{3,2,1,0:T(8,128)(2,1)S(1)}, bf16[2,3,64,128]{3,2,1,0:T(8,128)(2,1)S(1)}, u32[]{:S(2)}, u32[]{:S(2)}) collective-permute-start(bf16[2,3,64,128]{3,2,1,0:T(8,128)(2,1)S(1)} %get-tuple-element.32), channel_id=1, source_target_pairs={{0,24},{8,0},{16,8},{24,16},{1,25},{9,1},{17,9},{25,17},{2,26},{10... | collective-permute-start | bytes 294920 | tf_op jit(solution)/shard_map/ppermute | solution.py:582
  8.4 0.0 copy-done.13
  8.4 0.0 copy-start.2
  8.5 0.0 copy-start.3
  8.5 0.1 copy.18.head
  8.6 0.0 copy-start.4
  8.6 0.5 %copy-done.2 = f32[8,128]{1,0:T(8,128)S(1)} copy-done((f32[8,128]{1,0:T(8,128)S(1)}, f32[8,128]{1,0:T(8,128)}, u32[]{:S(2)}) %copy-start.2) | copy-done | bytes 4120
  9.1 0.0 copy-done.3
  9.2 0.1 copy-done.4
  9.2 0.1 shard_map.168
  9.3 0.3 collective-permute-done.refs_1_
  9.7 1.7 %collective-permute-done.1.refs_2_ = bf16[2,3,64,128]{3,2,1,0:T(8,128)(2,1)S(1)} collective-permute-done((bf16[2,3,64,128]{3,2,1,0:T(8,128)(2,1)S(1)}, bf16[2,3,64,128]{3,2,1,0:T(8,128)(2,1)S(1)}, u32[]{:S(2)}, u32[]{:S(2)}) %collective-permute-start.1) | collective-permute-done | bytes 98336 | tf_op jit(solution)/shard_map/ppermute | solution.py:582
  11.3 0.3 collective-permute-done.2.refs_3_
  11.7 0.1 collective-permute-start.3
  11.8 1.4 %collective-permute-done.3.got = bf16[4,3,64,128]{3,2,1,0:T(8,128)(2,1)S(1)} collective-permute-done((bf16[4,3,64,128]{3,2,1,0:T(8,128)(2,1)S(1)}, bf16[4,3,64,128]{3,2,1,0:T(8,128)(2,1)S(1)}, u32[]{:S(2)}, u32[]{:S(2)}) %collective-permute-start.3) | collective-permute-done | bytes 196640 | tf_op jit(solution)/shard_map/ppermute | solution.py:591
  13.2 0.2 shard_map.170
  13.4 0.2 collective-permute-start.4
  13.6 3.7 %collective-permute-start.5 = (f32[5,2,4,8,128]{4,3,2,1,0:T(8,128)S(1)}, f32[5,2,4,8,128]{4,3,2,1,0:T(8,128)S(1)}, u32[]{:S(2)}, u32[]{:S(2)}) collective-permute-start(f32[5,2,4,8,128]{4,3,2,1,0:T(8,128)S(1)} %get-tuple-element.38), channel_id=1, source_target_pairs={{0,3},{4,0},{8,4},{12,8},{24,12},{28,24},{16,28},{20,16},{21,20},{... | collective-permute-start | bytes 491528 | tf_op jit(solution)/shard_map/ppermute | solution.py:674
  17.3 0.0 copy-start.5
  17.3 0.0 copy-start.6
  17.3 0.0 copy-start.7
  17.3 0.0 copy-start.8
  17.3 0.0 copy-start.9
  17.3 0.0 copy-start.10
  17.3 0.0 copy-start.11
  17.4 1.5 %shard_map.171 = (bf16[4,48,512]{2,1,0:T(8,128)(2,1)S(1)}, f32[16,4,8,128]{3,2,1,0:T(8,128)S(1)}, f32[16,4,8,128]{3,2,1,0:T(8,128)S(1)}, f32[16,4,8,128]{3,2,1,0:T(8,128)S(1)}) custom-call(f32[16,2,4,8,128]{4,3,2,1,0:T(8,128)S(1)} %get-tuple-element.37.refs_0_.refs_1_), custom_call_target="tpu_custom_call" | custom-call | flops 300000000 | bytes 524288 | tf_op jit(solution)/shard_map/pallas_call | solution.py:26
  18.9 0.0 copy-done.5
  18.9 0.0 copy-done.6
  18.9 0.0 copy-done.7
  18.9 0.0 copy-done.8
  18.9 0.0 copy-done.9
  19.0 0.0 copy-done.10
  19.0 0.0 copy-done.11
  19.0 4.1 %shard_map.173.refs_11_ = f32[2,8,256]{2,1,0:T(8,128)S(1)} custom-call(bf16[4,48,512]{2,1,0:T(8,128)(2,1)S(1)} %get-tuple-element.45.refs_0_, bf16[128,512]{1,0:T(8,128)(2,1)S(1)} %copy-done.11, bf16[144,256]{1,0:T(8,128)(2,1)S(1)} %get-tuple-element.43.refs_2_, f32[8,128]{1,0:T(8,128)S(1)} %get-tuple-element.33.refs_4_.refs_3_, ...), custom_call_target="tpu_custom_call" | custom-call | flops 2415919104 | bytes 1000000 | tf_op jit(solution)/shard_map/pallas_call | solution.py:26
  23.1 0.0 collective-permute-done.4.refs_0_
  23.1 0.0 collective-permute-done.5.refs_2_
  23.1 0.0 copy-start.12
  23.1 1.4 %shard_map.172 = (bf16[5,48,512]{2,1,0:T(8,128)(2,1)S(1)}, f32[2,64,128]{2,1,0:T(8,128)S(1)}, f32[2,64,128]{2,1,0:T(8,128)S(1)}, f32[2,64,128]{2,1,0:T(8,128)S(1)}, f32[2,64,128]{2,1,0:T(8,128)S(1)}) custom-call(f32[5,2,4,8,128]{4,3,2,1,0:T(8,128)S(1)} %collective-permute-done.4.refs_0_, f32[16,2,4,8,128]{4,3,2,1,0:T(8,128)S(1)} %get-tuple-element.37.refs_0_.refs_1_, ...), custom_call_target="tpu_custom_call" | custom-call | flops 300000000 | bytes 851968 | tf_op jit(solution)/shard_map/pallas_call | solution.py:26
  24.6 0.0 copy-done.12
  24.6 0.0 copy-start
  24.6 4.7 %shard_map.174 = (bf16[2,112,128]{2,1,0:T(8,128)(2,1)S(1)}, bf16[2,112,128]{2,1,0:T(8,128)(2,1)S(1)}, bf16[2,112,128]{2,1,0:T(8,128)(2,1)S(1)}, bf16[2,112,128]{2,1,0:T(8,128)(2,1)S(1)}) custom-call(bf16[5,48,512]{2,1,0:T(8,128)(2,1)S(1)} %get-tuple-element.42.refs_0_, bf16[128,512]{1,0:T(8,128)(2,1)S(1)} %copy-done.11, ...), custom_call_target="tpu_custom_call" | custom-call | flops 3019898880 | bytes 1000000 | tf_op jit(solution)/shard_map/pallas_call | solution.py:26
  29.3 0.1 collective-permute-start.6
  29.4 0.7 %collective-permute-start.7 = (bf16[2,112,128]{2,1,0:T(8,128)(2,1)S(1)}, bf16[2,112,128]{2,1,0:T(8,128)(2,1)S(1)}, u32[]{:S(2)}, u32[]{:S(2)}) collective-permute-start(bf16[2,112,128]{2,1,0:T(8,128)(2,1)S(1)} %get-tuple-element.52), channel_id=1, source_target_pairs={{0,16},{8,24},{16,0},{24,8},{1,17},{9,25},{17,1},{25,9},{2,18},{10... | collective-permute-start | bytes 172040 | tf_op jit(solution)/shard_map/ppermute | solution.py:582
  30.1 2.2 %collective-permute-start.8 = (bf16[2,112,128]{2,1,0:T(8,128)(2,1)S(1)}, bf16[2,112,128]{2,1,0:T(8,128)(2,1)S(1)}, u32[]{:S(2)}, u32[]{:S(2)}) collective-permute-start(bf16[2,112,128]{2,1,0:T(8,128)(2,1)S(1)} %get-tuple-element.53), channel_id=1, source_target_pairs={{0,24},{8,0},{16,8},{24,16},{1,25},{9,1},{17,9},{25,17},{2,26},{10... | collective-permute-start | bytes 172040 | tf_op jit(solution)/shard_map/ppermute | solution.py:582
  32.3 2.1 %collective-permute-done.6.refs_1_ = bf16[2,112,128]{2,1,0:T(8,128)(2,1)S(1)} collective-permute-done((bf16[2,112,128]{2,1,0:T(8,128)(2,1)S(1)}, bf16[2,112,128]{2,1,0:T(8,128)(2,1)S(1)}, u32[]{:S(2)}, u32[]{:S(2)}) %collective-permute-start.6) | collective-permute-done | bytes 57376 | tf_op jit(solution)/shard_map/ppermute | solution.py:582
  34.4 0.0 collective-permute-done.7.refs_2_
  34.4 0.6 %collective-permute-done.8.refs_3_ = bf16[2,112,128]{2,1,0:T(8,128)(2,1)S(1)} collective-permute-done((bf16[2,112,128]{2,1,0:T(8,128)(2,1)S(1)}, bf16[2,112,128]{2,1,0:T(8,128)(2,1)S(1)}, u32[]{:S(2)}, u32[]{:S(2)}) %collective-permute-start.8) | collective-permute-done | bytes 57376 | tf_op jit(solution)/shard_map/ppermute | solution.py:582
  35.0 0.0 copy-start.1
  35.0 0.1 collective-permute-start.9
  35.1 1.3 %collective-permute-done.9.got = bf16[4,112,128]{2,1,0:T(8,128)(2,1)S(1)} collective-permute-done((bf16[4,112,128]{2,1,0:T(8,128)(2,1)S(1)}, bf16[4,112,128]{2,1,0:T(8,128)(2,1)S(1)}, u32[]{:S(2)}, u32[]{:S(2)}) %collective-permute-start.9) | collective-permute-done | bytes 114720 | tf_op jit(solution)/shard_map/ppermute | solution.py:591
  36.4 0.0 copy-done
  36.4 0.0 copy-done.1
  36.4 1.3 %shard_map.176 = (f32[4,4,32,128]{3,2,1,0:T(8,128)}, f32[4,4,32,128]{3,2,1,0:T(8,128)}) custom-call(bf16[4,112,128]{2,1,0:T(8,128)(2,1)S(1)} %get-tuple-element.54.mine, bf16[4,112,128]{2,1,0:T(8,128)(2,1)S(1)} %collective-permute-done.9.got, bf16[384,512]{1,0:T(8,128)(2,1)S(1)} %copy-done, bf16[128,128]{1,0:T(8,128)(2,1)S(1)} %copy-done.1), custom_call_target="tpu_custom_call" | custom-call | flops 1000000 | bytes 524288 | tf_op jit(solution)/shard_map/pallas_call | solution.py:26
  (2 shorter events, 0.0 us)
Async XLA Ops:
  2.5 7.2 %collective-permute-start = (bf16[2,3,64,128]{3,2,1,0:T(8,128)(2,1)S(1)}, bf16[2,3,64,128]{3,2,1,0:T(8,128)(2,1)S(1)}, u32[]{:S(2)}, u32[]{:S(2)}) collective-permute-start(bf16[2,3,64,128]{3,2,1,0:T(8,128)(2,1)S(1)} %get-tuple-element.30), channel_id=1, source_target_pairs={{0,8},{8,16},{16,24},{24,0},{1,9},{9,17},{17,25},{25,1},{2,10},{10... | collective-permute-start | bytes 294920 | tf_op jit(solution)/shard_map/ppermute | solution.py:582
  5.5 3.0 %copy-start.13 = (bf16[128,4]{0,1:T(4,128)(2,1)S(1)}, bf16[128,4]{0,1:T(4,128)(2,1)}, u32[]{:S(2)}) copy-start(bf16[128,4]{0,1:T(4,128)(2,1)} %param.27) | copy-start | bytes 3076
  5.5 5.9 %collective-permute-start.1 = (bf16[2,3,64,128]{3,2,1,0:T(8,128)(2,1)S(1)}, bf16[2,3,64,128]{3,2,1,0:T(8,128)(2,1)S(1)}, u32[]{:S(2)}, u32[]{:S(2)}) collective-permute-start(bf16[2,3,64,128]{3,2,1,0:T(8,128)(2,1)S(1)} %get-tuple-element.31), channel_id=1, source_target_pairs={{0,16},{8,24},{16,0},{24,8},{1,17},{9,25},{17,1},{25,9},{2,18},{10... | collective-permute-start | bytes 294920 | tf_op jit(solution)/shard_map/ppermute | solution.py:582
  7.0 4.7 %collective-permute-start.2 = (bf16[2,3,64,128]{3,2,1,0:T(8,128)(2,1)S(1)}, bf16[2,3,64,128]{3,2,1,0:T(8,128)(2,1)S(1)}, u32[]{:S(2)}, u32[]{:S(2)}) collective-permute-start(bf16[2,3,64,128]{3,2,1,0:T(8,128)(2,1)S(1)} %get-tuple-element.32), channel_id=1, source_target_pairs={{0,24},{8,0},{16,8},{24,16},{1,25},{9,1},{17,9},{25,17},{2,26},{10... | collective-permute-start | bytes 294920 | tf_op jit(solution)/shard_map/ppermute | solution.py:582
  8.4 0.7 %copy-start.2 = (f32[8,128]{1,0:T(8,128)S(1)}, f32[8,128]{1,0:T(8,128)}, u32[]{:S(2)}) copy-start(f32[8,128]{1,0:T(8,128)} %lift.1) | copy-start | bytes 12292
  8.5 0.7 %copy-start.3 = (f32[6,128]{1,0:T(8,128)S(1)}, f32[6,128]{1,0:T(8,128)}, u32[]{:S(2)}) copy-start(f32[6,128]{1,0:T(8,128)} %gains.1) | copy-start | bytes 9220
  8.6 0.7 %copy-start.4 = (f32[128]{0:T(128)S(1)}, f32[128]{0:T(128)}, u32[]{:S(2)}) copy-start(f32[128]{0:T(128)} %param.19) | copy-start | bytes 1540
  11.7 1.5 %collective-permute-start.3 = (bf16[4,3,64,128]{3,2,1,0:T(8,128)(2,1)S(1)}, bf16[4,3,64,128]{3,2,1,0:T(8,128)(2,1)S(1)}, u32[]{:S(2)}, u32[]{:S(2)}) collective-permute-start(bf16[4,3,64,128]{3,2,1,0:T(8,128)(2,1)S(1)} %get-tuple-element.35), channel_id=1, source_target_pairs={{0,4},{4,0},{1,5},{5,1},{2,6},{6,2},{3,7},{7,3},{8,12},{12,8},{9,1... | collective-permute-start | bytes 589832 | tf_op jit(solution)/shard_map/ppermute | solution.py:591
  13.4 9.7 %collective-permute-start.4 = (f32[5,2,4,8,128]{4,3,2,1,0:T(8,128)S(1)}, f32[5,2,4,8,128]{4,3,2,1,0:T(8,128)S(1)}, u32[]{:S(2)}, u32[]{:S(2)}) collective-permute-start(f32[5,2,4,8,128]{4,3,2,1,0:T(8,128)S(1)} %get-tuple-element.36), channel_id=1, source_target_pairs={{0,4},{4,8},{8,12},{12,24},{24,28},{28,16},{16,20},{20,21},{21,17}... | collective-permute-start | bytes 491528 | tf_op jit(solution)/shard_map/ppermute | solution.py:674
  13.6 9.5 %collective-permute-start.5 = (f32[5,2,4,8,128]{4,3,2,1,0:T(8,128)S(1)}, f32[5,2,4,8,128]{4,3,2,1,0:T(8,128)S(1)}, u32[]{:S(2)}, u32[]{:S(2)}) collective-permute-start(f32[5,2,4,8,128]{4,3,2,1,0:T(8,128)S(1)} %get-tuple-element.38), channel_id=1, source_target_pairs={{0,3},{4,0},{8,4},{12,8},{24,12},{28,24},{16,28},{20,16},{21,20},{... | collective-permute-start | bytes 491528 | tf_op jit(solution)/shard_map/ppermute | solution.py:674
  17.3 1.6 %copy-start.5 = (bf16[2,128,512]{2,1,0:T(8,128)(2,1)S(1)}, bf16[2,128,512]{2,1,0:T(8,128)(2,1)}, u32[]{:S(2)}) copy-start(bf16[2,128,512]{2,1,0:T(8,128)(2,1)} %refs_8_.3) | copy-start | bytes 786436
  17.3 1.6 %copy-start.6 = (bf16[2,512,128]{2,1,0:T(8,128)(2,1)S(1)}, bf16[2,512,128]{2,1,0:T(8,128)(2,1)}, u32[]{:S(2)}) copy-start(bf16[2,512,128]{2,1,0:T(8,128)(2,1)} %refs_9_.3) | copy-start | bytes 786436
  17.3 1.6 %copy-start.7 = (bf16[2,128,128]{2,1,0:T(8,128)(2,1)S(1)}, bf16[2,128,128]{2,1,0:T(8,128)(2,1)}, u32[]{:S(2)}) copy-start(bf16[2,128,128]{2,1,0:T(8,128)(2,1)} %refs_4_.3) | copy-start | bytes 196612
  17.3 1.6 %copy-start.8 = (bf16[2,128,128]{2,1,0:T(8,128)(2,1)S(1)}, bf16[2,128,128]{2,1,0:T(8,128)(2,1)}, u32[]{:S(2)}) copy-start(bf16[2,128,128]{2,1,0:T(8,128)(2,1)} %refs_5_.3) | copy-start | bytes 196612
  17.3 1.6 %copy-start.9 = (bf16[2,128,128]{2,1,0:T(8,128)(2,1)S(1)}, bf16[2,128,128]{2,1,0:T(8,128)(2,1)}, u32[]{:S(2)}) copy-start(bf16[2,128,128]{2,1,0:T(8,128)(2,1)} %refs_6_.3) | copy-start | bytes 196612
  17.3 1.6 %copy-start.10 = (bf16[2,128,128]{2,1,0:T(8,128)(2,1)S(1)}, bf16[2,128,128]{2,1,0:T(8,128)(2,1)}, u32[]{:S(2)}) copy-start(bf16[2,128,128]{2,1,0:T(8,128)(2,1)} %refs_7_.3) | copy-start | bytes 196612
  17.3 1.6 %copy-start.11 = (bf16[128,512]{1,0:T(8,128)(2,1)S(1)}, bf16[128,512]{1,0:T(8,128)(2,1)}, u32[]{:S(2)}) copy-start(bf16[128,512]{1,0:T(8,128)(2,1)} %constant.8.clone.refs_1_) | copy-start | bytes 393220
  23.1 1.5 %copy-start.12 = (bf16[256,256]{1,0:T(8,128)(2,1)S(1)}, bf16[256,256]{1,0:T(8,128)(2,1)}, u32[]{:S(2)}) copy-start(bf16[256,256]{1,0:T(8,128)(2,1)} %constant.9.clone.refs_12_) | copy-start | bytes 393220
  24.6 11.8 %copy-start = (bf16[384,512]{1,0:T(8,128)(2,1)S(1)}, bf16[384,512]{1,0:T(8,128)(2,1)}, u32[]{:S(2)}) copy-start(bf16[384,512]{1,0:T(8,128)(2,1)} %constant.10.clone.along_z) | copy-start | bytes 1179652
  29.3 5.1 %collective-permute-start.6 = (bf16[2,112,128]{2,1,0:T(8,128)(2,1)S(1)}, bf16[2,112,128]{2,1,0:T(8,128)(2,1)S(1)}, u32[]{:S(2)}, u32[]{:S(2)}) collective-permute-start(bf16[2,112,128]{2,1,0:T(8,128)(2,1)S(1)} %get-tuple-element.51), channel_id=1, source_target_pairs={{0,8},{8,16},{16,24},{24,0},{1,9},{9,17},{17,25},{25,1},{2,10},{10... | collective-permute-start | bytes 172040 | tf_op jit(solution)/shard_map/ppermute | solution.py:582
  29.4 5.1 %collective-permute-start.7 = (bf16[2,112,128]{2,1,0:T(8,128)(2,1)S(1)}, bf16[2,112,128]{2,1,0:T(8,128)(2,1)S(1)}, u32[]{:S(2)}, u32[]{:S(2)}) collective-permute-start(bf16[2,112,128]{2,1,0:T(8,128)(2,1)S(1)} %get-tuple-element.52), channel_id=1, source_target_pairs={{0,16},{8,24},{16,0},{24,8},{1,17},{9,25},{17,1},{25,9},{2,18},{10... | collective-permute-start | bytes 172040 | tf_op jit(solution)/shard_map/ppermute | solution.py:582
  30.1 4.9 %collective-permute-start.8 = (bf16[2,112,128]{2,1,0:T(8,128)(2,1)S(1)}, bf16[2,112,128]{2,1,0:T(8,128)(2,1)S(1)}, u32[]{:S(2)}, u32[]{:S(2)}) collective-permute-start(bf16[2,112,128]{2,1,0:T(8,128)(2,1)S(1)} %get-tuple-element.53), channel_id=1, source_target_pairs={{0,24},{8,0},{16,8},{24,16},{1,25},{9,1},{17,9},{25,17},{2,26},{10... | collective-permute-start | bytes 172040 | tf_op jit(solution)/shard_map/ppermute | solution.py:582
  35.0 1.4 %copy-start.1 = (bf16[128,128]{1,0:T(8,128)(2,1)S(1)}, bf16[128,128]{1,0:T(8,128)(2,1)}, u32[]{:S(2)}) copy-start(bf16[128,128]{1,0:T(8,128)(2,1)} %constant.11.clone.across) | copy-start | bytes 98308
  35.0 1.4 %collective-permute-start.9 = (bf16[4,112,128]{2,1,0:T(8,128)(2,1)S(1)}, bf16[4,112,128]{2,1,0:T(8,128)(2,1)S(1)}, u32[]{:S(2)}, u32[]{:S(2)}) collective-permute-start(bf16[4,112,128]{2,1,0:T(8,128)(2,1)S(1)} %get-tuple-element.55), channel_id=1, source_target_pairs={{0,4},{4,0},{1,5},{5,1},{2,6},{6,2},{3,7},{7,3},{8,12},{12,8},{9,1... | collective-permute-start | bytes 344072 | tf_op jit(solution)/shard_map/ppermute | solution.py:591
